TPU v7x, 512 devices: a whole 4x4x16 slice. The times are simulated.
512 devices in a mesh: segment: 8 (over x, core), dp: 64 (over y, z).
Axes of the slice: x: 4, y: 4, z: 16, core: 2. Of those that a mesh axis runs over, the one named last changes fastest.
Arguments:
- hidden: bfloat16 [8, 8192, 8192], P('segment', 'dp'), may hold values from -6 to 6
- store_a: bfloat16 [8, 32, 64, 8192], P('segment', None, None, 'dp'), may hold values from -0.0625 to 0.0625
- store_b: bfloat16 [8, 32, 64, 8192], P('segment', None, None, 'dp'), may hold values from -0.75 to 0.75
- request_start: int32 [8, 32], P('segment'), may hold values from 0 to 8128, as said below
- request_adapter: int32 [8, 32], P('segment'), may hold values from 0 to 31
Outputs:
- updated: bfloat16 [8, 8192, 8192], P('segment', 'dp')
Inputs may be any that keep to these rules, and one draw needn't show every extreme that they name: `request_start`: in each group the starts rise strictly from 0, are multiples of 64, and the last is 8128.
All inputs are finite; a program needn't handle non-finite values.
Results may differ from a plain program's by a relative error of at most 0.006.
Values may be sent and summed in bfloat16 or wider, within the bound.
No kernel may reach another device: no remote copies, remote signals or barrier semaphores. Data moves between devices by JAX's collectives and lax.ppermute only.
A program may use at most 64 MiB of HBM per device.

v0:
```python
import jax
import jax.numpy as jnp
from jax import lax
from jax.sharding import PartitionSpec as P

BLOCK = 64
STEPS = 2


EPS = 1e-05
ADAPTER_SCALE = 0.5


def from_behind(block, axis, distance):
    devices = range(lax.axis_size(axis))
    route = [((i - distance) % len(devices), i) for i in devices]
    return lax.ppermute(block, axis, route)


def block_adapters(starts, adapters, total_rows):
    blocks = total_rows // BLOCK
    block_start = jnp.arange(blocks, dtype=jnp.int32) * BLOCK
    request = jnp.sum((starts[None, :] <= block_start[:, None]).astype(jnp.int32), axis=1) - 1
    labels = jnp.arange(adapters.shape[0], dtype=jnp.int32)
    picked = jnp.where(request[:, None] == labels[None, :], adapters[None, :], 0)
    return jnp.sum(picked, axis=1)


def apply_layer(state, starts, adapters, slice_a, slice_b):
    value_rows = state.astype(jnp.float32)
    meansq = jnp.mean(value_rows * value_rows, axis=-1, keepdims=True)
    normed = (value_rows * lax.rsqrt(meansq + EPS)).astype(jnp.bfloat16)
    rank_width = slice_a.shape[1]
    columns = lax.all_to_all(normed, "dp", split_axis=1, concat_axis=0, tiled=True)
    total_rows, width = columns.shape
    blocks = total_rows // BLOCK
    chosen = block_adapters(starts, adapters, total_rows)
    down = jnp.take(slice_a, chosen, axis=0)
    grouped = columns.reshape(blocks, BLOCK, width)
    partial_rank = jnp.einsum("bic,brc->bir", grouped, down, preferred_element_type=jnp.float32)
    partial_rank = partial_rank.reshape(total_rows, rank_width)
    rank = lax.psum(partial_rank, "dp").astype(jnp.bfloat16)
    upper = jnp.take(slice_b, chosen, axis=0)
    adapter_update = jnp.einsum(
        "bir,brc->bic",
        rank.reshape(blocks, BLOCK, rank_width),
        upper,
        preferred_element_type=jnp.float32,
    )
    adapter_update = adapter_update.reshape(total_rows, width).astype(jnp.bfloat16)
    returned_rows = lax.all_to_all(adapter_update, "dp", split_axis=0, concat_axis=1, tiled=True)
    return (value_rows + ADAPTER_SCALE * returned_rows.astype(jnp.float32)).astype(jnp.bfloat16)


def shards(hidden, store_a, store_b, request_start, request_adapter):
    state = hidden[0]
    starts = request_start[0]
    adapters = request_adapter[0]
    slice_a = store_a[0]
    slice_b = store_b[0]
    for step in range(STEPS):
        if step > 0:
            state = from_behind(state, "segment", 1)
            starts, adapters = from_behind((starts, adapters), "segment", 1)
        state = apply_layer(state, starts, adapters, slice_a, slice_b)
    state = from_behind(state, "segment", 1 - STEPS)
    return state[None]


def solution(mesh):
    return jax.shard_map(
        shards,
        mesh=mesh,
        in_specs=(
            P("segment", "dp", None),
            P("segment", None, None, "dp"),
            P("segment", None, None, "dp"),
            P("segment", None),
            P("segment", None),
        ),
        out_specs=P("segment", "dp", None),
        check_vma=False,
    )
```

profile of v0, /device:TPU:6, one launch (start us, length us, event | category | flops | bytes accessed | tf_op | source)
XLA Modules:
  0.0 1124.4 jit_solution(4705812348207641893)
XLA Ops:
  0.0 0.0 copy-start
  0.0 0.0 copy-start.2
  0.0 2.2 convert_bitcast_fusion
  2.2 0.1 copy-done.2
  2.3 0.5 fusion.2
  2.8 0.7 copy.17
  3.5 3.8 fusion.7
  7.3 0.0 copy-start.3
  7.3 0.0 copy-start.4
  7.3 19.1 %all-to-all-start = ((bf16[128,64,128]{2,0,1:T(8,128)(2,1)}), bf16[128,64,128]{2,0,1:T(8,128)(2,1)}, u32[]{:S(2)}, u32[]{:S(2)}) async-start(bf16[128,64,128]{2,0,1:T(8,128)(2,1)} %fusion.7), calls=%async_computation | async-start | bytes 4194304 | tf_op jit(solution)/shard_map/all_to_all | solution.py:34
  26.4 0.0 copy-done.3
  26.4 0.0 collective-permute-start.1
  26.5 2.9 collective-permute-done.1
  29.4 0.1 convert_reduce_fusion
  29.5 0.0 copy-done.4
  29.5 0.1 select_reduce_fusion.1
  29.6 0.0 copy-done
  29.6 0.0 copy-start.1
  29.6 2.2 gather_fusion
  31.9 0.0 copy-done.1
  31.9 2.1 gather_fusion.1
  34.0 89.5 %all-to-all-done = bf16[128,64,128]{2,0,1:T(8,128)(2,1)} async-done(((bf16[128,64,128]{2,0,1:T(8,128)(2,1)}), bf16[128,64,128]{2,0,1:T(8,128)(2,1)}, u32[]{:S(2)}, u32[]{:S(2)}) %all-to-all-start) | async-done | bytes 2097184 | tf_op jit(solution)/shard_map/all_to_all | solution.py:34
  123.5 5.4 fusion.15
  129.0 354.7 %all-reduce.2 = bf16[8192,64]{1,0:T(8,128)(2,1)} all-reduce(f32[8192,64]{1,0:T(8,128)} %bitcast.57), channel_id=1, replica_groups=mesh['segment'=8,'dp'=64] {'dp'}, use_global_device_ids=true, to_apply=%region_3.5 | all-reduce | flops 524288 | bytes 3145728 | tf_op jit(solution)/shard_map/psum | solution.py:42
  483.7 3.0 fusion.21
  486.7 57.1 %all_to_all.49 = bf16[64,128,128]{2,1,0:T(8,128)(2,1)S(1)} all-to-all(bf16[64,128,128]{2,1,0:T(8,128)(2,1)S(1)} %bitcast.61), channel_id=1, replica_groups=mesh['segment'=8,'dp'=64] {'dp'}, dimensions={0} | all-to-all | bytes 4194304 | tf_op jit(solution)/shard_map/all_to_all | solution.py:51
  543.8 0.7 fusion.3
  544.5 0.0 collective-permute-start
  544.5 25.4 %collective-permute-done = bf16[128,8192]{1,0:T(8,128)(2,1)S(1)} collective-permute-done((bf16[128,8192]{1,0:T(8,128)(2,1)S(1)}, bf16[128,8192]{1,0:T(8,128)(2,1)S(1)}, u32[]{:S(2)}, u32[]{:S(2)}) %collective-permute-start) | collective-permute-done | bytes 2097184 | tf_op jit(solution)/shard_map/ppermute | solution.py:17
  569.9 0.5 fusion.4
  570.4 2.0 copy_bitcast_fusion
  572.4 9.2 all-to-all-start.2
  581.6 0.0 collective-permute-start.2
  581.6 2.9 collective-permute-done.2
  584.6 0.1 select_reduce_fusion
  584.7 2.2 gather_fusion.2
  586.9 2.1 gather_fusion.3
  589.0 88.6 %all-to-all-done.2 = bf16[128,64,128]{2,0,1:T(8,128)(2,1)} async-done(((bf16[128,64,128]{2,0,1:T(8,128)(2,1)}), bf16[128,64,128]{2,0,1:T(8,128)(2,1)}, u32[]{:S(2)}, u32[]{:S(2)}) %all-to-all-start.2) | async-done | bytes 2097184 | tf_op jit(solution)/shard_map/all_to_all | solution.py:34
  677.6 5.4 fusion.11
  683.1 355.6 %all-reduce.3 = bf16[8192,64]{1,0:T(8,128)(2,1)} all-reduce(f32[8192,64]{1,0:T(8,128)} %bitcast.58), channel_id=1, replica_groups=mesh['segment'=8,'dp'=64] {'dp'}, use_global_device_ids=true, to_apply=%region_7.9 | all-reduce | flops 524288 | bytes 3145728 | tf_op jit(solution)/shard_map/psum | solution.py:42
  1038.7 3.0 fusion.24
  1041.7 57.1 %all_to_all.50 = bf16[64,128,128]{2,1,0:T(8,128)(2,1)S(1)} all-to-all(bf16[64,128,128]{2,1,0:T(8,128)(2,1)S(1)} %bitcast.62), channel_id=1, replica_groups=mesh['segment'=8,'dp'=64] {'dp'}, dimensions={0} | all-to-all | bytes 4194304 | tf_op jit(solution)/shard_map/all_to_all | solution.py:51
  1098.8 0.7 fusion.6
  1099.5 0.0 collective-permute-start.3
  1099.5 23.5 %collective-permute-done.3 = bf16[128,8192]{1,0:T(8,128)(2,1)S(1)} collective-permute-done((bf16[128,8192]{1,0:T(8,128)(2,1)S(1)}, bf16[128,8192]{1,0:T(8,128)(2,1)S(1)}, u32[]{:S(2)}, u32[]{:S(2)}) %collective-permute-start.3) | collective-permute-done | bytes 2097184 | tf_op jit(solution)/shard_map/ppermute | solution.py:17
  1123.0 1.3 copy.29
  (11 shorter events, 0.1 us)
Async XLA Ops:
  0.0 29.6 %copy-start = (bf16[1,32,64,128]{3,2,1,0:T(8,128)(2,1)S(1)}, bf16[1,32,64,128]{3,2,1,0:T(8,128)(2,1)}, u32[]{:S(2)}) copy-start(bf16[1,32,64,128]{3,2,1,0:T(8,128)(2,1)} %param.8) | copy-start | bytes 1572868
  0.0 2.3 copy-start.2
  7.3 19.1 %copy-start.3 = (s32[1,32]{1,0:T(1,128)S(1)}, s32[1,32]{1,0:T(1,128)}, u32[]{:S(2)}) copy-start(s32[1,32]{1,0:T(1,128)} %param.10) | copy-start | bytes 388
  7.3 22.2 %copy-start.4 = (s32[1,32]{1,0:T(1,128)S(1)}, s32[1,32]{1,0:T(1,128)}, u32[]{:S(2)}) copy-start(s32[1,32]{1,0:T(1,128)} %param.11) | copy-start | bytes 388
  7.3 116.2 %all-to-all-start = ((bf16[128,64,128]{2,0,1:T(8,128)(2,1)}), bf16[128,64,128]{2,0,1:T(8,128)(2,1)}, u32[]{:S(2)}, u32[]{:S(2)}) async-start(bf16[128,64,128]{2,0,1:T(8,128)(2,1)} %fusion.7), calls=%async_computation | async-start | bytes 4194304 | tf_op jit(solution)/shard_map/all_to_all | solution.py:34
  26.4 3.0 collective-permute-start.1
  29.6 2.2 copy-start.1
  544.5 25.5 %collective-permute-start = (bf16[128,8192]{1,0:T(8,128)(2,1)S(1)}, bf16[128,8192]{1,0:T(8,128)(2,1)S(1)}, u32[]{:S(2)}, u32[]{:S(2)}) collective-permute-start(bf16[128,8192]{1,0:T(8,128)(2,1)S(1)} %fusion.3), channel_id=1, source_target_pairs={{448,0},{0,64},{64,128},{128,192},{192,256},{256,320},{320,384},{3... | collective-permute-start | bytes 6291464 | tf_op jit(solution)/shard_map/ppermute | solution.py:17
  572.4 105.2 %all-to-all-start.2 = ((bf16[128,64,128]{2,0,1:T(8,128)(2,1)}), bf16[128,64,128]{2,0,1:T(8,128)(2,1)}, u32[]{:S(2)}, u32[]{:S(2)}) async-start(bf16[128,64,128]{2,0,1:T(8,128)(2,1)} %copy_bitcast_fusion), calls=%async_computation.2 | async-start | bytes 4194304 | tf_op jit(solution)/shard_map/all_to_all | solution.py:34
  581.6 3.0 collective-permute-start.2
  1099.5 23.6 %collective-permute-start.3 = (bf16[128,8192]{1,0:T(8,128)(2,1)S(1)}, bf16[128,8192]{1,0:T(8,128)(2,1)S(1)}, u32[]{:S(2)}, u32[]{:S(2)}) collective-permute-start(bf16[128,8192]{1,0:T(8,128)(2,1)S(1)} %fusion.6), channel_id=1, source_target_pairs={{64,0},{128,64},{192,128},{256,192},{320,256},{384,320},{448,384},... | collective-permute-start | bytes 6291464 | tf_op jit(solution)/shard_map/ppermute | solution.py:17
where the time goes:
time: 1130 us; the launch traced here: 1120 us
  blocking collectives  825 us (73%)
  waiting for transfers between devices  233 us (21%)
  starting transfers between devices  28.4 us (3%)
  matrix products  16.9 us (1%)
    psum x2, blocking collectives, apply_layer(): rank = lax.psum(partial_rank, 'dp').astype(jnp.bfloat16)  710 us
    all_to_all x2, waiting for transfers between devices, apply_layer(): lax.all_to_all(normed, 'dp', split_axis=1, concat_axis=0, tiled=True)  178 us
    all_to_all x2, blocking collectives, apply_layer(): lax.all_to_all(adapter_update, 'dp', split_axis=0, concat_axis=1, tiled=T...  114 us
    ppermute x4, waiting for transfers between devices, from_behind(): return lax.ppermute(block, axis, route)  54.9 us
    all_to_all x2, starting transfers between devices, apply_layer(): lax.all_to_all(normed, 'dp', split_axis=1, concat_axis=0, tiled=True)  28.3 us
  transfers between devices with their start and end apart: 6, of which 6 were waited for; matrix products, arithmetic and copies ran while one was open for 1% of the time, Pallas kernels for 0%

commit v1 on v0

v1 whole, which is shorter than its diff:
```python
import functools

import jax
import jax.numpy as jnp
from jax import lax
from jax.experimental import pallas as pl
from jax.experimental.pallas import tpu as pltpu
from jax.sharding import Mesh, PartitionSpec as P

BLOCK = 64
EPS = 1e-05
ADAPTER_SCALE = 0.5
X, CORES, Y, Z = 4, 2, 4, 16
SEGMENT = ("x", "core")
LANES = 128
ROWS = 128
WIDTH = 8192
RANK = 64

BATCHES = (
    tuple((s, d) for d in (0, 1, 15) for s in (0, 1)),
    tuple((s, d) for d in (2, 14, 3, 13) for s in (0, 1)),
    tuple((s, d) for d in (4, 12, 5, 11) for s in (0, 1)),
    tuple((s, d) for d in (6, 10, 7, 9) for s in (0, 1)),
    tuple((s, 8) for s in (0, 1)),
)
PLACE = {
    (store, d): (b, c)
    for b, batch in enumerate(BATCHES)
    for c, (store, d) in enumerate(batch)
}
ORDER = tuple(d for batch in BATCHES for s, d in batch if s == 0)


def block_adapters(starts, adapters, total_rows):
    blocks = total_rows // BLOCK
    block_start = jnp.arange(blocks, dtype=jnp.int32) * BLOCK
    request = jnp.sum((starts[None, :] <= block_start[:, None]).astype(jnp.int32), axis=1) - 1
    labels = jnp.arange(adapters.shape[0], dtype=jnp.int32)
    picked = jnp.where(request[:, None] == labels[None, :], adapters[None, :], 0)
    return jnp.sum(picked, axis=1)


def pick_kernel(count, wanted, *refs):
    out = refs[count]
    for y in range(Y):
        for k in range(2):
            for b in range(2):
                which = wanted[y, k, b]
                for c in range(count):
                    out[y, k, c, b] = refs[c][which]


def pick(wanted, chunks):
    count = len(chunks)
    return pl.pallas_call(
        functools.partial(pick_kernel, count),
        out_shape=jax.ShapeDtypeStruct((Y, 2, count, 2, RANK, LANES), jnp.bfloat16),
        in_specs=[pl.BlockSpec(memory_space=pltpu.SMEM)]
        + [pl.BlockSpec(memory_space=pltpu.VMEM)] * count,
        out_specs=pl.BlockSpec(memory_space=pltpu.VMEM),
        compiler_params=pltpu.CompilerParams(vmem_limit_bytes=16 << 20),
        cost_estimate=pl.CostEstimate(
            flops=0, transcendentals=0, bytes_accessed=count * (3 << 18)
        ),
    )(wanted, *chunks)


def layers_kernel(z_ref, hidden, *refs):
    n = len(BATCHES)
    first, second = refs[:n], refs[n : 2 * n]
    out, state = refs[2 * n], refs[2 * n + 1]
    z = z_ref[0]

    def place(y, d):
        return pl.ds(pl.multiple_of(y * Z * LANES + ((z - d) & (Z - 1)) * LANES, LANES), LANES)

    def panel(step, store, y, d):
        b, c = PLACE[store, d]
        if step == 0:
            return first[b][y, 0, c].reshape(2 * RANK, LANES)
        return second[b][y, c].reshape(2 * RANK, LANES)

    def panels(step, store, y, ds):
        return jnp.concatenate([panel(step, store, y, d) for d in ds], axis=1)

    own = lax.broadcasted_iota(jnp.int32, (ROWS, 2 * RANK), 0) // BLOCK == (
        lax.broadcasted_iota(jnp.int32, (ROWS, 2 * RANK), 1) // RANK
    )
    groups = [(y, i, ORDER[i : i + 4]) for y in range(Y) for i in range(0, Z, 4)]

    def slot(y, i, width):
        return pl.ds((y * Z + i) * LANES, width * LANES)

    for y, i, ds in groups:
        state[:, slot(y, i, 4)] = jnp.concatenate([hidden[:, place(y, d)] for d in ds], axis=1)

    for step in range(2):
        total = jnp.zeros((ROWS, LANES), jnp.float32)
        for y, i, ds in groups:
            for j in range(4):
                v = state[:, slot(y, i + j, 1)].astype(jnp.float32)
                total = total + v * v
        scale = lax.rsqrt(jnp.sum(total, axis=1, keepdims=True) / WIDTH + EPS)
        scale = jnp.broadcast_to(scale, (ROWS, 4 * LANES))
        rank = jnp.zeros((ROWS, 2 * RANK), jnp.float32)
        for y, i, ds in groups:
            v = (state[:, slot(y, i, 4)].astype(jnp.float32) * scale).astype(jnp.bfloat16)
            rank = rank + lax.dot_general(
                v, panels(step, 0, y, ds), (((1,), (1,)), ((), ())),
                preferred_element_type=jnp.float32,
            )
        rank = jnp.where(own, rank, 0.0).astype(jnp.bfloat16)
        for y, i, ds in groups:
            delta = jnp.dot(rank, panels(step, 1, y, ds), preferred_element_type=jnp.float32)
            delta = delta.astype(jnp.bfloat16).astype(jnp.float32)
            new = state[:, slot(y, i, 4)].astype(jnp.float32) + ADAPTER_SCALE * delta
            new = new.astype(jnp.bfloat16)
            if step == 0:
                state[:, slot(y, i, 4)] = new
            else:
                for j, d in enumerate(ds):
                    out[:, place(y, d)] = new[:, j * LANES : (j + 1) * LANES]


def layers(z, hidden, first, second):
    whole = lambda i, z: (0, 0)
    return pl.pallas_call(
        layers_kernel,
        out_shape=jax.ShapeDtypeStruct((ROWS, WIDTH), jnp.bfloat16),
        grid_spec=pltpu.PrefetchScalarGridSpec(
            num_scalar_prefetch=1,
            grid=(1,),
            in_specs=[pl.BlockSpec((ROWS, WIDTH), whole, pipeline_mode=pl.Buffered(1))]
            + [
                pl.BlockSpec(
                    (Y, 1) + f.shape[2:], lambda i, z: (0,) * 6, pipeline_mode=pl.Buffered(1)
                )
                for f in first
            ]
            + [
                pl.BlockSpec(s.shape, lambda i, z: (0,) * 5, pipeline_mode=pl.Buffered(1))
                for s in second
            ],
            out_specs=pl.BlockSpec((ROWS, WIDTH), whole, pipeline_mode=pl.Buffered(1)),
            scratch_shapes=[pltpu.VMEM((ROWS, WIDTH), jnp.bfloat16)],
        ),
        compiler_params=pltpu.CompilerParams(vmem_limit_bytes=40 << 20),
        cost_estimate=pl.CostEstimate(
            flops=1 << 30, transcendentals=0, bytes_accessed=12 << 20
        ),
    )(z, hidden, *first, *second)


def shards(hidden, store_a, store_b, request_start, request_adapter):
    state = hidden[0]
    mine = block_adapters(request_start[0], request_adapter[0], Y * Z * ROWS)
    segments = X * CORES
    behind = lax.ppermute(mine, SEGMENT, [(s, (s + 1) % segments) for s in range(segments)])
    z = lax.axis_index("z")

    def at_z(chosen):
        rows = chosen.reshape(Y, Z, 2)
        here = lax.broadcasted_iota(jnp.int32, rows.shape, 1) == z
        return jnp.sum(jnp.where(here, rows, 0), axis=1)

    wanted = jnp.stack([at_z(mine), at_z(behind)], axis=1)

    up = [(i, (i + 1) % Z) for i in range(Z)]
    down = [(i, (i - 1) % Z) for i in range(Z)]
    chunks = {(0, 0): store_a[0], (1, 0): store_b[0]}
    for step in range(1, 9):
        for s in (0, 1):
            if step < 8 or s == 0:
                chunks[s, step] = lax.ppermute(chunks[s, step - 1], "z", up)
            if step < 8 or s == 1:
                chunks[s, Z - step] = lax.ppermute(chunks[s, (Z + 1 - step) % Z], "z", down)

    first, second = [], []
    for batch in BATCHES:
        picked = pick(wanted, [chunks[entry] for entry in batch])
        received = lax.all_to_all(picked, "y", split_axis=0, concat_axis=0, tiled=True)
        first.append(received)
        second.append(
            lax.ppermute(
                received[:, 1], SEGMENT, [(s, (s - 1) % segments) for s in range(segments)]
            )
        )
    return layers(z.astype(jnp.int32)[None], state, first, second)[None]


def solution(mesh):
    grid = Mesh(mesh.devices.reshape(X, CORES, Y, Z), ("x", "core", "y", "z"))
    return jax.shard_map(
        shards,
        mesh=grid,
        in_specs=(
            P(SEGMENT, ("y", "z"), None),
            P(SEGMENT, None, None, ("y", "z")),
            P(SEGMENT, None, None, ("y", "z")),
            P(SEGMENT, None),
            P(SEGMENT, None),
        ),
        out_specs=P(SEGMENT, ("y", "z"), None),
        check_vma=False,
    )
```

time: 1130 us -> 315 us (0.28)
  blocking collectives: 825 us -> 0 us
  starting transfers between devices: 28.4 us -> 130 us
  waiting for transfers between devices: 233 us -> 132 us
  local copies, waits for them, and re-layouts: 10.9 us -> 30.9 us
  matrix products: 16.9 us -> 0 us
  Pallas kernels: 0 us -> 15.3 us
    psum x2 -> x0, blocking collectives: 710 us -> none  [apply_layer(): rank = lax.psum(partial_rank, 'dp').astype(jnp.bfloat16)]
    all_to_all x2 -> x5, waiting for transfers between devices: 178 us -> 22.2 us  [shards(): lax.all_to_all(picked, 'y', split_axis=0, concat_axis=0, tiled=True)]
    all_to_all x2 -> x0, blocking collectives: 114 us -> none  [apply_layer(): lax.all_to_all(adapter_update, 'dp', split_axis=0, concat_axis=1, tiled=T...]
    ppermute x4 -> x36, starting transfers between devices: 0.07 us -> 107 us  [the longest x15 70.3 us: shards(): chunks[s, Z - step] = lax.ppermute(chunks[s, (Z + 1 - step) % Z], 'z', down)]
    ppermute x4 -> x36, waiting for transfers between devices: 54.9 us -> 110 us  [the longest x15 69.1 us: shards(): chunks[s, step] = lax.ppermute(chunks[s, step - 1], 'z', up)]
    unnamed x12 -> x60, local copies, waits for them, and re-layouts: 2.2 us -> 22.7 us
    dot_general x4 -> x0, matrix products: 16.9 us -> none  [the longest x2 10.9 us: apply_layer(): jnp.einsum('bic,brc->bir', grouped, down, preferred_element_type=jnp.floa...]
    pallas_call x0 -> x6, Pallas kernels: none -> 15.3 us  [the longest x1 10 us: layers(): pl.pallas_call(layers_kernel, out_shape=jax.ShapeDtypeStruct((ROWS, WIDTH...]
  transfers between devices with their start and end apart: 6 -> 41, of which waited for: 6 -> 21; matrix products, arithmetic and copies ran while one was open for 1% -> 3% of each run, Pallas kernels for 0% -> 1%
where the time goes in v1:
time: 315 us; the launch traced here: 310 us
  waiting for transfers between devices  132 us (42%)
  starting transfers between devices  130 us (41%)
  local copies, waits for them, and re-layouts  30.9 us (10%)
  Pallas kernels  15.3 us (5%)
    ppermute x15, starting transfers between devices, shards(): chunks[s, Z - step] = lax.ppermute(chunks[s, (Z + 1 - step) % Z], 'z', down)  70.3 us
    ppermute x15, waiting for transfers between devices, shards(): chunks[s, step] = lax.ppermute(chunks[s, step - 1], 'z', up)  69.1 us
    ppermute x15, starting transfers between devices, shards(): chunks[s, step] = lax.ppermute(chunks[s, step - 1], 'z', up)  35 us
    all_to_all x5, starting transfers between devices, shards(): lax.all_to_all(picked, 'y', split_axis=0, concat_axis=0, tiled=True)  23.1 us
    unnamed x60, local copies, waits for them, and re-layouts  22.7 us
    all_to_all x5, waiting for transfers between devices, shards(): lax.all_to_all(picked, 'y', split_axis=0, concat_axis=0, tiled=True)  22.2 us
    ppermute x5, waiting for transfers between devices, shards(): lax.ppermute(received[:, 1], SEGMENT, [(s, (s - 1) % segments) for s in r...  21.9 us
    ppermute x15, waiting for transfers between devices, shards(): chunks[s, Z - step] = lax.ppermute(chunks[s, (Z + 1 - step) % Z], 'z', down)  15.9 us
  transfers between devices with their start and end apart: 41, of which 21 were waited for; matrix products, arithmetic and copies ran while one was open for 3% of the time, Pallas kernels for 1%

profile of v1, /device:TPU:6, one launch (start us, length us, event | category | flops | bytes accessed | tf_op | source)
XLA Modules:
  0.0 310.2 jit_solution(11430834198430634138)
XLA Ops:
  0.0 3.8 %collective-permute-start.1 = (bf16[32,64,128]{2,1,0:T(8,128)(2,1)}, bf16[32,64,128]{2,1,0:T(8,128)(2,1)S(1)}, u32[]{:S(2)}, u32[]{:S(2)}) collective-permute-start(bf16[32,64,128]{2,1,0:T(8,128)(2,1)} %bitcast.34), channel_id=1, source_target_pairs={{0,1},{1,2},{2,3},{3,4},{4,5},{5,6},{6,7},{7,8},{8,9},{9,10},{10,1... | collective-permute-start | bytes 1572872 | tf_op jit(solution)/shard_map/ppermute | solution.py:175
  3.8 3.8 %collective-permute-start.2 = (bf16[32,64,128]{2,1,0:T(8,128)(2,1)}, bf16[32,64,128]{2,1,0:T(8,128)(2,1)S(1)}, u32[]{:S(2)}, u32[]{:S(2)}) collective-permute-start(bf16[32,64,128]{2,1,0:T(8,128)(2,1)} %bitcast.37), channel_id=1, source_target_pairs={{0,1},{1,2},{2,3},{3,4},{4,5},{5,6},{6,7},{7,8},{8,9},{9,10},{10,1... | collective-permute-start | bytes 1572872 | tf_op jit(solution)/shard_map/ppermute | solution.py:175
  7.7 7.6 %collective-permute-start.3 = (bf16[32,64,128]{2,1,0:T(8,128)(2,1)}, bf16[32,64,128]{2,1,0:T(8,128)(2,1)S(1)}, u32[]{:S(2)}, u32[]{:S(2)}) collective-permute-start(bf16[32,64,128]{2,1,0:T(8,128)(2,1)} %bitcast.35), channel_id=1, source_target_pairs={{0,15},{1,0},{2,1},{3,2},{4,3},{5,4},{6,5},{7,6},{8,7},{9,8},{10,9... | collective-permute-start | bytes 1572872 | tf_op jit(solution)/shard_map/ppermute | solution.py:177
  15.3 3.9 %collective-permute-start.4 = (bf16[32,64,128]{2,1,0:T(8,128)(2,1)}, bf16[32,64,128]{2,1,0:T(8,128)(2,1)S(1)}, u32[]{:S(2)}, u32[]{:S(2)}) collective-permute-start(bf16[32,64,128]{2,1,0:T(8,128)(2,1)} %bitcast.38), channel_id=1, source_target_pairs={{0,15},{1,0},{2,1},{3,2},{4,3},{5,4},{6,5},{7,6},{8,7},{9,8},{10,9... | collective-permute-start | bytes 1572872 | tf_op jit(solution)/shard_map/ppermute | solution.py:177
  19.2 5.2 %collective-permute-done.1.refs_2_ = bf16[32,64,128]{2,1,0:T(8,128)(2,1)S(1)} collective-permute-done((bf16[32,64,128]{2,1,0:T(8,128)(2,1)}, bf16[32,64,128]{2,1,0:T(8,128)(2,1)S(1)}, u32[]{:S(2)}, u32[]{:S(2)}) %collective-permute-start.1) | collective-permute-done | bytes 524320 | tf_op jit(solution)/shard_map/ppermute | solution.py:175
  27.1 8.5 %collective-permute-done.2.refs_3_ = bf16[32,64,128]{2,1,0:T(8,128)(2,1)S(1)} collective-permute-done((bf16[32,64,128]{2,1,0:T(8,128)(2,1)}, bf16[32,64,128]{2,1,0:T(8,128)(2,1)S(1)}, u32[]{:S(2)}, u32[]{:S(2)}) %collective-permute-start.2) | collective-permute-done | bytes 524320 | tf_op jit(solution)/shard_map/ppermute | solution.py:175
  38.3 5.1 %collective-permute-start.7 = (bf16[32,64,128]{2,1,0:T(8,128)(2,1)S(1)}, bf16[32,64,128]{2,1,0:T(8,128)(2,1)}, u32[]{:S(2)}, u32[]{:S(2)}) collective-permute-start(bf16[32,64,128]{2,1,0:T(8,128)(2,1)S(1)} %collective-permute-done.3.refs_4_), channel_id=1, source_target_pairs={{0,15},{1,0},{2,1},{3,2},{4,3},{5,4},{6,5},{7,6},{8,7},{9,8},{10,9... | collective-permute-start | bytes 1572872 | tf_op jit(solution)/shard_map/ppermute | solution.py:177
  44.2 2.7 collective-permute-start.8
  48.5 3.1 collective-permute-start.9
  51.6 6.5 %collective-permute-done.6.refs_1_ = bf16[32,64,128]{2,1,0:T(8,128)(2,1)} collective-permute-done((bf16[32,64,128]{2,1,0:T(8,128)(2,1)S(1)}, bf16[32,64,128]{2,1,0:T(8,128)(2,1)}, u32[]{:S(2)}, u32[]{:S(2)}) %collective-permute-start.6) | collective-permute-done | bytes 524320 | tf_op jit(solution)/shard_map/ppermute | solution.py:175
  60.1 5.1 %collective-permute-start.11 = (bf16[32,64,128]{2,1,0:T(8,128)(2,1)}, bf16[32,64,128]{2,1,0:T(8,128)(2,1)S(1)}, u32[]{:S(2)}, u32[]{:S(2)}) collective-permute-start(bf16[32,64,128]{2,1,0:T(8,128)(2,1)} %collective-permute-done.7.refs_2_), channel_id=1, source_target_pairs={{0,15},{1,0},{2,1},{3,2},{4,3},{5,4},{6,5},{7,6},{8,7},{9,8},{10,9... | collective-permute-start | bytes 1572872 | tf_op jit(solution)/shard_map/ppermute | solution.py:177
  65.2 5.0 %collective-permute-start.12 = (bf16[32,64,128]{2,1,0:T(8,128)(2,1)}, bf16[32,64,128]{2,1,0:T(8,128)(2,1)S(1)}, u32[]{:S(2)}, u32[]{:S(2)}) collective-permute-start(bf16[32,64,128]{2,1,0:T(8,128)(2,1)} %collective-permute-done.8.refs_3_), channel_id=1, source_target_pairs={{0,15},{1,0},{2,1},{3,2},{4,3},{5,4},{6,5},{7,6},{8,7},{9,8},{10,9... | collective-permute-start | bytes 1572872 | tf_op jit(solution)/shard_map/ppermute | solution.py:177
  71.2 2.8 collective-permute-done
  74.3 5.4 %collective-permute-done.10.refs_5_ = bf16[32,64,128]{2,1,0:T(8,128)(2,1)S(1)} collective-permute-done((bf16[32,64,128]{2,1,0:T(8,128)(2,1)}, bf16[32,64,128]{2,1,0:T(8,128)(2,1)S(1)}, u32[]{:S(2)}, u32[]{:S(2)}) %collective-permute-start.10) | collective-permute-done | bytes 524320 | tf_op jit(solution)/shard_map/ppermute | solution.py:175
  81.3 5.5 %collective-permute-done.12.refs_7_ = bf16[32,64,128]{2,1,0:T(8,128)(2,1)S(1)} collective-permute-done((bf16[32,64,128]{2,1,0:T(8,128)(2,1)}, bf16[32,64,128]{2,1,0:T(8,128)(2,1)S(1)}, u32[]{:S(2)}, u32[]{:S(2)}) %collective-permute-start.12) | collective-permute-done | bytes 524320 | tf_op jit(solution)/shard_map/ppermute | solution.py:177
  91.8 4.6 %all-to-all-start.1 = ((bf16[4,2,8,2,64,128]{5,4,3,2,1,0:T(8,128)(2,1)}), bf16[4,2,8,2,64,128]{5,4,3,2,1,0:T(8,128)(2,1)S(1)}, u32[]{:S(2)}, u32[]{:S(2)}) async-start(bf16[4,2,8,2,64,128]{5,4,3,2,1,0:T(8,128)(2,1)} %copy-done.1), calls=%async_computation.1 | async-start | bytes 4194304 | tf_op jit(solution)/shard_map/all_to_all | solution.py:182
  100.3 5.5 %collective-permute-start.15 = (bf16[32,64,128]{2,1,0:T(8,128)(2,1)S(1)}, bf16[32,64,128]{2,1,0:T(8,128)(2,1)S(1)}, u32[]{:S(2)}, u32[]{:S(2)}) collective-permute-start(bf16[32,64,128]{2,1,0:T(8,128)(2,1)S(1)} %copy-done.17), channel_id=1, source_target_pairs={{0,15},{1,0},{2,1},{3,2},{4,3},{5,4},{6,5},{7,6},{8,7},{9,8},{10,9... | collective-permute-start | bytes 1572872 | tf_op jit(solution)/shard_map/ppermute | solution.py:177
  105.8 3.9 %collective-permute-start.16 = (bf16[32,64,128]{2,1,0:T(8,128)(2,1)S(1)}, bf16[32,64,128]{2,1,0:T(8,128)(2,1)S(1)}, u32[]{:S(2)}, u32[]{:S(2)}) collective-permute-start(bf16[32,64,128]{2,1,0:T(8,128)(2,1)S(1)} %collective-permute-done.12.refs_7_), channel_id=1, source_target_pairs={{0,15},{1,0},{2,1},{3,2},{4,3},{5,4},{6,5},{7,6},{8,7},{9,8},{10,9... | collective-permute-start | bytes 1572872 | tf_op jit(solution)/shard_map/ppermute | solution.py:177
  109.7 5.2 %collective-permute-done.13.refs_0_ = bf16[32,64,128]{2,1,0:T(8,128)(2,1)S(1)} collective-permute-done((bf16[32,64,128]{2,1,0:T(8,128)(2,1)}, bf16[32,64,128]{2,1,0:T(8,128)(2,1)S(1)}, u32[]{:S(2)}, u32[]{:S(2)}) %collective-permute-start.13) | collective-permute-done | bytes 524320 | tf_op jit(solution)/shard_map/ppermute | solution.py:175
  116.9 9.3 %collective-permute-done.14.refs_1_ = bf16[32,64,128]{2,1,0:T(8,128)(2,1)S(1)} collective-permute-done((bf16[32,64,128]{2,1,0:T(8,128)(2,1)}, bf16[32,64,128]{2,1,0:T(8,128)(2,1)S(1)}, u32[]{:S(2)}, u32[]{:S(2)}) %collective-permute-start.14) | collective-permute-done | bytes 524320 | tf_op jit(solution)/shard_map/ppermute | solution.py:175
  128.1 5.1 %collective-permute-start.19 = (bf16[32,64,128]{2,1,0:T(8,128)(2,1)S(1)}, bf16[32,64,128]{2,1,0:T(8,128)(2,1)S(1)}, u32[]{:S(2)}, u32[]{:S(2)}) collective-permute-start(bf16[32,64,128]{2,1,0:T(8,128)(2,1)S(1)} %collective-permute-done.15.refs_2_), channel_id=1, source_target_pairs={{0,15},{1,0},{2,1},{3,2},{4,3},{5,4},{6,5},{7,6},{8,7},{9,8},{10,9... | collective-permute-start | bytes 1572872 | tf_op jit(solution)/shard_map/ppermute | solution.py:177
  133.3 2.7 collective-permute-start.20
  137.4 7.9 %collective-permute-done.18.refs_5_ = bf16[32,64,128]{2,1,0:T(8,128)(2,1)S(1)} collective-permute-done((bf16[32,64,128]{2,1,0:T(8,128)(2,1)S(1)}, bf16[32,64,128]{2,1,0:T(8,128)(2,1)S(1)}, u32[]{:S(2)}, u32[]{:S(2)}) %collective-permute-start.18) | collective-permute-done | bytes 524320 | tf_op jit(solution)/shard_map/ppermute | solution.py:175
  145.3 3.7 %collective-permute-done.20.refs_7_ = bf16[32,64,128]{2,1,0:T(8,128)(2,1)S(1)} collective-permute-done((bf16[32,64,128]{2,1,0:T(8,128)(2,1)S(1)}, bf16[32,64,128]{2,1,0:T(8,128)(2,1)S(1)}, u32[]{:S(2)}, u32[]{:S(2)}) %collective-permute-start.20) | collective-permute-done | bytes 524320 | tf_op jit(solution)/shard_map/ppermute | solution.py:177
  154.4 4.6 %all-to-all-start.2 = ((bf16[4,2,8,2,64,128]{5,4,3,2,1,0:T(8,128)(2,1)}), bf16[4,2,8,2,64,128]{5,4,3,2,1,0:T(8,128)(2,1)}, u32[]{:S(2)}, u32[]{:S(2)}) async-start(bf16[4,2,8,2,64,128]{5,4,3,2,1,0:T(8,128)(2,1)} %copy-done), calls=%async_computation.2 | async-start | bytes 4194304 | tf_op jit(solution)/shard_map/all_to_all | solution.py:182
  159.0 1.9 collective-permute-start.21
  161.0 2.3 collective-permute-start.22
  163.3 5.2 %collective-permute-start.23 = (bf16[32,64,128]{2,1,0:T(8,128)(2,1)}, bf16[32,64,128]{2,1,0:T(8,128)(2,1)S(1)}, u32[]{:S(2)}, u32[]{:S(2)}) collective-permute-start(bf16[32,64,128]{2,1,0:T(8,128)(2,1)} %copy-done.26), channel_id=1, source_target_pairs={{0,15},{1,0},{2,1},{3,2},{4,3},{5,4},{6,5},{7,6},{8,7},{9,8},{10,9... | collective-permute-start | bytes 1572872 | tf_op jit(solution)/shard_map/ppermute | solution.py:177
  168.5 3.9 %collective-permute-start.24 = (bf16[32,64,128]{2,1,0:T(8,128)(2,1)}, bf16[32,64,128]{2,1,0:T(8,128)(2,1)S(1)}, u32[]{:S(2)}, u32[]{:S(2)}) collective-permute-start(bf16[32,64,128]{2,1,0:T(8,128)(2,1)} %copy-done.27), channel_id=1, source_target_pairs={{0,15},{1,0},{2,1},{3,2},{4,3},{5,4},{6,5},{7,6},{8,7},{9,8},{10,9... | collective-permute-start | bytes 1572872 | tf_op jit(solution)/shard_map/ppermute | solution.py:177
  172.5 5.0 %collective-permute-done.21.refs_0_ = bf16[32,64,128]{2,1,0:T(8,128)(2,1)S(1)} collective-permute-done((bf16[32,64,128]{2,1,0:T(8,128)(2,1)S(1)}, bf16[32,64,128]{2,1,0:T(8,128)(2,1)S(1)}, u32[]{:S(2)}, u32[]{:S(2)}) %collective-permute-start.21) | collective-permute-done | bytes 524320 | tf_op jit(solution)/shard_map/ppermute | solution.py:175
  179.4 9.3 %collective-permute-done.22.refs_1_ = bf16[32,64,128]{2,1,0:T(8,128)(2,1)S(1)} collective-permute-done((bf16[32,64,128]{2,1,0:T(8,128)(2,1)S(1)}, bf16[32,64,128]{2,1,0:T(8,128)(2,1)S(1)}, u32[]{:S(2)}, u32[]{:S(2)}) %collective-permute-start.22) | collective-permute-done | bytes 524320 | tf_op jit(solution)/shard_map/ppermute | solution.py:175
  190.6 5.1 %collective-permute-start.27 = (bf16[32,64,128]{2,1,0:T(8,128)(2,1)S(1)}, bf16[32,64,128]{2,1,0:T(8,128)(2,1)S(1)}, u32[]{:S(2)}, u32[]{:S(2)}) collective-permute-start(bf16[32,64,128]{2,1,0:T(8,128)(2,1)S(1)} %collective-permute-done.23.refs_2_), channel_id=1, source_target_pairs={{0,15},{1,0},{2,1},{3,2},{4,3},{5,4},{6,5},{7,6},{8,7},{9,8},{10,9... | collective-permute-start | bytes 1572872 | tf_op jit(solution)/shard_map/ppermute | solution.py:177
  195.8 2.7 collective-permute-start.28
  198.5 4.3 %collective-permute-done.26.refs_5_ = bf16[32,64,128]{2,1,0:T(8,128)(2,1)S(1)} collective-permute-done((bf16[32,64,128]{2,1,0:T(8,128)(2,1)S(1)}, bf16[32,64,128]{2,1,0:T(8,128)(2,1)S(1)}, u32[]{:S(2)}, u32[]{:S(2)}) %collective-permute-start.26) | collective-permute-done | bytes 524320 | tf_op jit(solution)/shard_map/ppermute | solution.py:175
  202.8 5.3 %collective-permute-done.28.refs_7_ = bf16[32,64,128]{2,1,0:T(8,128)(2,1)S(1)} collective-permute-done((bf16[32,64,128]{2,1,0:T(8,128)(2,1)S(1)}, bf16[32,64,128]{2,1,0:T(8,128)(2,1)S(1)}, u32[]{:S(2)}, u32[]{:S(2)}) %collective-permute-start.28) | collective-permute-done | bytes 524320 | tf_op jit(solution)/shard_map/ppermute | solution.py:177
  211.9 4.9 %all-to-all-start.3 = ((bf16[4,2,8,2,64,128]{5,4,3,2,1,0:T(8,128)(2,1)}), bf16[4,2,8,2,64,128]{5,4,3,2,1,0:T(8,128)(2,1)}, u32[]{:S(2)}, u32[]{:S(2)}) async-start(bf16[4,2,8,2,64,128]{5,4,3,2,1,0:T(8,128)(2,1)} %copy-done.2), calls=%async_computation.3 | async-start | bytes 4194304 | tf_op jit(solution)/shard_map/all_to_all | solution.py:182
  222.8 14.8 %all-to-all-done.3.refs_3_ = bf16[4,2,8,2,64,128]{5,4,3,2,1,0:T(8,128)(2,1)} async-done(((bf16[4,2,8,2,64,128]{5,4,3,2,1,0:T(8,128)(2,1)}), bf16[4,2,8,2,64,128]{5,4,3,2,1,0:T(8,128)(2,1)}, u32[]{:S(2)}, u32[]{:S(2)}) %all-to-all-start.3) | async-done | bytes 2097184 | tf_op jit(solution)/shard_map/all_to_all | solution.py:182
  237.5 4.4 %all-to-all-start = ((bf16[4,2,6,2,64,128]{5,4,3,2,1,0:T(8,128)(2,1)}), bf16[4,2,6,2,64,128]{5,4,3,2,1,0:T(8,128)(2,1)}, u32[]{:S(2)}, u32[]{:S(2)}) async-start(bf16[4,2,6,2,64,128]{5,4,3,2,1,0:T(8,128)(2,1)} %copy-done.3), calls=%async_computation | async-start | bytes 3145728 | tf_op jit(solution)/shard_map/all_to_all | solution.py:182
  241.9 2.9 collective-permute-start.29
  244.8 6.5 %collective-permute-start.30 = (bf16[32,64,128]{2,1,0:T(8,128)(2,1)S(1)}, bf16[32,64,128]{2,1,0:T(8,128)(2,1)S(1)}, u32[]{:S(2)}, u32[]{:S(2)}) collective-permute-start(bf16[32,64,128]{2,1,0:T(8,128)(2,1)S(1)} %copy-done.29), channel_id=1, source_target_pairs={{0,15},{1,0},{2,1},{3,2},{4,3},{5,4},{6,5},{7,6},{8,7},{9,8},{10,9... | collective-permute-start | bytes 1572872 | tf_op jit(solution)/shard_map/ppermute | solution.py:177
  252.4 2.3 slice_bitcast_fusion.1
  259.4 2.4 slice_bitcast_fusion
  261.8 4.7 %all-to-all-start.4 = ((bf16[4,2,2,2,64,128]{5,4,3,2,1,0:T(8,128)(2,1)}), bf16[4,2,2,2,64,128]{5,4,3,2,1,0:T(8,128)(2,1)S(1)}, u32[]{:S(2)}, u32[]{:S(2)}) async-start(bf16[4,2,2,2,64,128]{5,4,3,2,1,0:T(8,128)(2,1)} %shard_map.59), calls=%async_computation.4 | async-start | bytes 1048576 | tf_op jit(solution)/shard_map/all_to_all | solution.py:182
  266.5 2.1 slice_bitcast_fusion.3
  269.3 7.4 %all-to-all-done.4.refs_4_ = bf16[4,2,2,2,64,128]{5,4,3,2,1,0:T(8,128)(2,1)S(1)} async-done(((bf16[4,2,2,2,64,128]{5,4,3,2,1,0:T(8,128)(2,1)}), bf16[4,2,2,2,64,128]{5,4,3,2,1,0:T(8,128)(2,1)S(1)}, u32[]{:S(2)}, u32[]{:S(2)}) %all-to-all-start.4) | async-done | bytes 524320 | tf_op jit(solution)/shard_map/all_to_all | solution.py:182
  276.7 19.2 %collective-permute-done.31.refs_5_ = bf16[4,6,2,64,128]{4,3,2,1,0:T(8,128)(2,1)S(1)} collective-permute-done((bf16[4,6,2,64,128]{4,3,2,1,0:T(8,128)(2,1)}, bf16[4,6,2,64,128]{4,3,2,1,0:T(8,128)(2,1)S(1)}, u32[]{:S(2)}, u32[]{:S(2)}) %collective-permute-start.31) | collective-permute-done | bytes 786464 | tf_op jit(solution)/shard_map/ppermute | solution.py:185
  295.9 2.7 collective-permute-done.35.refs_9_
  300.2 10.0 %shard_map.60 = bf16[128,8192]{1,0:T(8,128)(2,1)} custom-call(s32[1]{0:T(128)} %bitcast.z_ref, bf16[128,8192]{1,0:T(8,128)(2,1)S(1)} %bitcast.33, bf16[4,2,6,2,64,128]{5,4,3,2,1,0:T(8,128)(2,1)} %all-to-all-done.refs_0_, bf16[4,2,8,2,64,128]{5,4,3,2,1,0:T(8,128)(2,1)S(1)} %all-to-all-done.1.refs_1_, bf16[4,2,8,2,64,128]{5,4,3,2,1,0:T(8,128)(2,1)} %all-to-all-done.2.refs_2_, ...), custom_call_target="tpu_custom_call" | custom-call | flops 1073741824 | bytes 12582912 | tf_op jit(solution)/shard_map/pallas_call | solution.py:128
  (114 shorter events, 53.6 us)
Async XLA Ops:
  0.0 24.3 %collective-permute-start.1 = (bf16[32,64,128]{2,1,0:T(8,128)(2,1)}, bf16[32,64,128]{2,1,0:T(8,128)(2,1)S(1)}, u32[]{:S(2)}, u32[]{:S(2)}) collective-permute-start(bf16[32,64,128]{2,1,0:T(8,128)(2,1)} %bitcast.34), channel_id=1, source_target_pairs={{0,1},{1,2},{2,3},{3,4},{4,5},{5,6},{6,7},{7,8},{8,9},{9,10},{10,1... | collective-permute-start | bytes 1572872 | tf_op jit(solution)/shard_map/ppermute | solution.py:175
  3.8 31.8 %collective-permute-start.2 = (bf16[32,64,128]{2,1,0:T(8,128)(2,1)}, bf16[32,64,128]{2,1,0:T(8,128)(2,1)S(1)}, u32[]{:S(2)}, u32[]{:S(2)}) collective-permute-start(bf16[32,64,128]{2,1,0:T(8,128)(2,1)} %bitcast.37), channel_id=1, source_target_pairs={{0,1},{1,2},{2,3},{3,4},{4,5},{5,6},{6,7},{7,8},{8,9},{9,10},{10,1... | collective-permute-start | bytes 1572872 | tf_op jit(solution)/shard_map/ppermute | solution.py:175
  7.7 30.6 %collective-permute-start.3 = (bf16[32,64,128]{2,1,0:T(8,128)(2,1)}, bf16[32,64,128]{2,1,0:T(8,128)(2,1)S(1)}, u32[]{:S(2)}, u32[]{:S(2)}) collective-permute-start(bf16[32,64,128]{2,1,0:T(8,128)(2,1)} %bitcast.35), channel_id=1, source_target_pairs={{0,15},{1,0},{2,1},{3,2},{4,3},{5,4},{6,5},{7,6},{8,7},{9,8},{10,9... | collective-permute-start | bytes 1572872 | tf_op jit(solution)/shard_map/ppermute | solution.py:177
  15.3 29.0 %collective-permute-start.4 = (bf16[32,64,128]{2,1,0:T(8,128)(2,1)}, bf16[32,64,128]{2,1,0:T(8,128)(2,1)S(1)}, u32[]{:S(2)}, u32[]{:S(2)}) collective-permute-start(bf16[32,64,128]{2,1,0:T(8,128)(2,1)} %bitcast.38), channel_id=1, source_target_pairs={{0,15},{1,0},{2,1},{3,2},{4,3},{5,4},{6,5},{7,6},{8,7},{9,8},{10,9... | collective-permute-start | bytes 1572872 | tf_op jit(solution)/shard_map/ppermute | solution.py:177
  24.3 24.2 %collective-permute-start.5 = (bf16[32,64,128]{2,1,0:T(8,128)(2,1)S(1)}, bf16[32,64,128]{2,1,0:T(8,128)(2,1)S(1)}, u32[]{:S(2)}, u32[]{:S(2)}) collective-permute-start(bf16[32,64,128]{2,1,0:T(8,128)(2,1)S(1)} %collective-permute-done.1.refs_2_), channel_id=1, source_target_pairs={{0,1},{1,2},{2,3},{3,4},{4,5},{5,6},{6,7},{7,8},{8,9},{9,10},{10,1... | collective-permute-start | bytes 1572872 | tf_op jit(solution)/shard_map/ppermute | solution.py:175
  35.6 22.6 %collective-permute-start.6 = (bf16[32,64,128]{2,1,0:T(8,128)(2,1)S(1)}, bf16[32,64,128]{2,1,0:T(8,128)(2,1)}, u32[]{:S(2)}, u32[]{:S(2)}) collective-permute-start(bf16[32,64,128]{2,1,0:T(8,128)(2,1)S(1)} %collective-permute-done.2.refs_3_), channel_id=1, source_target_pairs={{0,1},{1,2},{2,3},{3,4},{4,5},{5,6},{6,7},{7,8},{8,9},{9,10},{10,1... | collective-permute-start | bytes 1572872 | tf_op jit(solution)/shard_map/ppermute | solution.py:175
  38.3 21.8 %collective-permute-start.7 = (bf16[32,64,128]{2,1,0:T(8,128)(2,1)S(1)}, bf16[32,64,128]{2,1,0:T(8,128)(2,1)}, u32[]{:S(2)}, u32[]{:S(2)}) collective-permute-start(bf16[32,64,128]{2,1,0:T(8,128)(2,1)S(1)} %collective-permute-done.3.refs_4_), channel_id=1, source_target_pairs={{0,15},{1,0},{2,1},{3,2},{4,3},{5,4},{6,5},{7,6},{8,7},{9,8},{10,9... | collective-permute-start | bytes 1572872 | tf_op jit(solution)/shard_map/ppermute | solution.py:177
  44.2 21.0 %collective-permute-start.8 = (bf16[32,64,128]{2,1,0:T(8,128)(2,1)S(1)}, bf16[32,64,128]{2,1,0:T(8,128)(2,1)}, u32[]{:S(2)}, u32[]{:S(2)}) collective-permute-start(bf16[32,64,128]{2,1,0:T(8,128)(2,1)S(1)} %collective-permute-done.4.refs_5_), channel_id=1, source_target_pairs={{0,15},{1,0},{2,1},{3,2},{4,3},{5,4},{6,5},{7,6},{8,7},{9,8},{10,9... | collective-permute-start | bytes 1572872 | tf_op jit(solution)/shard_map/ppermute | solution.py:177
  48.5 25.7 %collective-permute-start.9 = (bf16[32,64,128]{2,1,0:T(8,128)(2,1)S(1)}, bf16[32,64,128]{2,1,0:T(8,128)(2,1)}, u32[]{:S(2)}, u32[]{:S(2)}) collective-permute-start(bf16[32,64,128]{2,1,0:T(8,128)(2,1)S(1)} %collective-permute-done.5.refs_0_), channel_id=1, source_target_pairs={{0,1},{1,2},{2,3},{3,4},{4,5},{5,6},{6,7},{7,8},{8,9},{9,10},{10,1... | collective-permute-start | bytes 1572872 | tf_op jit(solution)/shard_map/ppermute | solution.py:175
  58.2 21.5 %collective-permute-start.10 = (bf16[32,64,128]{2,1,0:T(8,128)(2,1)}, bf16[32,64,128]{2,1,0:T(8,128)(2,1)S(1)}, u32[]{:S(2)}, u32[]{:S(2)}) collective-permute-start(bf16[32,64,128]{2,1,0:T(8,128)(2,1)} %collective-permute-done.6.refs_1_), channel_id=1, source_target_pairs={{0,1},{1,2},{2,3},{3,4},{4,5},{5,6},{6,7},{7,8},{8,9},{9,10},{10,1... | collective-permute-start | bytes 1572872 | tf_op jit(solution)/shard_map/ppermute | solution.py:175
  60.1 20.4 %collective-permute-start.11 = (bf16[32,64,128]{2,1,0:T(8,128)(2,1)}, bf16[32,64,128]{2,1,0:T(8,128)(2,1)S(1)}, u32[]{:S(2)}, u32[]{:S(2)}) collective-permute-start(bf16[32,64,128]{2,1,0:T(8,128)(2,1)} %collective-permute-done.7.refs_2_), channel_id=1, source_target_pairs={{0,15},{1,0},{2,1},{3,2},{4,3},{5,4},{6,5},{7,6},{8,7},{9,8},{10,9... | collective-permute-start | bytes 1572872 | tf_op jit(solution)/shard_map/ppermute | solution.py:177
  65.2 21.5 %collective-permute-start.12 = (bf16[32,64,128]{2,1,0:T(8,128)(2,1)}, bf16[32,64,128]{2,1,0:T(8,128)(2,1)S(1)}, u32[]{:S(2)}, u32[]{:S(2)}) collective-permute-start(bf16[32,64,128]{2,1,0:T(8,128)(2,1)} %collective-permute-done.8.refs_3_), channel_id=1, source_target_pairs={{0,15},{1,0},{2,1},{3,2},{4,3},{5,4},{6,5},{7,6},{8,7},{9,8},{10,9... | collective-permute-start | bytes 1572872 | tf_op jit(solution)/shard_map/ppermute | solution.py:177
  71.0 3.0 collective-permute-start
  91.8 8.4 %copy-start.17 = (bf16[32,64,128]{2,1,0:T(8,128)(2,1)S(1)}, bf16[32,64,128]{2,1,0:T(8,128)(2,1)}, u32[]{:S(2)}) copy-start(bf16[32,64,128]{2,1,0:T(8,128)(2,1)} %copy-done.15) | copy-start | bytes 1572868
  91.8 62.6 %all-to-all-start.1 = ((bf16[4,2,8,2,64,128]{5,4,3,2,1,0:T(8,128)(2,1)}), bf16[4,2,8,2,64,128]{5,4,3,2,1,0:T(8,128)(2,1)S(1)}, u32[]{:S(2)}, u32[]{:S(2)}) async-start(bf16[4,2,8,2,64,128]{5,4,3,2,1,0:T(8,128)(2,1)} %copy-done.1), calls=%async_computation.1 | async-start | bytes 4194304 | tf_op jit(solution)/shard_map/all_to_all | solution.py:182
  96.4 18.5 %collective-permute-start.13 = (bf16[32,64,128]{2,1,0:T(8,128)(2,1)}, bf16[32,64,128]{2,1,0:T(8,128)(2,1)S(1)}, u32[]{:S(2)}, u32[]{:S(2)}) collective-permute-start(bf16[32,64,128]{2,1,0:T(8,128)(2,1)} %collective-permute-done.9.refs_4_), channel_id=1, source_target_pairs={{0,1},{1,2},{2,3},{3,4},{4,5},{5,6},{6,7},{7,8},{8,9},{9,10},{10,1... | collective-permute-start | bytes 1572872 | tf_op jit(solution)/shard_map/ppermute | solution.py:175
  98.3 27.8 %collective-permute-start.14 = (bf16[32,64,128]{2,1,0:T(8,128)(2,1)}, bf16[32,64,128]{2,1,0:T(8,128)(2,1)S(1)}, u32[]{:S(2)}, u32[]{:S(2)}) collective-permute-start(bf16[32,64,128]{2,1,0:T(8,128)(2,1)} %copy-done.18), channel_id=1, source_target_pairs={{0,1},{1,2},{2,3},{3,4},{4,5},{5,6},{6,7},{7,8},{8,9},{9,10},{10,1... | collective-permute-start | bytes 1572872 | tf_op jit(solution)/shard_map/ppermute | solution.py:175
  100.3 27.8 %collective-permute-start.15 = (bf16[32,64,128]{2,1,0:T(8,128)(2,1)S(1)}, bf16[32,64,128]{2,1,0:T(8,128)(2,1)S(1)}, u32[]{:S(2)}, u32[]{:S(2)}) collective-permute-start(bf16[32,64,128]{2,1,0:T(8,128)(2,1)S(1)} %copy-done.17), channel_id=1, source_target_pairs={{0,15},{1,0},{2,1},{3,2},{4,3},{5,4},{6,5},{7,6},{8,7},{9,8},{10,9... | collective-permute-start | bytes 1572872 | tf_op jit(solution)/shard_map/ppermute | solution.py:177
  105.8 27.5 %collective-permute-start.16 = (bf16[32,64,128]{2,1,0:T(8,128)(2,1)S(1)}, bf16[32,64,128]{2,1,0:T(8,128)(2,1)S(1)}, u32[]{:S(2)}, u32[]{:S(2)}) collective-permute-start(bf16[32,64,128]{2,1,0:T(8,128)(2,1)S(1)} %collective-permute-done.12.refs_7_), channel_id=1, source_target_pairs={{0,15},{1,0},{2,1},{3,2},{4,3},{5,4},{6,5},{7,6},{8,7},{9,8},{10,9... | collective-permute-start | bytes 1572872 | tf_op jit(solution)/shard_map/ppermute | solution.py:177
  114.9 22.5 %collective-permute-start.17 = (bf16[32,64,128]{2,1,0:T(8,128)(2,1)S(1)}, bf16[32,64,128]{2,1,0:T(8,128)(2,1)S(1)}, u32[]{:S(2)}, u32[]{:S(2)}) collective-permute-start(bf16[32,64,128]{2,1,0:T(8,128)(2,1)S(1)} %collective-permute-done.13.refs_0_), channel_id=1, source_target_pairs={{0,1},{1,2},{2,3},{3,4},{4,5},{5,6},{6,7},{7,8},{8,9},{9,10},{10,1... | collective-permute-start | bytes 1572872 | tf_op jit(solution)/shard_map/ppermute | solution.py:175
  126.2 19.2 %collective-permute-start.18 = (bf16[32,64,128]{2,1,0:T(8,128)(2,1)S(1)}, bf16[32,64,128]{2,1,0:T(8,128)(2,1)S(1)}, u32[]{:S(2)}, u32[]{:S(2)}) collective-permute-start(bf16[32,64,128]{2,1,0:T(8,128)(2,1)S(1)} %collective-permute-done.14.refs_1_), channel_id=1, source_target_pairs={{0,1},{1,2},{2,3},{3,4},{4,5},{5,6},{6,7},{7,8},{8,9},{9,10},{10,1... | collective-permute-start | bytes 1572872 | tf_op jit(solution)/shard_map/ppermute | solution.py:175
  128.1 17.2 %collective-permute-start.19 = (bf16[32,64,128]{2,1,0:T(8,128)(2,1)S(1)}, bf16[32,64,128]{2,1,0:T(8,128)(2,1)S(1)}, u32[]{:S(2)}, u32[]{:S(2)}) collective-permute-start(bf16[32,64,128]{2,1,0:T(8,128)(2,1)S(1)} %collective-permute-done.15.refs_2_), channel_id=1, source_target_pairs={{0,15},{1,0},{2,1},{3,2},{4,3},{5,4},{6,5},{7,6},{8,7},{9,8},{10,9... | collective-permute-start | bytes 1572872 | tf_op jit(solution)/shard_map/ppermute | solution.py:177
  133.3 15.8 %collective-permute-start.20 = (bf16[32,64,128]{2,1,0:T(8,128)(2,1)S(1)}, bf16[32,64,128]{2,1,0:T(8,128)(2,1)S(1)}, u32[]{:S(2)}, u32[]{:S(2)}) collective-permute-start(bf16[32,64,128]{2,1,0:T(8,128)(2,1)S(1)} %collective-permute-done.16.refs_3_), channel_id=1, source_target_pairs={{0,15},{1,0},{2,1},{3,2},{4,3},{5,4},{6,5},{7,6},{8,7},{9,8},{10,9... | collective-permute-start | bytes 1572872 | tf_op jit(solution)/shard_map/ppermute | solution.py:177
  154.4 4.6 %copy-start.23 = (bf16[32,64,128]{2,1,0:T(8,128)(2,1)S(1)}, bf16[32,64,128]{2,1,0:T(8,128)(2,1)}, u32[]{:S(2)}) copy-start(bf16[32,64,128]{2,1,0:T(8,128)(2,1)} %copy-done.22) | copy-start | bytes 1572868
  154.4 6.5 %copy-start.25 = (bf16[32,64,128]{2,1,0:T(8,128)(2,1)S(1)}, bf16[32,64,128]{2,1,0:T(8,128)(2,1)}, u32[]{:S(2)}) copy-start(bf16[32,64,128]{2,1,0:T(8,128)(2,1)} %copy-done.24) | copy-start | bytes 1572868
  154.4 57.4 %all-to-all-start.2 = ((bf16[4,2,8,2,64,128]{5,4,3,2,1,0:T(8,128)(2,1)}), bf16[4,2,8,2,64,128]{5,4,3,2,1,0:T(8,128)(2,1)}, u32[]{:S(2)}, u32[]{:S(2)}) async-start(bf16[4,2,8,2,64,128]{5,4,3,2,1,0:T(8,128)(2,1)} %copy-done), calls=%async_computation.2 | async-start | bytes 4194304 | tf_op jit(solution)/shard_map/all_to_all | solution.py:182
  159.0 18.4 %collective-permute-start.21 = (bf16[32,64,128]{2,1,0:T(8,128)(2,1)S(1)}, bf16[32,64,128]{2,1,0:T(8,128)(2,1)S(1)}, u32[]{:S(2)}, u32[]{:S(2)}) collective-permute-start(bf16[32,64,128]{2,1,0:T(8,128)(2,1)S(1)} %copy-done.23), channel_id=1, source_target_pairs={{0,1},{1,2},{2,3},{3,4},{4,5},{5,6},{6,7},{7,8},{8,9},{9,10},{10,1... | collective-permute-start | bytes 1572872 | tf_op jit(solution)/shard_map/ppermute | solution.py:175
  161.0 27.7 %collective-permute-start.22 = (bf16[32,64,128]{2,1,0:T(8,128)(2,1)S(1)}, bf16[32,64,128]{2,1,0:T(8,128)(2,1)S(1)}, u32[]{:S(2)}, u32[]{:S(2)}) collective-permute-start(bf16[32,64,128]{2,1,0:T(8,128)(2,1)S(1)} %copy-done.25), channel_id=1, source_target_pairs={{0,1},{1,2},{2,3},{3,4},{4,5},{5,6},{6,7},{7,8},{8,9},{9,10},{10,1... | collective-permute-start | bytes 1572872 | tf_op jit(solution)/shard_map/ppermute | solution.py:175
  163.3 27.3 %collective-permute-start.23 = (bf16[32,64,128]{2,1,0:T(8,128)(2,1)}, bf16[32,64,128]{2,1,0:T(8,128)(2,1)S(1)}, u32[]{:S(2)}, u32[]{:S(2)}) collective-permute-start(bf16[32,64,128]{2,1,0:T(8,128)(2,1)} %copy-done.26), channel_id=1, source_target_pairs={{0,15},{1,0},{2,1},{3,2},{4,3},{5,4},{6,5},{7,6},{8,7},{9,8},{10,9... | collective-permute-start | bytes 1572872 | tf_op jit(solution)/shard_map/ppermute | solution.py:177
  168.5 27.3 %collective-permute-start.24 = (bf16[32,64,128]{2,1,0:T(8,128)(2,1)}, bf16[32,64,128]{2,1,0:T(8,128)(2,1)S(1)}, u32[]{:S(2)}, u32[]{:S(2)}) collective-permute-start(bf16[32,64,128]{2,1,0:T(8,128)(2,1)} %copy-done.27), channel_id=1, source_target_pairs={{0,15},{1,0},{2,1},{3,2},{4,3},{5,4},{6,5},{7,6},{8,7},{9,8},{10,9... | collective-permute-start | bytes 1572872 | tf_op jit(solution)/shard_map/ppermute | solution.py:177
  177.5 21.0 %collective-permute-start.25 = (bf16[32,64,128]{2,1,0:T(8,128)(2,1)S(1)}, bf16[32,64,128]{2,1,0:T(8,128)(2,1)S(1)}, u32[]{:S(2)}, u32[]{:S(2)}) collective-permute-start(bf16[32,64,128]{2,1,0:T(8,128)(2,1)S(1)} %collective-permute-done.21.refs_0_), channel_id=1, source_target_pairs={{0,1},{1,2},{2,3},{3,4},{4,5},{5,6},{6,7},{7,8},{8,9},{9,10},{10,1... | collective-permute-start | bytes 1572872 | tf_op jit(solution)/shard_map/ppermute | solution.py:175
  188.7 14.1 %collective-permute-start.26 = (bf16[32,64,128]{2,1,0:T(8,128)(2,1)S(1)}, bf16[32,64,128]{2,1,0:T(8,128)(2,1)S(1)}, u32[]{:S(2)}, u32[]{:S(2)}) collective-permute-start(bf16[32,64,128]{2,1,0:T(8,128)(2,1)S(1)} %collective-permute-done.22.refs_1_), channel_id=1, source_target_pairs={{0,1},{1,2},{2,3},{3,4},{4,5},{5,6},{6,7},{7,8},{8,9},{9,10},{10,1... | collective-permute-start | bytes 1572872 | tf_op jit(solution)/shard_map/ppermute | solution.py:175
  190.6 12.2 %collective-permute-start.27 = (bf16[32,64,128]{2,1,0:T(8,128)(2,1)S(1)}, bf16[32,64,128]{2,1,0:T(8,128)(2,1)S(1)}, u32[]{:S(2)}, u32[]{:S(2)}) collective-permute-start(bf16[32,64,128]{2,1,0:T(8,128)(2,1)S(1)} %collective-permute-done.23.refs_2_), channel_id=1, source_target_pairs={{0,15},{1,0},{2,1},{3,2},{4,3},{5,4},{6,5},{7,6},{8,7},{9,8},{10,9... | collective-permute-start | bytes 1572872 | tf_op jit(solution)/shard_map/ppermute | solution.py:177
  195.8 12.3 %collective-permute-start.28 = (bf16[32,64,128]{2,1,0:T(8,128)(2,1)S(1)}, bf16[32,64,128]{2,1,0:T(8,128)(2,1)S(1)}, u32[]{:S(2)}, u32[]{:S(2)}) collective-permute-start(bf16[32,64,128]{2,1,0:T(8,128)(2,1)S(1)} %collective-permute-done.24.refs_3_), channel_id=1, source_target_pairs={{0,15},{1,0},{2,1},{3,2},{4,3},{5,4},{6,5},{7,6},{8,7},{9,8},{10,9... | collective-permute-start | bytes 1572872 | tf_op jit(solution)/shard_map/ppermute | solution.py:177
  211.9 4.9 %copy-start.5 = (bf16[1,32,64,128]{3,2,1,0:T(8,128)(2,1)S(1)}, bf16[1,32,64,128]{3,2,1,0:T(8,128)(2,1)}, u32[]{:S(2)}) copy-start(bf16[1,32,64,128]{3,2,1,0:T(8,128)(2,1)} %param.6) | copy-start | bytes 1572868
  211.9 4.9 %copy-start.6 = (bf16[1,32,64,128]{3,2,1,0:T(8,128)(2,1)S(1)}, bf16[1,32,64,128]{3,2,1,0:T(8,128)(2,1)}, u32[]{:S(2)}) copy-start(bf16[1,32,64,128]{3,2,1,0:T(8,128)(2,1)} %param.7) | copy-start | bytes 1572868
  211.9 25.7 %all-to-all-start.3 = ((bf16[4,2,8,2,64,128]{5,4,3,2,1,0:T(8,128)(2,1)}), bf16[4,2,8,2,64,128]{5,4,3,2,1,0:T(8,128)(2,1)}, u32[]{:S(2)}, u32[]{:S(2)}) async-start(bf16[4,2,8,2,64,128]{5,4,3,2,1,0:T(8,128)(2,1)} %copy-done.2), calls=%async_computation.3 | async-start | bytes 4194304 | tf_op jit(solution)/shard_map/all_to_all | solution.py:182
  222.8 19.1 %copy-start.21 = (bf16[32,64,128]{2,1,0:T(8,128)(2,1)S(1)}, bf16[32,64,128]{2,1,0:T(8,128)(2,1)}, u32[]{:S(2)}) copy-start(bf16[32,64,128]{2,1,0:T(8,128)(2,1)} %copy-done.20) | copy-start | bytes 1572868
  222.8 22.0 %copy-start.29 = (bf16[32,64,128]{2,1,0:T(8,128)(2,1)S(1)}, bf16[32,64,128]{2,1,0:T(8,128)(2,1)}, u32[]{:S(2)}) copy-start(bf16[32,64,128]{2,1,0:T(8,128)(2,1)} %copy-done.28) | copy-start | bytes 1572868
  237.5 24.2 %all-to-all-start = ((bf16[4,2,6,2,64,128]{5,4,3,2,1,0:T(8,128)(2,1)}), bf16[4,2,6,2,64,128]{5,4,3,2,1,0:T(8,128)(2,1)}, u32[]{:S(2)}, u32[]{:S(2)}) async-start(bf16[4,2,6,2,64,128]{5,4,3,2,1,0:T(8,128)(2,1)} %copy-done.3), calls=%async_computation | async-start | bytes 3145728 | tf_op jit(solution)/shard_map/all_to_all | solution.py:182
  241.9 14.6 %collective-permute-start.29 = (bf16[32,64,128]{2,1,0:T(8,128)(2,1)S(1)}, bf16[32,64,128]{2,1,0:T(8,128)(2,1)S(1)}, u32[]{:S(2)}, u32[]{:S(2)}) collective-permute-start(bf16[32,64,128]{2,1,0:T(8,128)(2,1)S(1)} %copy-done.21), channel_id=1, source_target_pairs={{0,1},{1,2},{2,3},{3,4},{4,5},{5,6},{6,7},{7,8},{8,9},{9,10},{10,1... | collective-permute-start | bytes 1572872 | tf_op jit(solution)/shard_map/ppermute | solution.py:175
  244.8 13.2 %collective-permute-start.30 = (bf16[32,64,128]{2,1,0:T(8,128)(2,1)S(1)}, bf16[32,64,128]{2,1,0:T(8,128)(2,1)S(1)}, u32[]{:S(2)}, u32[]{:S(2)}) collective-permute-start(bf16[32,64,128]{2,1,0:T(8,128)(2,1)S(1)} %copy-done.29), channel_id=1, source_target_pairs={{0,15},{1,0},{2,1},{3,2},{4,3},{5,4},{6,5},{7,6},{8,7},{9,8},{10,9... | collective-permute-start | bytes 1572872 | tf_op jit(solution)/shard_map/ppermute | solution.py:177
  252.4 43.5 %collective-permute-start.32 = (bf16[4,8,2,64,128]{4,3,2,1,0:T(8,128)(2,1)}, bf16[4,8,2,64,128]{4,3,2,1,0:T(8,128)(2,1)}, u32[]{:S(2)}, u32[]{:S(2)}) collective-permute-start(bf16[4,8,2,64,128]{4,3,2,1,0:T(8,128)(2,1)} %slice_bitcast_fusion.2), channel_id=1, source_target_pairs={{0,448},{64,0},{128,64},{192,128},{256,192},{320,256},{384,320},{4... | collective-permute-start | bytes 3145736 | tf_op jit(solution)/shard_map/ppermute | solution.py:185
  254.7 43.9 %collective-permute-start.33 = (bf16[4,8,2,64,128]{4,3,2,1,0:T(8,128)(2,1)}, bf16[4,8,2,64,128]{4,3,2,1,0:T(8,128)(2,1)}, u32[]{:S(2)}, u32[]{:S(2)}) collective-permute-start(bf16[4,8,2,64,128]{4,3,2,1,0:T(8,128)(2,1)} %slice_bitcast_fusion.1), channel_id=1, source_target_pairs={{0,448},{64,0},{128,64},{192,128},{256,192},{320,256},{384,320},{4... | collective-permute-start | bytes 3145736 | tf_op jit(solution)/shard_map/ppermute | solution.py:185
  261.8 36.9 %collective-permute-start.34 = (bf16[4,8,2,64,128]{4,3,2,1,0:T(8,128)(2,1)}, bf16[4,8,2,64,128]{4,3,2,1,0:T(8,128)(2,1)}, u32[]{:S(2)}, u32[]{:S(2)}) collective-permute-start(bf16[4,8,2,64,128]{4,3,2,1,0:T(8,128)(2,1)} %slice_bitcast_fusion), channel_id=1, source_target_pairs={{0,448},{64,0},{128,64},{192,128},{256,192},{320,256},{384,320},{4... | collective-permute-start | bytes 3145736 | tf_op jit(solution)/shard_map/ppermute | solution.py:185
  261.8 14.9 %all-to-all-start.4 = ((bf16[4,2,2,2,64,128]{5,4,3,2,1,0:T(8,128)(2,1)}), bf16[4,2,2,2,64,128]{5,4,3,2,1,0:T(8,128)(2,1)S(1)}, u32[]{:S(2)}, u32[]{:S(2)}) async-start(bf16[4,2,2,2,64,128]{5,4,3,2,1,0:T(8,128)(2,1)} %shard_map.59), calls=%async_computation.4 | async-start | bytes 1048576 | tf_op jit(solution)/shard_map/all_to_all | solution.py:182
  268.6 27.3 %collective-permute-start.31 = (bf16[4,6,2,64,128]{4,3,2,1,0:T(8,128)(2,1)}, bf16[4,6,2,64,128]{4,3,2,1,0:T(8,128)(2,1)S(1)}, u32[]{:S(2)}, u32[]{:S(2)}) collective-permute-start(bf16[4,6,2,64,128]{4,3,2,1,0:T(8,128)(2,1)} %slice_bitcast_fusion.3), channel_id=1, source_target_pairs={{0,448},{64,0},{128,64},{192,128},{256,192},{320,256},{384,320},{4... | collective-permute-start | bytes 2359304 | tf_op jit(solution)/shard_map/ppermute | solution.py:185
  276.7 21.9 %collective-permute-start.35 = (bf16[4,2,2,64,128]{4,3,2,1,0:T(8,128)(2,1)S(1)}, bf16[4,2,2,64,128]{4,3,2,1,0:T(8,128)(2,1)S(1)}, u32[]{:S(2)}, u32[]{:S(2)}) collective-permute-start(bf16[4,2,2,64,128]{4,3,2,1,0:T(8,128)(2,1)S(1)} %slice_bitcast_fusion.4), channel_id=1, source_target_pairs={{0,448},{64,0},{128,64},{192,128},{256,192},{320,256},{384,320},{4... | collective-permute-start | bytes 786440 | tf_op jit(solution)/shard_map/ppermute | solution.py:185
  (23 other events, 22.8 us)

commit v2 on v1

v2 whole, which is shorter than its diff:
```python
import functools

import jax
import jax.numpy as jnp
from jax import lax
from jax.experimental import pallas as pl
from jax.experimental.pallas import tpu as pltpu
from jax.sharding import Mesh, PartitionSpec as P

BLOCK = 64
EPS = 1e-05
ADAPTER_SCALE = 0.5
X, CORES, Y, Z = 4, 2, 4, 16
SEGMENT = ("x", "core")
LANES = 128
ROWS = 128
WIDTH = 8192
RANK = 64

BATCHES = ((0, 1, 15), (2, 14, 3, 13), (4, 12, 5, 11), (6, 10, 7, 9), (8,))
ORDER = tuple(d for batch in BATCHES for d in batch)
PARTS = 2
PART = RANK // PARTS


def block_adapters(starts, adapters, total_rows):
    blocks = total_rows // BLOCK
    block_start = jnp.arange(blocks, dtype=jnp.int32) * BLOCK
    request = jnp.sum((starts[None, :] <= block_start[:, None]).astype(jnp.int32), axis=1) - 1
    labels = jnp.arange(adapters.shape[0], dtype=jnp.int32)
    picked = jnp.where(request[:, None] == labels[None, :], adapters[None, :], 0)
    return jnp.sum(picked, axis=1)


def pick_kernel(count, *refs):
    wanted, chunks, out, sem = refs[0], refs[1 : 1 + count], refs[-2], refs[-1]
    for y in range(Y):
        for k in range(2):
            for b in range(2):
                which = wanted[y, k, b]
                for c in range(count):
                    pltpu.make_async_copy(chunks[c].at[which], out.at[y, k, c, b], sem).start()
    pltpu.make_async_copy(out, out, sem).wait()


def pick(wanted, chunks, after):
    count = len(chunks)
    anywhere = pl.BlockSpec(memory_space=pltpu.HBM)
    return pl.pallas_call(
        functools.partial(pick_kernel, count),
        out_shape=jax.ShapeDtypeStruct((Y, 2, count, 2, RANK, LANES), jnp.bfloat16),
        in_specs=[pl.BlockSpec(memory_space=pltpu.SMEM)] + [anywhere] * (count + len(after)),
        out_specs=anywhere,
        scratch_shapes=[pltpu.SemaphoreType.DMA],
        cost_estimate=pl.CostEstimate(
            flops=0, transcendentals=0, bytes_accessed=count * (1 << 19)
        ),
    )(wanted, *chunks, *after)


def pick_gathered_kernel(wanted, gathered, *refs):
    mine, theirs, sem, their_sem = refs[-4:]
    for k, (out, s) in enumerate(((mine, sem), (theirs, their_sem))):
        for y in range(Y):
            for b in range(2):
                pltpu.make_async_copy(
                    gathered.at[:, wanted[y, k, b]], out.at[y, :, b], s
                ).start()
    pltpu.make_async_copy(mine, mine, sem).wait()
    pltpu.make_async_copy(theirs, theirs, their_sem).wait()


def pick_gathered(wanted, gathered, after):
    anywhere = pl.BlockSpec(memory_space=pltpu.HBM)
    return pl.pallas_call(
        pick_gathered_kernel,
        out_shape=[jax.ShapeDtypeStruct((Y, Z, 2, PART, LANES), jnp.bfloat16)] * 2,
        in_specs=[pl.BlockSpec(memory_space=pltpu.SMEM)] + [anywhere] * (1 + len(after)),
        out_specs=[anywhere] * 2,
        scratch_shapes=[pltpu.SemaphoreType.DMA] * 2,
        cost_estimate=pl.CostEstimate(
            flops=0, transcendentals=0, bytes_accessed=(8 << 20) // PARTS
        ),
    )(wanted, gathered, *after)


def layers_kernel(z_ref, *refs):
    n, m = len(BATCHES), PARTS
    hidden_hbm, refs = refs[0], refs[1:]
    down, refs = (refs[:m], refs[m : 2 * m]), refs[2 * m :]
    first, second, refs = refs[:n], refs[n : 2 * n], refs[2 * n :]
    out_hbm, hidden, state, out, a0, b0, a1, b1, sems = refs
    z = z_ref[0]
    copies = {}

    def copy(key, src, dst):
        copies.setdefault(key, []).append(
            pltpu.make_async_copy(src, dst, sems.at[sum(len(v) for v in copies.values())])
        )

    copy("hidden", hidden_hbm, hidden)
    for step, a_ref, b_ref in ((0, a0, b0), (1, a1, b1)):
        for p in range(PARTS):
            copy((step, 0), down[step][p], a_ref.at[:, :, :, pl.ds(p * PART, PART)])
        at = 0
        for b, batch in enumerate(BATCHES):
            src = first[b].at[:, 0] if step == 0 else second[b]
            copy((step, 1), src, b_ref.at[:, pl.ds(at, len(batch))])
            at += len(batch)
    for group in copies.values():
        for c in group:
            c.start()

    def arrived(key):
        for c in copies[key]:
            c.wait()

    def source(d):
        return (z - d) & (Z - 1)

    def place(y, d):
        return pl.ds(pl.multiple_of((y * Z + source(d)) * LANES, LANES), LANES)

    def down_panels(ref, y, ds):
        return jnp.concatenate(
            [ref[y, source(d)].reshape(2 * RANK, LANES) for d in ds], axis=1
        )

    def up_panels(ref, y, i):
        return jnp.concatenate(
            [ref[y, i + j].reshape(2 * RANK, LANES) for j in range(4)], axis=1
        )

    own = lax.broadcasted_iota(jnp.int32, (ROWS, 2 * RANK), 0) // BLOCK == (
        lax.broadcasted_iota(jnp.int32, (ROWS, 2 * RANK), 1) // RANK
    )
    groups = [(y, i, ORDER[i : i + 4]) for y in range(Y) for i in range(0, Z, 4)]

    def slot(y, i, width):
        return pl.ds((y * Z + i) * LANES, width * LANES)

    arrived("hidden")
    total = jnp.zeros((ROWS, LANES), jnp.float32)
    for y, i, ds in groups:
        for j, d in enumerate(ds):
            v = hidden[:, place(y, d)]
            state[:, slot(y, i + j, 1)] = v
            v = v.astype(jnp.float32)
            total = total + v * v

    for step, a_ref, b_ref in ((0, a0, b0), (1, a1, b1)):
        scale = lax.rsqrt(jnp.sum(total, axis=1, keepdims=True) / WIDTH + EPS)
        scale = jnp.broadcast_to(scale, (ROWS, 4 * LANES))
        rank = jnp.zeros((ROWS, 2 * RANK), jnp.float32)
        arrived((step, 0))
        for y, i, ds in groups:
            v = (state[:, slot(y, i, 4)].astype(jnp.float32) * scale).astype(jnp.bfloat16)
            rank = rank + lax.dot_general(
                v, down_panels(a_ref, y, ds), (((1,), (1,)), ((), ())),
                preferred_element_type=jnp.float32,
            )
        rank = jnp.where(own, rank, 0.0).astype(jnp.bfloat16)
        total = jnp.zeros((ROWS, LANES), jnp.float32)
        arrived((step, 1))
        for y, i, ds in groups:
            delta = jnp.dot(rank, up_panels(b_ref, y, i), preferred_element_type=jnp.float32)
            delta = delta.astype(jnp.bfloat16).astype(jnp.float32)
            new = state[:, slot(y, i, 4)].astype(jnp.float32) + ADAPTER_SCALE * delta
            new = new.astype(jnp.bfloat16)
            if step == 0:
                state[:, slot(y, i, 4)] = new
                v = new.astype(jnp.float32)
                v = v * v
                for j in range(4):
                    total = total + v[:, j * LANES : (j + 1) * LANES]
            else:
                for j, d in enumerate(ds):
                    out[:, place(y, d)] = new[:, j * LANES : (j + 1) * LANES]
                if i + 4 == Z:
                    part = pl.ds(y * Z * LANES, Z * LANES)
                    copy("out", out.at[:, part], out_hbm.at[:, part])
                    copies["out"][-1].start()
    arrived("out")


def layers(z, hidden, down, first, second):
    anywhere = pl.BlockSpec(memory_space=pltpu.HBM)
    rows = pltpu.VMEM((ROWS, WIDTH), jnp.bfloat16)
    store = pltpu.VMEM((Y, Z, 2, RANK, LANES), jnp.bfloat16)
    return pl.pallas_call(
        layers_kernel,
        out_shape=jax.ShapeDtypeStruct((ROWS, WIDTH), jnp.bfloat16),
        in_specs=[pl.BlockSpec(memory_space=pltpu.SMEM)]
        + [anywhere] * (1 + 2 * PARTS + 2 * len(BATCHES)),
        out_specs=anywhere,
        scratch_shapes=[rows] * 3
        + [store] * 4
        + [pltpu.SemaphoreType.DMA((1 + 2 * PARTS + 2 * len(BATCHES) + Y,))],
        compiler_params=pltpu.CompilerParams(vmem_limit_bytes=32 << 20),
        cost_estimate=pl.CostEstimate(
            flops=1 << 30, transcendentals=0, bytes_accessed=12 << 20
        ),
    )(z, hidden, *down[0], *down[1], *first, *second)


def after(value, *others):
    return lax.optimization_barrier((value, *others))[0]


def shards(hidden, store_a, store_b, request_start, request_adapter):
    mine = block_adapters(request_start[0], request_adapter[0], Y * Z * ROWS)
    segments = X * CORES
    ahead = [(s, (s + 1) % segments) for s in range(segments)]
    back = [(s, (s - 1) % segments) for s in range(segments)]
    behind = lax.ppermute(mine, SEGMENT, ahead)
    z = lax.axis_index("z")

    def at_z(chosen):
        rows = chosen.reshape(Y, Z, 2)
        here = lax.broadcasted_iota(jnp.int32, rows.shape, 1) == z
        return jnp.sum(jnp.where(here, rows, 0), axis=1)

    wanted = jnp.stack([at_z(mine), at_z(behind)], axis=1)

    def over_y(x):
        return lax.all_to_all(x, "y", split_axis=0, concat_axis=0, tiled=True)

    parts = [
        lax.all_gather(store_a[0][:, p * PART : (p + 1) * PART], "z") for p in range(PARTS)
    ]
    down = ([], [])

    def send_down(after):
        ours, theirs = pick_gathered(wanted, parts[len(down[0])], after)
        down[0].append(over_y(ours))
        down[1].append(over_y(lax.ppermute(theirs, SEGMENT, back)))
        return ours

    up = [(i, (i + 1) % Z) for i in range(Z)]
    low = [(i, (i - 1) % Z) for i in range(Z)]
    chunks = {0: store_b[0]}
    first, second = [], []
    for step in range(1, 9):
        if step == 6:
            chunks[5] = after(chunks[5], send_down([chunks[4]]))
        if step == 8:
            chunks[7] = after(chunks[7], down[1][0])
        chunks[step] = lax.ppermute(chunks[step - 1], "z", up)
        if step < 8:
            chunks[Z - step] = lax.ppermute(chunks[(Z + 1 - step) % Z], "z", low)
        b = len(first)
        if all(d in chunks for d in BATCHES[b]):
            picked = pick(wanted, [chunks[d] for d in BATCHES[b]], second[b - 2 : b - 1] if b > 1 else [])
            received = over_y(picked)
            first.append(received)
            second.append(lax.ppermute(received[:, 1], SEGMENT, back))
    send_down([chunks[8]])
    return layers(z.astype(jnp.int32)[None], hidden[0], down, first, second)[None]


def solution(mesh):
    grid = Mesh(mesh.devices.reshape(X, CORES, Y, Z), ("x", "core", "y", "z"))
    return jax.shard_map(
        shards,
        mesh=grid,
        in_specs=(
            P(SEGMENT, ("y", "z"), None),
            P(SEGMENT, None, None, ("y", "z")),
            P(SEGMENT, None, None, ("y", "z")),
            P(SEGMENT, None),
            P(SEGMENT, None),
        ),
        out_specs=P(SEGMENT, ("y", "z"), None),
        check_vma=False,
    )
```

time: 315 us -> 528 us (1.68)
  Pallas kernels: 15.3 us -> 275 us
  starting transfers between devices: 130 us -> 92 us
  blocking collectives: 0 us -> 31.1 us
  waiting for transfers between devices: 132 us -> 101 us
  local copies, waits for them, and re-layouts: 30.9 us -> 11.4 us
  between operations: 0.56 us -> 13.9 us
    pallas_call x5, Pallas kernels: 5.28 us -> 136 us  [pick(): pl.pallas_call(functools.partial(pick_kernel, count), out_shape=jax.Shape...]
    pallas_call x0 -> x2, Pallas kernels: none -> 131 us  [pick_gathered(): pl.pallas_call(pick_gathered_kernel, out_shape=[jax.ShapeDtypeStruct((Y,...]
    ppermute x36 -> x23, starting transfers between devices: 107 us -> 59.3 us  [the longest x7 41.2 us: shards(): chunks[Z - step] = lax.ppermute(chunks[(Z + 1 - step) % Z], 'z', low)]
    all_to_all x0 -> x2, blocking collectives: none -> 31.1 us  [over_y(): return lax.all_to_all(x, 'y', split_axis=0, concat_axis=0, tiled=True)]
    ppermute x36 -> x23, waiting for transfers between devices: 110 us -> 85.8 us  [the longest x8 58.2 us: shards(): chunks[step] = lax.ppermute(chunks[step - 1], 'z', up)]
    unnamed x60 -> x34, local copies, waits for them, and re-layouts: 22.7 us -> 8.27 us
    all_to_all x5 -> x7, starting transfers between devices: 23.1 us -> 32.6 us  [over_y(): return lax.all_to_all(x, 'y', split_axis=0, concat_axis=0, tiled=True)]
    all_to_all x5 -> x7, waiting for transfers between devices: 22.2 us -> 14.5 us  [over_y(): return lax.all_to_all(x, 'y', split_axis=0, concat_axis=0, tiled=True)]
  transfers between devices with their start and end apart: 41 -> 32, of which waited for: 21 -> 14; matrix products, arithmetic and copies ran while one was open for 3% -> 1% of each run, Pallas kernels for 1% -> 51%
where the time goes in v2:
time: 528 us; the launch traced here: 526 us
  Pallas kernels  275 us (52%)
  waiting for transfers between devices  101 us (19%)
  starting transfers between devices  92 us (17%)
  blocking collectives  31.1 us (6%)
  between operations  13.9 us (3%)
  local copies, waits for them, and re-layouts  11.4 us (2%)
    pallas_call x5, Pallas kernels, pick(): pl.pallas_call(functools.partial(pick_kernel, count), out_shape=jax.Shape...  136 us
    pallas_call x2, Pallas kernels, pick_gathered(): pl.pallas_call(pick_gathered_kernel, out_shape=[jax.ShapeDtypeStruct((Y,...  131 us
    ppermute x8, waiting for transfers between devices, shards(): chunks[step] = lax.ppermute(chunks[step - 1], 'z', up)  58.2 us
    ppermute x7, starting transfers between devices, shards(): chunks[Z - step] = lax.ppermute(chunks[(Z + 1 - step) % Z], 'z', low)  41.2 us
    all_to_all x7, starting transfers between devices, over_y(): return lax.all_to_all(x, 'y', split_axis=0, concat_axis=0, tiled=True)  32.6 us
    all_to_all x2, blocking collectives, over_y(): return lax.all_to_all(x, 'y', split_axis=0, concat_axis=0, tiled=True)  31.1 us
    ppermute x8, starting transfers between devices, shards(): chunks[step] = lax.ppermute(chunks[step - 1], 'z', up)  17.2 us
    ppermute x7, waiting for transfers between devices, shards(): chunks[Z - step] = lax.ppermute(chunks[(Z + 1 - step) % Z], 'z', low)  15.8 us
  transfers between devices with their start and end apart: 32, of which 14 were waited for; matrix products, arithmetic and copies ran while one was open for 1% of the time, Pallas kernels for 51%

profile of v2, /device:TPU:6, one launch (start us, length us, event | category | flops | bytes accessed | tf_op | source)
XLA Modules:
  0.0 526.4 jit_solution(9806401272390216674)
XLA Ops:
  6.5 1.9 fusion
  9.2 3.8 collective-permute-start.1
  13.0 9.5 %collective-permute-start.11 = (bf16[32,64,128]{2,1,0:T(8,128)(2,1)}, bf16[32,64,128]{2,1,0:T(8,128)(2,1)S(1)}, u32[]{:S(2)}, u32[]{:S(2)}) collective-permute-start(bf16[32,64,128]{2,1,0:T(8,128)(2,1)} %bitcast.40), channel_id=1, source_target_pairs={{0,15},{1,0},{2,1},{3,2},{4,3},{5,4},{6,5},{7,6},{8,7},{9,8},{10,9... | collective-permute-start | bytes 1572872 | tf_op jit(solution)/shard_map/ppermute | solution.py:250
  22.5 10.2 %collective-permute-done.1.refs_2_ = bf16[32,64,128]{2,1,0:T(8,128)(2,1)S(1)} collective-permute-done((bf16[32,64,128]{2,1,0:T(8,128)(2,1)}, bf16[32,64,128]{2,1,0:T(8,128)(2,1)S(1)}, u32[]{:S(2)}, u32[]{:S(2)}) %collective-permute-start.1) | collective-permute-done | bytes 524320 | tf_op jit(solution)/shard_map/ppermute | solution.py:248
  32.7 1.9 collective-permute-start.2
  34.6 3.1 collective-permute-done.11.refs_3_
  37.8 5.5 %collective-permute-start.12 = (bf16[32,64,128]{2,1,0:T(8,128)(2,1)S(1)}, bf16[32,64,128]{2,1,0:T(8,128)(2,1)S(1)}, u32[]{:S(2)}, u32[]{:S(2)}) collective-permute-start(bf16[32,64,128]{2,1,0:T(8,128)(2,1)S(1)} %collective-permute-done.11.refs_3_), channel_id=1, source_target_pairs={{0,15},{1,0},{2,1},{3,2},{4,3},{5,4},{6,5},{7,6},{8,7},{9,8},{10,9... | collective-permute-start | bytes 1572872 | tf_op jit(solution)/shard_map/ppermute | solution.py:250
  44.8 16.0 %collective-permute-done.2.refs_1_ = bf16[32,64,128]{2,1,0:T(8,128)(2,1)S(1)} collective-permute-done((bf16[32,64,128]{2,1,0:T(8,128)(2,1)S(1)}, bf16[32,64,128]{2,1,0:T(8,128)(2,1)S(1)}, u32[]{:S(2)}, u32[]{:S(2)}) %collective-permute-start.2) | collective-permute-done | bytes 524320 | tf_op jit(solution)/shard_map/ppermute | solution.py:248
  60.8 1.9 collective-permute-start.3
  62.7 1.9 collective-permute-done.12.refs_2_
  64.6 5.6 %collective-permute-start.13 = (bf16[32,64,128]{2,1,0:T(8,128)(2,1)S(1)}, bf16[32,64,128]{2,1,0:T(8,128)(2,1)}, u32[]{:S(2)}, u32[]{:S(2)}) collective-permute-start(bf16[32,64,128]{2,1,0:T(8,128)(2,1)S(1)} %collective-permute-done.12.refs_2_), channel_id=1, source_target_pairs={{0,15},{1,0},{2,1},{3,2},{4,3},{5,4},{6,5},{7,6},{8,7},{9,8},{10,9... | collective-permute-start | bytes 1572872 | tf_op jit(solution)/shard_map/ppermute | solution.py:250
  71.2 25.7 %shard_map.57 = bf16[4,2,3,2,64,128]{5,4,3,2,1,0:T(8,128)(2,1)} custom-call(s32[4,2,2]{2,1,0:T(2,128)} %pad_add_fusion.wanted.refs_0_, bf16[32,64,128]{2,1,0:T(8,128)(2,1)} %bitcast.41, bf16[32,64,128]{2,1,0:T(8,128)(2,1)} %copy-done.14, bf16[32,64,128]{2,1,0:T(8,128)(2,1)} %copy-done.15), custom_call_target="tpu_custom_call" | custom-call | bytes 1572864 | tf_op jit(solution)/shard_map/pallas_call | solution.py:49
  96.8 5.5 %all-to-all-start.4 = ((bf16[4,2,3,2,64,128]{5,4,3,2,1,0:T(8,128)(2,1)}), bf16[4,2,3,2,64,128]{5,4,3,2,1,0:T(8,128)(2,1)S(1)}, u32[]{:S(2)}, u32[]{:S(2)}) async-start(bf16[4,2,3,2,64,128]{5,4,3,2,1,0:T(8,128)(2,1)} %shard_map.57), calls=%async_computation.4 | async-start | bytes 1572864 | tf_op jit(solution)/shard_map/all_to_all | solution.py:226
  102.4 1.9 collective-permute-start.4
  104.3 5.1 collective-permute-start.14
  109.5 33.6 %shard_map.58 = bf16[4,2,4,2,64,128]{5,4,3,2,1,0:T(8,128)(2,1)} custom-call(s32[4,2,2]{2,1,0:T(2,128)} %pad_add_fusion.wanted.refs_0_, bf16[32,64,128]{2,1,0:T(8,128)(2,1)} %copy-done.12, bf16[32,64,128]{2,1,0:T(8,128)(2,1)} %copy-done.13, bf16[32,64,128]{2,1,0:T(8,128)(2,1)} %copy-done.16, bf16[32,64,128]{2,1,0:T(8,128)(2,1)} %collective-permute-done.13.refs_4_), custom_call_target="tpu_custom_call" | custom-call | bytes 2097152 | tf_op jit(solution)/shard_map/pallas_call | solution.py:49
  143.1 4.8 all-to-all-start.5
  147.9 1.9 collective-permute-start.5
  149.8 5.1 collective-permute-start.15
  155.0 5.3 %collective-permute-done.16.refs_5_.refs_10_ = bf16[4,3,2,64,128]{4,3,2,1,0:T(8,128)(2,1)S(1)} collective-permute-done((bf16[4,3,2,64,128]{4,3,2,1,0:T(8,128)(2,1)S(1)}, bf16[4,3,2,64,128]{4,3,2,1,0:T(8,128)(2,1)S(1)}, u32[]{:S(2)}, u32[]{:S(2)}) %collective-permute-start.16) | collective-permute-done | bytes 393248 | tf_op jit(solution)/shard_map/ppermute | solution.py:256
  160.3 13.1 %collective-permute-done.5.refs_3_ = bf16[32,64,128]{2,1,0:T(8,128)(2,1)S(1)} collective-permute-done((bf16[32,64,128]{2,1,0:T(8,128)(2,1)S(1)}, bf16[32,64,128]{2,1,0:T(8,128)(2,1)S(1)}, u32[]{:S(2)}, u32[]{:S(2)}) %collective-permute-start.5) | collective-permute-done | bytes 524320 | tf_op jit(solution)/shard_map/ppermute | solution.py:248
  174.3 33.6 %shard_map.59 = bf16[4,2,4,2,64,128]{5,4,3,2,1,0:T(8,128)(2,1)} custom-call(s32[4,2,2]{2,1,0:T(2,128)} %pad_add_fusion.wanted.refs_0_, bf16[32,64,128]{2,1,0:T(8,128)(2,1)} %copy-done.10, bf16[32,64,128]{2,1,0:T(8,128)(2,1)} %collective-permute-done.14.refs_2_, bf16[32,64,128]{2,1,0:T(8,128)(2,1)} %copy-done.11, ...), custom_call_target="tpu_custom_call" | custom-call | bytes 2097152 | tf_op jit(solution)/shard_map/pallas_call | solution.py:49
  207.9 4.2 all-to-all-start.6
  212.1 65.4 %shard_map.55 = (bf16[4,16,2,32,128]{4,3,2,1,0:T(8,128)(2,1)}, bf16[4,16,2,32,128]{4,3,2,1,0:T(8,128)(2,1)}) custom-call(s32[4,2,2]{2,1,0:T(2,128)} %pad_add_fusion.wanted.refs_0_, bf16[16,32,32,128]{3,2,1,0:T(8,128)(2,1)} %bitcast.37, bf16[32,64,128]{2,1,0:T(8,128)(2,1)} %copy-done.10), custom_call_target="tpu_custom_call" | custom-call | bytes 4194304 | tf_op jit(solution)/shard_map/pallas_call | solution.py:75
  277.5 4.8 all-to-all-start
  282.3 5.2 collective-permute-start.17
  287.5 1.9 collective-permute-start.6
  289.5 8.6 %all-to-all-done.refs_1_ = bf16[4,16,2,32,128]{4,3,2,1,0:T(8,128)(2,1)S(1)} async-done(((bf16[4,16,2,32,128]{4,3,2,1,0:T(8,128)(2,1)}), bf16[4,16,2,32,128]{4,3,2,1,0:T(8,128)(2,1)S(1)}, u32[]{:S(2)}, u32[]{:S(2)}) %all-to-all-start) | async-done | bytes 1048608 | tf_op jit(solution)/shard_map/all_to_all | solution.py:226
  298.1 4.3 all-to-all-start.1
  302.4 5.2 collective-permute-start.18
  307.6 1.9 collective-permute-start.7
  309.6 10.2 %collective-permute-done.18.refs_4_ = bf16[32,64,128]{2,1,0:T(8,128)(2,1)} collective-permute-done((bf16[32,64,128]{2,1,0:T(8,128)(2,1)}, bf16[32,64,128]{2,1,0:T(8,128)(2,1)}, u32[]{:S(2)}, u32[]{:S(2)}) %collective-permute-start.18) | collective-permute-done | bytes 524320 | tf_op jit(solution)/shard_map/ppermute | solution.py:250
  319.8 5.3 %collective-permute-done.7.refs_3_ = bf16[32,64,128]{2,1,0:T(8,128)(2,1)} collective-permute-done((bf16[32,64,128]{2,1,0:T(8,128)(2,1)}, bf16[32,64,128]{2,1,0:T(8,128)(2,1)}, u32[]{:S(2)}, u32[]{:S(2)}) %collective-permute-start.7) | collective-permute-done | bytes 524320 | tf_op jit(solution)/shard_map/ppermute | solution.py:248
  325.1 33.6 %shard_map.60 = bf16[4,2,4,2,64,128]{5,4,3,2,1,0:T(8,128)(2,1)} custom-call(s32[4,2,2]{2,1,0:T(2,128)} %pad_add_fusion.wanted.refs_0_, bf16[32,64,128]{2,1,0:T(8,128)(2,1)} %collective-permute-done.6.refs_1_, bf16[32,64,128]{2,1,0:T(8,128)(2,1)} %collective-permute-done.17.refs_2_, bf16[32,64,128]{2,1,0:T(8,128)(2,1)} %collective-permute-done.7.refs_3_, ...), custom_call_target="tpu_custom_call" | custom-call | bytes 2097152 | tf_op jit(solution)/shard_map/pallas_call | solution.py:49
  358.7 4.8 all-to-all-start.7
  363.5 1.9 collective-permute-start.9
  366.2 13.6 %collective-permute-done.9.refs_0_.refs_1_ = bf16[32,64,128]{2,1,0:T(8,128)(2,1)} collective-permute-done((bf16[32,64,128]{2,1,0:T(8,128)(2,1)}, bf16[32,64,128]{2,1,0:T(8,128)(2,1)}, u32[]{:S(2)}, u32[]{:S(2)}) %collective-permute-start.9) | collective-permute-done | bytes 524320 | tf_op jit(solution)/shard_map/ppermute | solution.py:248
  379.8 65.4 %shard_map.56 = (bf16[4,16,2,32,128]{4,3,2,1,0:T(8,128)(2,1)}, bf16[4,16,2,32,128]{4,3,2,1,0:T(8,128)(2,1)}) custom-call(s32[4,2,2]{2,1,0:T(2,128)} %pad_add_fusion.wanted.refs_0_, bf16[16,32,32,128]{3,2,1,0:T(8,128)(2,1)} %bitcast.36, bf16[32,64,128]{2,1,0:T(8,128)(2,1)} %collective-permute-done.9.refs_0_.refs_1_), custom_call_target="tpu_custom_call" | custom-call | bytes 4194304 | tf_op jit(solution)/shard_map/pallas_call | solution.py:75
  445.2 9.8 %shard_map.61 = bf16[4,2,1,2,64,128]{5,4,3,2,1,0:T(8,128)(2,1)} custom-call(s32[4,2,2]{2,1,0:T(2,128)} %pad_add_fusion.wanted.refs_0_, bf16[32,64,128]{2,1,0:T(8,128)(2,1)} %collective-permute-done.9.refs_0_.refs_1_, bf16[4,4,2,64,128]{4,3,2,1,0:T(8,128)(2,1)} %collective-permute-done.20.refs_2_.refs_12_), custom_call_target="tpu_custom_call" | custom-call | bytes 524288 | tf_op jit(solution)/shard_map/pallas_call | solution.py:49
  455.0 11.8 %all_to_all.45.refs_9_ = bf16[4,2,1,2,64,128]{5,4,3,2,1,0:T(8,128)(2,1)S(1)} all-to-all(bf16[4,2,1,2,64,128]{5,4,3,2,1,0:T(8,128)(2,1)} %shard_map.61), channel_id=1, replica_groups=mesh['x'=4,'core'=2,'y'=4,'z'=16] {'y'}, dimensions={0} | all-to-all | bytes 524288 | tf_op jit(solution)/shard_map/all_to_all | solution.py:226
  466.9 19.2 %all_to_all.46.refs_2_ = bf16[4,16,2,32,128]{4,3,2,1,0:T(8,128)(2,1)} all-to-all(bf16[4,16,2,32,128]{4,3,2,1,0:T(8,128)(2,1)} %get-tuple-element.15), channel_id=1, replica_groups=mesh['x'=4,'core'=2,'y'=4,'z'=16] {'y'}, dimensions={0} | all-to-all | bytes 2097152 | tf_op jit(solution)/shard_map/all_to_all | solution.py:226
  486.1 4.2 all-to-all-start.3
  491.2 5.9 %collective-permute-done.21.refs_13_ = bf16[4,4,2,64,128]{4,3,2,1,0:T(8,128)(2,1)S(1)} collective-permute-done((bf16[4,4,2,64,128]{4,3,2,1,0:T(8,128)(2,1)S(1)}, bf16[4,4,2,64,128]{4,3,2,1,0:T(8,128)(2,1)S(1)}, u32[]{:S(2)}, u32[]{:S(2)}) %collective-permute-start.21) | collective-permute-done | bytes 524320 | tf_op jit(solution)/shard_map/ppermute | solution.py:256
  498.5 5.9 %all-to-all-done.3.refs_4_ = bf16[4,16,2,32,128]{4,3,2,1,0:T(8,128)(2,1)} async-done(((bf16[4,16,2,32,128]{4,3,2,1,0:T(8,128)(2,1)}), bf16[4,16,2,32,128]{4,3,2,1,0:T(8,128)(2,1)}, u32[]{:S(2)}, u32[]{:S(2)}) %all-to-all-start.3) | async-done | bytes 1048608 | tf_op jit(solution)/shard_map/all_to_all | solution.py:226
  505.6 1.2 copy-done.3
  506.8 1.2 copy-done.4
  508.0 1.6 copy-done.5
  511.6 7.9 %shard_map.62 = bf16[128,8192]{1,0:T(8,128)(2,1)} custom-call(s32[1]{0:T(128)} %bitcast.z_ref, bf16[128,8192]{1,0:T(8,128)(2,1)S(1)} %bitcast.35, bf16[4,16,2,32,128]{4,3,2,1,0:T(8,128)(2,1)S(1)} %copy-done.3, bf16[4,16,2,32,128]{4,3,2,1,0:T(8,128)(2,1)S(1)} %copy-done.4, bf16[4,16,2,32,128]{4,3,2,1,0:T(8,128)(2,1)} %all-to-all-done.1.refs_3_, ...), custom_call_target="tpu_custom_call" | custom-call | flops 1073741824 | bytes 12582912 | tf_op jit(solution)/shard_map/pallas_call | solution.py:190
  (77 shorter events, 10.4 us)
Async XLA Ops:
  6.5 205.6 %all-gather.5.cloned.1.call-start = ((), (), s32[]{:S(2)}) async-start(), calls=%async_computation.9 | async-start | bytes 4456448 | tf_op jit(solution)/shard_map/all_gather | solution.py:229
  8.4 357.8 %all-gather.7.cloned.1.call-start = ((), (), s32[]{:S(2)}) async-start(), calls=%async_computation.10 | async-start | bytes 4456448 | tf_op jit(solution)/shard_map/all_gather | solution.py:229
  9.2 23.5 %collective-permute-start.1 = (bf16[32,64,128]{2,1,0:T(8,128)(2,1)}, bf16[32,64,128]{2,1,0:T(8,128)(2,1)S(1)}, u32[]{:S(2)}, u32[]{:S(2)}) collective-permute-start(bf16[32,64,128]{2,1,0:T(8,128)(2,1)} %bitcast.39), channel_id=1, source_target_pairs={{0,1},{1,2},{2,3},{3,4},{4,5},{5,6},{6,7},{7,8},{8,9},{9,10},{10,1... | collective-permute-start | bytes 1572872 | tf_op jit(solution)/shard_map/ppermute | solution.py:248
  13.0 24.7 %collective-permute-start.11 = (bf16[32,64,128]{2,1,0:T(8,128)(2,1)}, bf16[32,64,128]{2,1,0:T(8,128)(2,1)S(1)}, u32[]{:S(2)}, u32[]{:S(2)}) collective-permute-start(bf16[32,64,128]{2,1,0:T(8,128)(2,1)} %bitcast.40), channel_id=1, source_target_pairs={{0,15},{1,0},{2,1},{3,2},{4,3},{5,4},{6,5},{7,6},{8,7},{9,8},{10,9... | collective-permute-start | bytes 1572872 | tf_op jit(solution)/shard_map/ppermute | solution.py:250
  32.7 38.4 %copy-start.14 = (bf16[32,64,128]{2,1,0:T(8,128)(2,1)}, bf16[32,64,128]{2,1,0:T(8,128)(2,1)S(1)}, u32[]{:S(2)}) copy-start(bf16[32,64,128]{2,1,0:T(8,128)(2,1)S(1)} %collective-permute-done.1.refs_2_) | copy-start | bytes 1572868
  32.7 28.0 %collective-permute-start.2 = (bf16[32,64,128]{2,1,0:T(8,128)(2,1)S(1)}, bf16[32,64,128]{2,1,0:T(8,128)(2,1)S(1)}, u32[]{:S(2)}, u32[]{:S(2)}) collective-permute-start(bf16[32,64,128]{2,1,0:T(8,128)(2,1)S(1)} %collective-permute-done.1.refs_2_), channel_id=1, source_target_pairs={{0,1},{1,2},{2,3},{3,4},{4,5},{5,6},{6,7},{7,8},{8,9},{9,10},{10,1... | collective-permute-start | bytes 1572872 | tf_op jit(solution)/shard_map/ppermute | solution.py:248
  37.8 33.4 %copy-start.15 = (bf16[32,64,128]{2,1,0:T(8,128)(2,1)}, bf16[32,64,128]{2,1,0:T(8,128)(2,1)S(1)}, u32[]{:S(2)}) copy-start(bf16[32,64,128]{2,1,0:T(8,128)(2,1)S(1)} %collective-permute-done.11.refs_3_) | copy-start | bytes 1572868
  37.8 26.8 %collective-permute-start.12 = (bf16[32,64,128]{2,1,0:T(8,128)(2,1)S(1)}, bf16[32,64,128]{2,1,0:T(8,128)(2,1)S(1)}, u32[]{:S(2)}, u32[]{:S(2)}) collective-permute-start(bf16[32,64,128]{2,1,0:T(8,128)(2,1)S(1)} %collective-permute-done.11.refs_3_), channel_id=1, source_target_pairs={{0,15},{1,0},{2,1},{3,2},{4,3},{5,4},{6,5},{7,6},{8,7},{9,8},{10,9... | collective-permute-start | bytes 1572872 | tf_op jit(solution)/shard_map/ppermute | solution.py:250
  44.8 25.5 %collective-permute-start = (s32[128]{0:T(128)S(1)}, s32[128]{0:T(128)S(1)}, u32[]{:S(2)}, u32[]{:S(2)}) collective-permute-start(s32[128]{0:T(128)S(1)} %select_reduce_fusion.2), channel_id=1, source_target_pairs={{0,64},{64,128},{128,192},{192,256},{256,320},{320,384},{384,448},... | collective-permute-start | bytes 1544 | tf_op jit(solution)/shard_map/ppermute | solution.py:215
  60.8 48.7 %copy-start.12 = (bf16[32,64,128]{2,1,0:T(8,128)(2,1)}, bf16[32,64,128]{2,1,0:T(8,128)(2,1)S(1)}, u32[]{:S(2)}) copy-start(bf16[32,64,128]{2,1,0:T(8,128)(2,1)S(1)} %collective-permute-done.2.refs_1_) | copy-start | bytes 1572868
  60.8 41.6 %collective-permute-start.3 = (bf16[32,64,128]{2,1,0:T(8,128)(2,1)S(1)}, bf16[32,64,128]{2,1,0:T(8,128)(2,1)S(1)}, u32[]{:S(2)}, u32[]{:S(2)}) collective-permute-start(bf16[32,64,128]{2,1,0:T(8,128)(2,1)S(1)} %collective-permute-done.2.refs_1_), channel_id=1, source_target_pairs={{0,1},{1,2},{2,3},{3,4},{4,5},{5,6},{6,7},{7,8},{8,9},{9,10},{10,1... | collective-permute-start | bytes 1572872 | tf_op jit(solution)/shard_map/ppermute | solution.py:248
  64.6 44.9 %copy-start.13 = (bf16[32,64,128]{2,1,0:T(8,128)(2,1)}, bf16[32,64,128]{2,1,0:T(8,128)(2,1)S(1)}, u32[]{:S(2)}) copy-start(bf16[32,64,128]{2,1,0:T(8,128)(2,1)S(1)} %collective-permute-done.12.refs_2_) | copy-start | bytes 1572868
  64.6 39.7 %collective-permute-start.13 = (bf16[32,64,128]{2,1,0:T(8,128)(2,1)S(1)}, bf16[32,64,128]{2,1,0:T(8,128)(2,1)}, u32[]{:S(2)}, u32[]{:S(2)}) collective-permute-start(bf16[32,64,128]{2,1,0:T(8,128)(2,1)S(1)} %collective-permute-done.12.refs_2_), channel_id=1, source_target_pairs={{0,15},{1,0},{2,1},{3,2},{4,3},{5,4},{6,5},{7,6},{8,7},{9,8},{10,9... | collective-permute-start | bytes 1572872 | tf_op jit(solution)/shard_map/ppermute | solution.py:250
  96.8 46.2 %all-to-all-start.4 = ((bf16[4,2,3,2,64,128]{5,4,3,2,1,0:T(8,128)(2,1)}), bf16[4,2,3,2,64,128]{5,4,3,2,1,0:T(8,128)(2,1)S(1)}, u32[]{:S(2)}, u32[]{:S(2)}) async-start(bf16[4,2,3,2,64,128]{5,4,3,2,1,0:T(8,128)(2,1)} %shard_map.57), calls=%async_computation.4 | async-start | bytes 1572864 | tf_op jit(solution)/shard_map/all_to_all | solution.py:226
  102.4 7.1 %copy-start.16 = (bf16[32,64,128]{2,1,0:T(8,128)(2,1)}, bf16[32,64,128]{2,1,0:T(8,128)(2,1)S(1)}, u32[]{:S(2)}) copy-start(bf16[32,64,128]{2,1,0:T(8,128)(2,1)S(1)} %collective-permute-done.3.refs_3_) | copy-start | bytes 1572868
  102.4 45.5 %collective-permute-start.4 = (bf16[32,64,128]{2,1,0:T(8,128)(2,1)S(1)}, bf16[32,64,128]{2,1,0:T(8,128)(2,1)S(1)}, u32[]{:S(2)}, u32[]{:S(2)}) collective-permute-start(bf16[32,64,128]{2,1,0:T(8,128)(2,1)S(1)} %collective-permute-done.3.refs_3_), channel_id=1, source_target_pairs={{0,1},{1,2},{2,3},{3,4},{4,5},{5,6},{6,7},{7,8},{8,9},{9,10},{10,1... | collective-permute-start | bytes 1572872 | tf_op jit(solution)/shard_map/ppermute | solution.py:248
  104.3 45.5 %collective-permute-start.14 = (bf16[32,64,128]{2,1,0:T(8,128)(2,1)}, bf16[32,64,128]{2,1,0:T(8,128)(2,1)}, u32[]{:S(2)}, u32[]{:S(2)}) collective-permute-start(bf16[32,64,128]{2,1,0:T(8,128)(2,1)} %collective-permute-done.13.refs_4_), channel_id=1, source_target_pairs={{0,15},{1,0},{2,1},{3,2},{4,3},{5,4},{6,5},{7,6},{8,7},{9,8},{10,9... | collective-permute-start | bytes 1572872 | tf_op jit(solution)/shard_map/ppermute | solution.py:250
  143.1 64.8 %copy-start = (bf16[4,2,3,2,64,128]{5,4,3,2,1,0:T(8,128)(2,1)}, bf16[4,2,3,2,64,128]{5,4,3,2,1,0:T(8,128)(2,1)S(1)}, u32[]{:S(2)}) copy-start(bf16[4,2,3,2,64,128]{5,4,3,2,1,0:T(8,128)(2,1)S(1)} %all-to-all-done.4.refs_5_) | copy-start | bytes 2359300
  143.1 64.8 %all-to-all-start.5 = ((bf16[4,2,4,2,64,128]{5,4,3,2,1,0:T(8,128)(2,1)}), bf16[4,2,4,2,64,128]{5,4,3,2,1,0:T(8,128)(2,1)S(1)}, u32[]{:S(2)}, u32[]{:S(2)}) async-start(bf16[4,2,4,2,64,128]{5,4,3,2,1,0:T(8,128)(2,1)} %shard_map.58), calls=%async_computation.5 | async-start | bytes 2097152 | tf_op jit(solution)/shard_map/all_to_all | solution.py:226
  147.9 26.1 %copy-start.10 = (bf16[32,64,128]{2,1,0:T(8,128)(2,1)}, bf16[32,64,128]{2,1,0:T(8,128)(2,1)S(1)}, u32[]{:S(2)}) copy-start(bf16[32,64,128]{2,1,0:T(8,128)(2,1)S(1)} %collective-permute-done.4.refs_0_.refs_1_) | copy-start | bytes 1572868
  147.9 25.6 %collective-permute-start.5 = (bf16[32,64,128]{2,1,0:T(8,128)(2,1)S(1)}, bf16[32,64,128]{2,1,0:T(8,128)(2,1)S(1)}, u32[]{:S(2)}, u32[]{:S(2)}) collective-permute-start(bf16[32,64,128]{2,1,0:T(8,128)(2,1)S(1)} %collective-permute-done.4.refs_0_.refs_1_), channel_id=1, source_target_pairs={{0,1},{1,2},{2,3},{3,4},{4,5},{5,6},{6,7},{7,8},{8,9},{9,10},{10,1... | collective-permute-start | bytes 1572872 | tf_op jit(solution)/shard_map/ppermute | solution.py:248
  149.8 24.2 %collective-permute-start.15 = (bf16[32,64,128]{2,1,0:T(8,128)(2,1)}, bf16[32,64,128]{2,1,0:T(8,128)(2,1)}, u32[]{:S(2)}, u32[]{:S(2)}) collective-permute-start(bf16[32,64,128]{2,1,0:T(8,128)(2,1)} %collective-permute-done.14.refs_2_), channel_id=1, source_target_pairs={{0,15},{1,0},{2,1},{3,2},{4,3},{5,4},{6,5},{7,6},{8,7},{9,8},{10,9... | collective-permute-start | bytes 1572872 | tf_op jit(solution)/shard_map/ppermute | solution.py:250
  155.0 5.3 %collective-permute-start.16 = (bf16[4,3,2,64,128]{4,3,2,1,0:T(8,128)(2,1)S(1)}, bf16[4,3,2,64,128]{4,3,2,1,0:T(8,128)(2,1)S(1)}, u32[]{:S(2)}, u32[]{:S(2)}) collective-permute-start(bf16[4,3,2,64,128]{4,3,2,1,0:T(8,128)(2,1)S(1)} %slice_bitcast_fusion.3), channel_id=1, source_target_pairs={{0,448},{64,0},{128,64},{192,128},{256,192},{320,256},{384,320},{4... | collective-permute-start | bytes 1179656 | tf_op jit(solution)/shard_map/ppermute | solution.py:256
  160.3 13.7 %copy-start.6 = (bf16[4,3,2,64,128]{4,3,2,1,0:T(8,128)(2,1)}, bf16[4,3,2,64,128]{4,3,2,1,0:T(8,128)(2,1)S(1)}, u32[]{:S(2)}) copy-start(bf16[4,3,2,64,128]{4,3,2,1,0:T(8,128)(2,1)S(1)} %collective-permute-done.16.refs_5_.refs_10_) | copy-start | bytes 1179652
  207.9 69.6 %all-to-all-start.6 = ((bf16[4,2,4,2,64,128]{5,4,3,2,1,0:T(8,128)(2,1)}), bf16[4,2,4,2,64,128]{5,4,3,2,1,0:T(8,128)(2,1)S(1)}, u32[]{:S(2)}, u32[]{:S(2)}) async-start(bf16[4,2,4,2,64,128]{5,4,3,2,1,0:T(8,128)(2,1)} %shard_map.59), calls=%async_computation.6 | async-start | bytes 2097152 | tf_op jit(solution)/shard_map/all_to_all | solution.py:226
  277.5 20.6 %collective-permute-start.8 = (bf16[4,16,2,32,128]{4,3,2,1,0:T(8,128)(2,1)}, bf16[4,16,2,32,128]{4,3,2,1,0:T(8,128)(2,1)}, u32[]{:S(2)}, u32[]{:S(2)}) collective-permute-start(bf16[4,16,2,32,128]{4,3,2,1,0:T(8,128)(2,1)} %get-tuple-element.13), channel_id=1, source_target_pairs={{0,448},{64,0},{128,64},{192,128},{256,192},{320,256},{384,320},{4... | collective-permute-start | bytes 3145736 | tf_op jit(solution)/shard_map/ppermute | solution.py:236
  277.5 20.5 %all-to-all-start = ((bf16[4,16,2,32,128]{4,3,2,1,0:T(8,128)(2,1)}), bf16[4,16,2,32,128]{4,3,2,1,0:T(8,128)(2,1)S(1)}, u32[]{:S(2)}, u32[]{:S(2)}) async-start(bf16[4,16,2,32,128]{4,3,2,1,0:T(8,128)(2,1)} %get-tuple-element.11), calls=%async_computation | async-start | bytes 2097152 | tf_op jit(solution)/shard_map/all_to_all | solution.py:226
  282.3 20.1 %collective-permute-start.17 = (bf16[32,64,128]{2,1,0:T(8,128)(2,1)}, bf16[32,64,128]{2,1,0:T(8,128)(2,1)}, u32[]{:S(2)}, u32[]{:S(2)}) collective-permute-start(bf16[32,64,128]{2,1,0:T(8,128)(2,1)} %collective-permute-done.15.refs_4_), channel_id=1, source_target_pairs={{0,15},{1,0},{2,1},{3,2},{4,3},{5,4},{6,5},{7,6},{8,7},{9,8},{10,9... | collective-permute-start | bytes 1572872 | tf_op jit(solution)/shard_map/ppermute | solution.py:250
  287.5 20.1 %collective-permute-start.6 = (bf16[32,64,128]{2,1,0:T(8,128)(2,1)}, bf16[32,64,128]{2,1,0:T(8,128)(2,1)}, u32[]{:S(2)}, u32[]{:S(2)}) collective-permute-start(bf16[32,64,128]{2,1,0:T(8,128)(2,1)} %copy-done.11), channel_id=1, source_target_pairs={{0,1},{1,2},{2,3},{3,4},{4,5},{5,6},{6,7},{7,8},{8,9},{9,10},{10,1... | collective-permute-start | bytes 1572872 | tf_op jit(solution)/shard_map/ppermute | solution.py:248
  298.1 60.6 %copy-start.2 = (bf16[4,16,2,32,128]{4,3,2,1,0:T(8,128)(2,1)}, bf16[4,16,2,32,128]{4,3,2,1,0:T(8,128)(2,1)S(1)}, u32[]{:S(2)}) copy-start(bf16[4,16,2,32,128]{4,3,2,1,0:T(8,128)(2,1)S(1)} %all-to-all-done.refs_1_) | copy-start | bytes 3145732
  298.1 60.6 %all-to-all-start.1 = ((bf16[4,16,2,32,128]{4,3,2,1,0:T(8,128)(2,1)}), bf16[4,16,2,32,128]{4,3,2,1,0:T(8,128)(2,1)}, u32[]{:S(2)}, u32[]{:S(2)}) async-start(bf16[4,16,2,32,128]{4,3,2,1,0:T(8,128)(2,1)} %collective-permute-done.8), calls=%async_computation.1 | async-start | bytes 2097152 | tf_op jit(solution)/shard_map/all_to_all | solution.py:226
  302.4 7.2 %collective-permute-start.19 = (bf16[4,4,2,64,128]{4,3,2,1,0:T(8,128)(2,1)S(1)}, bf16[4,4,2,64,128]{4,3,2,1,0:T(8,128)(2,1)}, u32[]{:S(2)}, u32[]{:S(2)}) collective-permute-start(bf16[4,4,2,64,128]{4,3,2,1,0:T(8,128)(2,1)S(1)} %slice_bitcast_fusion.2), channel_id=1, source_target_pairs={{0,448},{64,0},{128,64},{192,128},{256,192},{320,256},{384,320},{4... | collective-permute-start | bytes 1572872 | tf_op jit(solution)/shard_map/ppermute | solution.py:256
  302.4 17.3 %collective-permute-start.18 = (bf16[32,64,128]{2,1,0:T(8,128)(2,1)}, bf16[32,64,128]{2,1,0:T(8,128)(2,1)}, u32[]{:S(2)}, u32[]{:S(2)}) collective-permute-start(bf16[32,64,128]{2,1,0:T(8,128)(2,1)} %collective-permute-done.17.refs_2_), channel_id=1, source_target_pairs={{0,15},{1,0},{2,1},{3,2},{4,3},{5,4},{6,5},{7,6},{8,7},{9,8},{10,9... | collective-permute-start | bytes 1572872 | tf_op jit(solution)/shard_map/ppermute | solution.py:250
  307.6 17.4 %collective-permute-start.7 = (bf16[32,64,128]{2,1,0:T(8,128)(2,1)}, bf16[32,64,128]{2,1,0:T(8,128)(2,1)}, u32[]{:S(2)}, u32[]{:S(2)}) collective-permute-start(bf16[32,64,128]{2,1,0:T(8,128)(2,1)} %collective-permute-done.6.refs_1_), channel_id=1, source_target_pairs={{0,1},{1,2},{2,3},{3,4},{4,5},{5,6},{6,7},{7,8},{8,9},{9,10},{10,1... | collective-permute-start | bytes 1572872 | tf_op jit(solution)/shard_map/ppermute | solution.py:248
  358.7 96.3 %all-to-all-start.7 = ((bf16[4,2,4,2,64,128]{5,4,3,2,1,0:T(8,128)(2,1)}), bf16[4,2,4,2,64,128]{5,4,3,2,1,0:T(8,128)(2,1)S(1)}, u32[]{:S(2)}, u32[]{:S(2)}) async-start(bf16[4,2,4,2,64,128]{5,4,3,2,1,0:T(8,128)(2,1)} %shard_map.60), calls=%async_computation.7 | async-start | bytes 2097152 | tf_op jit(solution)/shard_map/all_to_all | solution.py:226
  363.5 16.3 %collective-permute-start.9 = (bf16[32,64,128]{2,1,0:T(8,128)(2,1)}, bf16[32,64,128]{2,1,0:T(8,128)(2,1)}, u32[]{:S(2)}, u32[]{:S(2)}) collective-permute-start(bf16[32,64,128]{2,1,0:T(8,128)(2,1)} %collective-permute-done.7.refs_3_), channel_id=1, source_target_pairs={{0,1},{1,2},{2,3},{3,4},{4,5},{5,6},{6,7},{7,8},{8,9},{9,10},{10,1... | collective-permute-start | bytes 1572872 | tf_op jit(solution)/shard_map/ppermute | solution.py:248
  366.2 79.0 %collective-permute-start.20 = (bf16[4,4,2,64,128]{4,3,2,1,0:T(8,128)(2,1)}, bf16[4,4,2,64,128]{4,3,2,1,0:T(8,128)(2,1)}, u32[]{:S(2)}, u32[]{:S(2)}) collective-permute-start(bf16[4,4,2,64,128]{4,3,2,1,0:T(8,128)(2,1)} %slice_bitcast_fusion.1), channel_id=1, source_target_pairs={{0,448},{64,0},{128,64},{192,128},{256,192},{320,256},{384,320},{4... | collective-permute-start | bytes 1572872 | tf_op jit(solution)/shard_map/ppermute | solution.py:256
  445.2 40.9 %collective-permute-start.10 = (bf16[4,16,2,32,128]{4,3,2,1,0:T(8,128)(2,1)}, bf16[4,16,2,32,128]{4,3,2,1,0:T(8,128)(2,1)}, u32[]{:S(2)}, u32[]{:S(2)}) collective-permute-start(bf16[4,16,2,32,128]{4,3,2,1,0:T(8,128)(2,1)} %get-tuple-element.16), channel_id=1, source_target_pairs={{0,448},{64,0},{128,64},{192,128},{256,192},{320,256},{384,320},{4... | collective-permute-start | bytes 3145736 | tf_op jit(solution)/shard_map/ppermute | solution.py:236
  486.1 18.3 %all-to-all-start.3 = ((bf16[4,16,2,32,128]{4,3,2,1,0:T(8,128)(2,1)}), bf16[4,16,2,32,128]{4,3,2,1,0:T(8,128)(2,1)}, u32[]{:S(2)}, u32[]{:S(2)}) async-start(bf16[4,16,2,32,128]{4,3,2,1,0:T(8,128)(2,1)} %collective-permute-done.10), calls=%async_computation.3 | async-start | bytes 2097152 | tf_op jit(solution)/shard_map/all_to_all | solution.py:226
  490.4 6.7 %collective-permute-start.21 = (bf16[4,4,2,64,128]{4,3,2,1,0:T(8,128)(2,1)S(1)}, bf16[4,4,2,64,128]{4,3,2,1,0:T(8,128)(2,1)S(1)}, u32[]{:S(2)}, u32[]{:S(2)}) collective-permute-start(bf16[4,4,2,64,128]{4,3,2,1,0:T(8,128)(2,1)S(1)} %slice_bitcast_fusion), channel_id=1, source_target_pairs={{0,448},{64,0},{128,64},{192,128},{256,192},{320,256},{384,320},{4... | collective-permute-start | bytes 1572872 | tf_op jit(solution)/shard_map/ppermute | solution.py:256
  490.5 8.1 %collective-permute-start.22 = (bf16[4,1,2,64,128]{4,3,2,1,0:T(8,128)(2,1)S(1)}, bf16[4,1,2,64,128]{4,3,2,1,0:T(8,128)(2,1)S(1)}, u32[]{:S(2)}, u32[]{:S(2)}) collective-permute-start(bf16[4,1,2,64,128]{4,3,2,1,0:T(8,128)(2,1)S(1)} %slice_bitcast_fusion.4), channel_id=1, source_target_pairs={{0,448},{64,0},{128,64},{192,128},{256,192},{320,256},{384,320},{4... | collective-permute-start | bytes 393224 | tf_op jit(solution)/shard_map/ppermute | solution.py:256
  497.1 0.8 copy-start.8
  504.4 1.1 copy-start.1
  505.6 1.2 copy-start.3
  506.8 1.2 copy-start.4
  508.0 1.6 copy-start.5
  509.6 1.0 copy-start.7
  510.6 1.0 copy-start.9
  (1 other events, 0.8 us)
Sparse Core Ops, SparseCore 0:
  9.4 98.6 all-gather.4
  110.2 81.0 all-gather.6

commit v3 on v0

v3 whole, which is shorter than its diff:
```python
import functools

import jax
import jax.numpy as jnp
from jax import lax
from jax.experimental import pallas as pl
from jax.experimental.pallas import tpu as pltpu
from jax.sharding import Mesh, PartitionSpec as P

BLOCK = 64
EPS = 1e-05
ADAPTER_SCALE = 0.5
X, CORES, Y, Z = 4, 2, 4, 16
SEGMENT = ("x", "core")
LANES = 128
ROWS = 128
WIDTH = 8192
RANK = 64

BATCHES = ((0, 1, 15), (2, 14, 3, 13), (4, 12, 5, 11), (6, 10), (7, 9, 8))
ORDER = tuple(d for batch in BATCHES for d in batch)

def block_adapters(starts, adapters, total_rows):
    blocks = total_rows // BLOCK
    block_start = jnp.arange(blocks, dtype=jnp.int32) * BLOCK
    request = jnp.sum((starts[None, :] <= block_start[:, None]).astype(jnp.int32), axis=1) - 1
    labels = jnp.arange(adapters.shape[0], dtype=jnp.int32)
    picked = jnp.where(request[:, None] == labels[None, :], adapters[None, :], 0)
    return jnp.sum(picked, axis=1)


def pick_kernel(count, wanted, *refs):
    out = refs[-1]
    for y in range(Y):
        for k in range(2):
            for b in range(2):
                which = wanted[y, k, b]
                for c in range(count):
                    out[y, k, c, b] = refs[c][which]


def pick(wanted, chunks, after):
    count = len(chunks)
    return pl.pallas_call(
        functools.partial(pick_kernel, count),
        out_shape=jax.ShapeDtypeStruct((Y, 2, count, 2, RANK, LANES), jnp.bfloat16),
        in_specs=[pl.BlockSpec(memory_space=pltpu.SMEM)]
        + [pl.BlockSpec(memory_space=pltpu.VMEM)] * count
        + [pl.BlockSpec(memory_space=pl.ANY)] * len(after),
        out_specs=pl.BlockSpec(memory_space=pltpu.VMEM),
        compiler_params=pltpu.CompilerParams(vmem_limit_bytes=12 << 20),
        cost_estimate=pl.CostEstimate(
            flops=0, transcendentals=0, bytes_accessed=count * (3 << 18)
        ),
    )(wanted, *chunks, *after)


def norm_kernel(hidden, out):
    total = jnp.zeros((ROWS, LANES), jnp.float32)
    for i in range(WIDTH // LANES):
        v = hidden[:, i * LANES : (i + 1) * LANES].astype(jnp.float32)
        total = total + v * v
    scale = lax.rsqrt(jnp.sum(total, axis=1, keepdims=True) / WIDTH + EPS)
    scale = jnp.broadcast_to(scale, (ROWS, LANES))
    for y in range(Y):
        for i in range(Z):
            v = hidden[:, (y * Z + i) * LANES : (y * Z + i + 1) * LANES].astype(jnp.float32)
            out[y, :, i * LANES : (i + 1) * LANES] = (v * scale).astype(jnp.bfloat16)


def norm(hidden):
    vmem = pl.BlockSpec(memory_space=pltpu.VMEM)
    return pl.pallas_call(
        norm_kernel,
        out_shape=jax.ShapeDtypeStruct((Y, ROWS, Z * LANES), jnp.bfloat16),
        in_specs=[vmem],
        out_specs=vmem,
        compiler_params=pltpu.CompilerParams(vmem_limit_bytes=12 << 20),
        cost_estimate=pl.CostEstimate(
            flops=1 << 22, transcendentals=0, bytes_accessed=4 << 20
        ),
    )(hidden)


HALF = RANK // 2


def down_kernel(wanted, gathered, normed, *refs):
    *halves, partial = refs[-3:]
    for y in range(Y):
        for b in range(2):
            which = wanted[y, 1, b]
            for z in range(Z):
                for h, theirs in enumerate(halves):
                    theirs[y, z, b] = gathered[z, which, h * HALF : (h + 1) * HALF]
    for y in range(Y):
        for b in range(2):
            which = wanted[y, 0, b]
            rows = slice(b * BLOCK, (b + 1) * BLOCK)
            panel = jnp.concatenate([gathered[z, which] for z in range(Z)], axis=1)
            product = lax.dot_general(
                normed[y, rows], panel, (((1,), (1,)), ((), ())),
                preferred_element_type=jnp.float32,
            )
            partial[y, rows] = jnp.concatenate([product, product], axis=1)


def down(wanted, gathered, normed, *after):
    vmem = pl.BlockSpec(memory_space=pltpu.VMEM)
    return pl.pallas_call(
        down_kernel,
        out_shape=[
            jax.ShapeDtypeStruct((Y, Z, 2, HALF, LANES), jnp.bfloat16),
            jax.ShapeDtypeStruct((Y, Z, 2, HALF, LANES), jnp.bfloat16),
            jax.ShapeDtypeStruct((Y, ROWS, 2 * RANK), jnp.float32),
        ],
        in_specs=[pl.BlockSpec(memory_space=pltpu.SMEM), vmem, vmem]
        + [pl.BlockSpec(memory_space=pl.ANY)] * len(after),
        out_specs=[vmem] * 3,
        compiler_params=pltpu.CompilerParams(vmem_limit_bytes=20 << 20),
        cost_estimate=pl.CostEstimate(
            flops=1 << 27, transcendentals=0, bytes_accessed=12 << 20
        ),
    )(wanted, gathered, normed, *after)


def place(z, y, d):
    return pl.ds(pl.multiple_of((y * Z + ((z - d) & (Z - 1))) * LANES, LANES), LANES)


def slot(y, i, width):
    return pl.ds((y * Z + i) * LANES, width * LANES)


def up_panels(ref, y, i):
    return jnp.concatenate(
        [ref[y, i + j].reshape(2 * RANK, LANES) for j in range(4)], axis=1
    )


def own_block():
    return lax.broadcasted_iota(jnp.int32, (ROWS, 2 * RANK), 0) // BLOCK == (
        lax.broadcasted_iota(jnp.int32, (ROWS, 2 * RANK), 1) // RANK
    )


GROUPS = tuple((y, i, ORDER[i : i + 4]) for y in range(Y) for i in range(0, Z, 4))


def updated(state, rank, panel):
    delta = jnp.dot(rank, panel, preferred_element_type=jnp.float32)
    delta = delta.astype(jnp.bfloat16).astype(jnp.float32)
    return (state.astype(jnp.float32) + ADAPTER_SCALE * delta).astype(jnp.bfloat16)


def first_kernel(z_ref, rank_ref, hidden_hbm, *refs):
    n = len(BATCHES)
    batches, state_hbm = refs[:n], refs[n]
    hidden, state, panels, sems = refs[n + 1 :]
    z = z_ref[0]
    loads = [pltpu.make_async_copy(hidden_hbm, hidden, sems.at[0])]
    at = 0
    for b, batch in enumerate(BATCHES):
        loads.append(
            pltpu.make_async_copy(
                batches[b].at[:, 0], panels.at[:, pl.ds(at, len(batch))], sems.at[b + 1]
            )
        )
        at += len(batch)
    for c in loads:
        c.start()
    rank = rank_ref[0]
    for y in range(1, Y):
        rank = rank + rank_ref[y]
    rank = jnp.where(own_block(), rank, 0.0).astype(jnp.bfloat16)
    for c in loads:
        c.wait()
    stores = []
    for y, i, ds in GROUPS:
        old = jnp.concatenate([hidden[:, place(z, y, d)] for d in ds], axis=1)
        state[:, slot(y, i, 4)] = updated(old, rank, up_panels(panels, y, i))
        if i + 4 == Z:
            part = slot(y, 0, Z)
            stores.append(
                pltpu.make_async_copy(
                    state.at[:, part], state_hbm.at[:, part], sems.at[n + 1 + y]
                )
            )
            stores[-1].start()
    for c in stores:
        c.wait()


def second_kernel(z_ref, state_hbm, *refs):
    halves, refs = refs[:2], refs[2:]
    n = len(BATCHES)
    batches, out_hbm = refs[:n], refs[n]
    state, low, panels, out, sems = refs[n + 1 :]
    z = z_ref[0]
    state_in = pltpu.make_async_copy(state_hbm, state, sems.at[0])
    low_in = [
        pltpu.make_async_copy(
            half, low.at[:, :, :, pl.ds(h * HALF, HALF)], sems.at[n + 2 + Y + h]
        )
        for h, half in enumerate(halves)
    ]
    loads = []
    at = 0
    for b, batch in enumerate(BATCHES):
        loads.append(
            pltpu.make_async_copy(
                batches[b], panels.at[:, pl.ds(at, len(batch))], sems.at[b + 2]
            )
        )
        at += len(batch)
    for c in [state_in] + low_in + loads:
        c.start()
    state_in.wait()
    total = jnp.zeros((ROWS, LANES), jnp.float32)
    for y, i, ds in GROUPS:
        for j in range(4):
            v = state[:, slot(y, i + j, 1)].astype(jnp.float32)
            total = total + v * v
    scale = lax.rsqrt(jnp.sum(total, axis=1, keepdims=True) / WIDTH + EPS)
    scale = jnp.broadcast_to(scale, (ROWS, 4 * LANES))
    rank = jnp.zeros((ROWS, 2 * RANK), jnp.float32)
    for c in low_in:
        c.wait()
    for y, i, ds in GROUPS:
        v = (state[:, slot(y, i, 4)].astype(jnp.float32) * scale).astype(jnp.bfloat16)
        panel = jnp.concatenate(
            [low[y, (z - d) & (Z - 1)].reshape(2 * RANK, LANES) for d in ds], axis=1
        )
        rank = rank + lax.dot_general(
            v, panel, (((1,), (1,)), ((), ())), preferred_element_type=jnp.float32
        )
    rank = jnp.where(own_block(), rank, 0.0).astype(jnp.bfloat16)
    for c in loads:
        c.wait()
    stores = []
    for y, i, ds in GROUPS:
        new = updated(state[:, slot(y, i, 4)], rank, up_panels(panels, y, i))
        for j, d in enumerate(ds):
            out[:, place(z, y, d)] = new[:, j * LANES : (j + 1) * LANES]
        if i + 4 == Z:
            part = slot(y, 0, Z)
            stores.append(
                pltpu.make_async_copy(
                    out.at[:, part], out_hbm.at[:, part], sems.at[n + 2 + y]
                )
            )
            stores[-1].start()
    for c in stores:
        c.wait()


ROW_BUFFER = pltpu.VMEM((ROWS, WIDTH), jnp.bfloat16)
PANEL_BUFFER = pltpu.VMEM((Y, Z, 2, RANK, LANES), jnp.bfloat16)


def layer_call(kernel, in_specs, scratch, *operands):
    anywhere = pl.BlockSpec(memory_space=pl.ANY)
    return pl.pallas_call(
        kernel,
        out_shape=jax.ShapeDtypeStruct((ROWS, WIDTH), jnp.bfloat16),
        in_specs=in_specs + [anywhere] * (len(operands) - len(in_specs)),
        out_specs=anywhere,
        scratch_shapes=scratch + [pltpu.SemaphoreType.DMA((4 + len(BATCHES) + Y,))],
        compiler_params=pltpu.CompilerParams(vmem_limit_bytes=60 << 20),
        cost_estimate=pl.CostEstimate(
            flops=1 << 29, transcendentals=0, bytes_accessed=6 << 20
        ),
    )(*operands)


def after(value, *others):
    return lax.optimization_barrier((value, *others))[0]


def shards(hidden, store_a, store_b, request_start, request_adapter):
    mine = block_adapters(request_start[0], request_adapter[0], Y * Z * ROWS)
    segments = X * CORES
    ahead = [(s, (s + 1) % segments) for s in range(segments)]
    back = [(s, (s - 1) % segments) for s in range(segments)]
    behind = lax.ppermute(mine, SEGMENT, ahead)
    z = lax.axis_index("z")

    def at_z(chosen):
        rows = chosen.reshape(Y, Z, 2)
        here = lax.broadcasted_iota(jnp.int32, rows.shape, 1) == z
        return jnp.sum(jnp.where(here, rows, 0), axis=1)

    wanted = jnp.stack([at_z(mine), at_z(behind)], axis=1)

    def over_y(x):
        return lax.all_to_all(x, "y", split_axis=0, concat_axis=0, tiled=True)

    gathered = lax.all_gather(store_a[0], "z")
    normed = over_y(norm(hidden[0]))

    up = [(i, (i + 1) % Z) for i in range(Z)]
    low = [(i, (i - 1) % Z) for i in range(Z)]
    chunks = {0: store_b[0]}
    first, second = [], []

    def send_on(*earlier):
        picked = pick(wanted, [chunks[d] for d in BATCHES[len(first)]], earlier)
        received = over_y(picked)
        first.append(received)
        second.append(lax.ppermute(received[:, 1], SEGMENT, back))
        return picked

    for step in range(1, 9):
        chunks[step] = lax.ppermute(chunks[step - 1], "z", up)
        if step < 8:
            chunks[Z - step] = lax.ppermute(chunks[(Z + 1 - step) % Z], "z", low)
        b = len(first)
        if b < 4 and all(d in chunks for d in BATCHES[b]):
            picked = send_on(*second[b - 2 : b - 1] if b > 1 else (normed,) if b == 0 else ())
    *halves, partial = down(wanted, gathered, normed, chunks[6])
    halves = [lax.ppermute(half, SEGMENT, back) for half in halves]
    rank = over_y(after(partial, chunks[7], chunks[9]))
    halves = [over_y(after(halves[0], rank)), over_y(after(halves[1], chunks[8]))]
    send_on(second[2], rank)
    z = z.astype(jnp.int32)[None]
    smem, vmem = (pl.BlockSpec(memory_space=m) for m in (pltpu.SMEM, pltpu.VMEM))
    state = layer_call(
        first_kernel, [smem, vmem], [ROW_BUFFER] * 2 + [PANEL_BUFFER], z, rank, hidden[0], *first
    )
    updated_rows = layer_call(
        second_kernel, [smem], [ROW_BUFFER] + [PANEL_BUFFER] * 2 + [ROW_BUFFER],
        z, state, *halves, *second,
    )
    return updated_rows[None]


def solution(mesh):
    grid = Mesh(mesh.devices.reshape(X, CORES, Y, Z), ("x", "core", "y", "z"))
    return jax.shard_map(
        shards,
        mesh=grid,
        in_specs=(
            P(SEGMENT, ("y", "z"), None),
            P(SEGMENT, None, None, ("y", "z")),
            P(SEGMENT, None, None, ("y", "z")),
            P(SEGMENT, None),
            P(SEGMENT, None),
        ),
        out_specs=P(SEGMENT, ("y", "z"), None),
        check_vma=False,
    )
```

time: 1130 us -> 280 us (0.25)
  blocking collectives: 825 us -> 0 us
  waiting for transfers between devices: 233 us -> 120 us
  starting transfers between devices: 28.4 us -> 102 us
  Pallas kernels: 0 us -> 25.2 us
  matrix products: 16.9 us -> 0 us
  between operations: 0.16 us -> 13.8 us
    psum x2 -> x0, blocking collectives: 710 us -> none  [apply_layer(): rank = lax.psum(partial_rank, 'dp').astype(jnp.bfloat16)]
    all_to_all x2 -> x9, waiting for transfers between devices: 178 us -> 29.2 us  [over_y(): return lax.all_to_all(x, 'y', split_axis=0, concat_axis=0, tiled=True)]
    all_to_all x2 -> x0, blocking collectives: 114 us -> none  [apply_layer(): lax.all_to_all(adapter_update, 'dp', split_axis=0, concat_axis=1, tiled=T...]
    ppermute x4 -> x23, starting transfers between devices: 0.07 us -> 62.3 us  [the longest x7 42.6 us: shards(): chunks[Z - step] = lax.ppermute(chunks[(Z + 1 - step) % Z], 'z', low)]
    ppermute x4 -> x23, waiting for transfers between devices: 54.9 us -> 89.6 us  [the longest x8 82.5 us: shards(): chunks[step] = lax.ppermute(chunks[step - 1], 'z', up)]
    pallas_call x0 -> x9, Pallas kernels: none -> 25.2 us  [the longest x5 11.3 us: pick(): pl.pallas_call(functools.partial(pick_kernel, count), out_shape=jax.Shape...]
    dot_general x4 -> x0, matrix products: 16.9 us -> none  [the longest x2 10.9 us: apply_layer(): jnp.einsum('bic,brc->bir', grouped, down, preferred_element_type=jnp.floa...]
    all_to_all x2 -> x9, starting transfers between devices: 28.3 us -> 39.7 us  [over_y(): return lax.all_to_all(x, 'y', split_axis=0, concat_axis=0, tiled=True)]
  transfers between devices with their start and end apart: 6 -> 33, of which waited for: 6 -> 17; matrix products, arithmetic and copies ran while one was open for 1% -> 2% of each run, Pallas kernels for 0% -> 7%
where the time goes in v3:
time: 280 us; the launch traced here: 277 us
  waiting for transfers between devices  120 us (43%)
  starting transfers between devices  102 us (36%)
  Pallas kernels  25.2 us (9%)
  local copies, waits for them, and re-layouts  16.3 us (6%)
  between operations  13.8 us (5%)
    ppermute x8, waiting for transfers between devices, shards(): chunks[step] = lax.ppermute(chunks[step - 1], 'z', up)  82.5 us
    ppermute x7, starting transfers between devices, shards(): chunks[Z - step] = lax.ppermute(chunks[(Z + 1 - step) % Z], 'z', low)  42.6 us
    all_to_all x9, starting transfers between devices, over_y(): return lax.all_to_all(x, 'y', split_axis=0, concat_axis=0, tiled=True)  39.7 us
    all_to_all x9, waiting for transfers between devices, over_y(): return lax.all_to_all(x, 'y', split_axis=0, concat_axis=0, tiled=True)  29.2 us
    ppermute x8, starting transfers between devices, shards(): chunks[step] = lax.ppermute(chunks[step - 1], 'z', up)  17.2 us
    pallas_call x5, Pallas kernels, pick(): pl.pallas_call(functools.partial(pick_kernel, count), out_shape=jax.Shape...  11.3 us
    pallas_call x2, Pallas kernels, layer_call(): pl.pallas_call(kernel, out_shape=jax.ShapeDtypeStruct((ROWS, WIDTH), jnp....  10.7 us
    unnamed x36, local copies, waits for them, and re-layouts  10.2 us
  transfers between devices with their start and end apart: 33, of which 17 were waited for; matrix products, arithmetic and copies ran while one was open for 2% of the time, Pallas kernels for 7%

profile of v3, /device:TPU:6, one launch (start us, length us, event | category | flops | bytes accessed | tf_op | source)
XLA Modules:
  0.0 277.1 jit_solution(7291099506847083110)
XLA Ops:
  7.3 3.8 %collective-permute-start.1 = (bf16[32,64,128]{2,1,0:T(8,128)(2,1)}, bf16[32,64,128]{2,1,0:T(8,128)(2,1)S(1)}, u32[]{:S(2)}, u32[]{:S(2)}) collective-permute-start(bf16[32,64,128]{2,1,0:T(8,128)(2,1)} %bitcast.34), channel_id=1, source_target_pairs={{0,1},{1,2},{2,3},{3,4},{4,5},{5,6},{6,7},{7,8},{8,9},{9,10},{10,1... | collective-permute-start | bytes 1572872 | tf_op jit(solution)/shard_map/ppermute | solution.py:314
  11.1 9.5 %collective-permute-start.8 = (bf16[32,64,128]{2,1,0:T(8,128)(2,1)}, bf16[32,64,128]{2,1,0:T(8,128)(2,1)}, u32[]{:S(2)}, u32[]{:S(2)}) collective-permute-start(bf16[32,64,128]{2,1,0:T(8,128)(2,1)} %bitcast.35), channel_id=1, source_target_pairs={{0,15},{1,0},{2,1},{3,2},{4,3},{5,4},{6,5},{7,6},{8,7},{9,8},{10,9... | collective-permute-start | bytes 1572872 | tf_op jit(solution)/shard_map/ppermute | solution.py:316
  20.6 1.6 copy-done
  24.5 4.6 %all-to-all-start = ((bf16[4,128,2048]{2,1,0:T(8,128)(2,1)}), bf16[4,128,2048]{2,1,0:T(8,128)(2,1)S(1)}, u32[]{:S(2)}, u32[]{:S(2)}) async-start(bf16[4,128,2048]{2,1,0:T(8,128)(2,1)} %copy-done.2), calls=%async_computation | async-start | bytes 4194304 | tf_op jit(solution)/shard_map/all_to_all | solution.py:296
  29.1 1.7 collective-permute-done.1.refs_1_
  30.8 1.9 collective-permute-start.2
  32.7 2.3 collective-permute-done.8.refs_2_
  35.0 5.6 %collective-permute-start.9 = (bf16[32,64,128]{2,1,0:T(8,128)(2,1)}, bf16[32,64,128]{2,1,0:T(8,128)(2,1)}, u32[]{:S(2)}, u32[]{:S(2)}) collective-permute-start(bf16[32,64,128]{2,1,0:T(8,128)(2,1)} %collective-permute-done.8.refs_2_), channel_id=1, source_target_pairs={{0,15},{1,0},{2,1},{3,2},{4,3},{5,4},{6,5},{7,6},{8,7},{9,8},{10,9... | collective-permute-start | bytes 1572872 | tf_op jit(solution)/shard_map/ppermute | solution.py:316
  40.7 18.7 %collective-permute-done.2.refs_0_ = bf16[32,64,128]{2,1,0:T(8,128)(2,1)} collective-permute-done((bf16[32,64,128]{2,1,0:T(8,128)(2,1)S(1)}, bf16[32,64,128]{2,1,0:T(8,128)(2,1)}, u32[]{:S(2)}, u32[]{:S(2)}) %collective-permute-start.2) | collective-permute-done | bytes 524320 | tf_op jit(solution)/shard_map/ppermute | solution.py:314
  59.3 1.9 collective-permute-start.3
  62.3 5.6 %collective-permute-start.10 = (bf16[32,64,128]{2,1,0:T(8,128)(2,1)}, bf16[32,64,128]{2,1,0:T(8,128)(2,1)}, u32[]{:S(2)}, u32[]{:S(2)}) collective-permute-start(bf16[32,64,128]{2,1,0:T(8,128)(2,1)} %collective-permute-done.9.refs_1_), channel_id=1, source_target_pairs={{0,15},{1,0},{2,1},{3,2},{4,3},{5,4},{6,5},{7,6},{8,7},{9,8},{10,9... | collective-permute-start | bytes 1572872 | tf_op jit(solution)/shard_map/ppermute | solution.py:316
  68.2 2.8 %collective-permute-done = s32[128]{0:T(128)S(1)} collective-permute-done((s32[128]{0:T(128)S(1)}, s32[128]{0:T(128)S(1)}, u32[]{:S(2)}, u32[]{:S(2)}) %collective-permute-start) | collective-permute-done | bytes 544 | tf_op jit(solution)/shard_map/ppermute | solution.py:285
  71.2 2.0 shard_map.57
  73.2 5.0 %all-to-all-start.2 = ((bf16[4,2,3,2,64,128]{5,4,3,2,1,0:T(8,128)(2,1)}), bf16[4,2,3,2,64,128]{5,4,3,2,1,0:T(8,128)(2,1)}, u32[]{:S(2)}, u32[]{:S(2)}) async-start(bf16[4,2,3,2,64,128]{5,4,3,2,1,0:T(8,128)(2,1)} %shard_map.57), calls=%async_computation.2 | async-start | bytes 1572864 | tf_op jit(solution)/shard_map/all_to_all | solution.py:296
  78.2 9.6 %collective-permute-done.3.refs_2_ = bf16[32,64,128]{2,1,0:T(8,128)(2,1)} collective-permute-done((bf16[32,64,128]{2,1,0:T(8,128)(2,1)}, bf16[32,64,128]{2,1,0:T(8,128)(2,1)}, u32[]{:S(2)}, u32[]{:S(2)}) %collective-permute-start.3) | collective-permute-done | bytes 524320 | tf_op jit(solution)/shard_map/ppermute | solution.py:314
  87.8 1.9 collective-permute-start.4
  90.1 5.6 %collective-permute-start.11 = (bf16[32,64,128]{2,1,0:T(8,128)(2,1)}, bf16[32,64,128]{2,1,0:T(8,128)(2,1)}, u32[]{:S(2)}, u32[]{:S(2)}) collective-permute-start(bf16[32,64,128]{2,1,0:T(8,128)(2,1)} %collective-permute-done.10.refs_3_), channel_id=1, source_target_pairs={{0,15},{1,0},{2,1},{3,2},{4,3},{5,4},{6,5},{7,6},{8,7},{9,8},{10,9... | collective-permute-start | bytes 1572872 | tf_op jit(solution)/shard_map/ppermute | solution.py:316
  95.7 20.2 %collective-permute-done.4.refs_0_ = bf16[32,64,128]{2,1,0:T(8,128)(2,1)S(1)} collective-permute-done((bf16[32,64,128]{2,1,0:T(8,128)(2,1)}, bf16[32,64,128]{2,1,0:T(8,128)(2,1)S(1)}, u32[]{:S(2)}, u32[]{:S(2)}) %collective-permute-start.4) | collective-permute-done | bytes 524320 | tf_op jit(solution)/shard_map/ppermute | solution.py:314
  115.9 1.9 collective-permute-start.5
  117.9 5.6 %collective-permute-start.12 = (bf16[32,64,128]{2,1,0:T(8,128)(2,1)}, bf16[32,64,128]{2,1,0:T(8,128)(2,1)}, u32[]{:S(2)}, u32[]{:S(2)}) collective-permute-start(bf16[32,64,128]{2,1,0:T(8,128)(2,1)} %collective-permute-done.11.refs_1_), channel_id=1, source_target_pairs={{0,15},{1,0},{2,1},{3,2},{4,3},{5,4},{6,5},{7,6},{8,7},{9,8},{10,9... | collective-permute-start | bytes 1572872 | tf_op jit(solution)/shard_map/ppermute | solution.py:316
  123.5 2.6 shard_map.58
  126.1 4.8 %all-to-all-start.3 = ((bf16[4,2,4,2,64,128]{5,4,3,2,1,0:T(8,128)(2,1)}), bf16[4,2,4,2,64,128]{5,4,3,2,1,0:T(8,128)(2,1)}, u32[]{:S(2)}, u32[]{:S(2)}) async-start(bf16[4,2,4,2,64,128]{5,4,3,2,1,0:T(8,128)(2,1)} %shard_map.58), calls=%async_computation.3 | async-start | bytes 2097152 | tf_op jit(solution)/shard_map/all_to_all | solution.py:296
  131.9 11.7 %collective-permute-done.5.refs_2_ = bf16[32,64,128]{2,1,0:T(8,128)(2,1)} collective-permute-done((bf16[32,64,128]{2,1,0:T(8,128)(2,1)S(1)}, bf16[32,64,128]{2,1,0:T(8,128)(2,1)}, u32[]{:S(2)}, u32[]{:S(2)}) %collective-permute-start.5) | collective-permute-done | bytes 524320 | tf_op jit(solution)/shard_map/ppermute | solution.py:314
  143.6 1.9 collective-permute-start.6
  145.6 5.6 %collective-permute-start.13 = (bf16[32,64,128]{2,1,0:T(8,128)(2,1)}, bf16[32,64,128]{2,1,0:T(8,128)(2,1)}, u32[]{:S(2)}, u32[]{:S(2)}) collective-permute-start(bf16[32,64,128]{2,1,0:T(8,128)(2,1)} %collective-permute-done.12.refs_3_), channel_id=1, source_target_pairs={{0,15},{1,0},{2,1},{3,2},{4,3},{5,4},{6,5},{7,6},{8,7},{9,8},{10,9... | collective-permute-start | bytes 1572872 | tf_op jit(solution)/shard_map/ppermute | solution.py:316
  151.2 2.5 shard_map.59
  153.8 4.7 %all-to-all-start.4 = ((bf16[4,2,4,2,64,128]{5,4,3,2,1,0:T(8,128)(2,1)}), bf16[4,2,4,2,64,128]{5,4,3,2,1,0:T(8,128)(2,1)}, u32[]{:S(2)}, u32[]{:S(2)}) async-start(bf16[4,2,4,2,64,128]{5,4,3,2,1,0:T(8,128)(2,1)} %shard_map.59), calls=%async_computation.4 | async-start | bytes 2097152 | tf_op jit(solution)/shard_map/all_to_all | solution.py:296
  158.5 12.7 %collective-permute-done.6.refs_0_ = bf16[32,64,128]{2,1,0:T(8,128)(2,1)S(1)} collective-permute-done((bf16[32,64,128]{2,1,0:T(8,128)(2,1)}, bf16[32,64,128]{2,1,0:T(8,128)(2,1)S(1)}, u32[]{:S(2)}, u32[]{:S(2)}) %collective-permute-start.6) | collective-permute-done | bytes 524320 | tf_op jit(solution)/shard_map/ppermute | solution.py:314
  171.2 1.9 collective-permute-start.7
  173.1 5.1 %collective-permute-start.14 = (bf16[32,64,128]{2,1,0:T(8,128)(2,1)}, bf16[32,64,128]{2,1,0:T(8,128)(2,1)}, u32[]{:S(2)}, u32[]{:S(2)}) collective-permute-start(bf16[32,64,128]{2,1,0:T(8,128)(2,1)} %collective-permute-done.13.refs_1_), channel_id=1, source_target_pairs={{0,15},{1,0},{2,1},{3,2},{4,3},{5,4},{6,5},{7,6},{8,7},{9,8},{10,9... | collective-permute-start | bytes 1572872 | tf_op jit(solution)/shard_map/ppermute | solution.py:316
  178.3 1.9 slice_bitcast_fusion.1
  180.2 3.4 %copy-done.1 = bf16[16,32,64,128]{3,2,1,0:T(8,128)(2,1)S(1)} copy-done((bf16[16,32,64,128]{3,2,1,0:T(8,128)(2,1)S(1)}, bf16[16,32,64,128]{3,2,1,0:T(8,128)(2,1)}, u32[]{:S(2)}) %copy-start.1) | copy-done | bytes 8388632
  183.6 2.2 shard_map.56
  187.8 4.6 %all-to-all-start.1 = ((f32[4,128,128]{2,1,0:T(8,128)}), f32[4,128,128]{2,1,0:T(8,128)S(1)}, u32[]{:S(2)}, u32[]{:S(2)}) async-start(f32[4,128,128]{2,1,0:T(8,128)} %get-tuple-element.12), calls=%async_computation.1 | async-start | bytes 524288 | tf_op jit(solution)/shard_map/all_to_all | solution.py:296
  192.3 1.9 slice_bitcast_fusion
  194.9 1.9 collective-permute-start.17
  197.1 2.1 shard_map.60
  199.7 4.3 %all-to-all-start.5 = ((bf16[4,2,2,2,64,128]{5,4,3,2,1,0:T(8,128)(2,1)}), bf16[4,2,2,2,64,128]{5,4,3,2,1,0:T(8,128)(2,1)}, u32[]{:S(2)}, u32[]{:S(2)}) async-start(bf16[4,2,2,2,64,128]{5,4,3,2,1,0:T(8,128)(2,1)} %shard_map.60), calls=%async_computation.5 | async-start | bytes 1048576 | tf_op jit(solution)/shard_map/all_to_all | solution.py:296
  204.0 7.9 %collective-permute-done.17.refs_2_ = bf16[32,64,128]{2,1,0:T(8,128)(2,1)S(1)} collective-permute-done((bf16[32,64,128]{2,1,0:T(8,128)(2,1)}, bf16[32,64,128]{2,1,0:T(8,128)(2,1)S(1)}, u32[]{:S(2)}, u32[]{:S(2)}) %collective-permute-start.17) | collective-permute-done | bytes 524320 | tf_op jit(solution)/shard_map/ppermute | solution.py:314
  211.9 2.1 shard_map.61
  214.0 4.8 %all-to-all-start.6 = ((bf16[4,2,3,2,64,128]{5,4,3,2,1,0:T(8,128)(2,1)}), bf16[4,2,3,2,64,128]{5,4,3,2,1,0:T(8,128)(2,1)S(1)}, u32[]{:S(2)}, u32[]{:S(2)}) async-start(bf16[4,2,3,2,64,128]{5,4,3,2,1,0:T(8,128)(2,1)} %shard_map.61), calls=%async_computation.6 | async-start | bytes 1572864 | tf_op jit(solution)/shard_map/all_to_all | solution.py:296
  218.8 11.8 %all-to-all-done.6.refs_4_ = bf16[4,2,3,2,64,128]{5,4,3,2,1,0:T(8,128)(2,1)S(1)} async-done(((bf16[4,2,3,2,64,128]{5,4,3,2,1,0:T(8,128)(2,1)}), bf16[4,2,3,2,64,128]{5,4,3,2,1,0:T(8,128)(2,1)S(1)}, u32[]{:S(2)}, u32[]{:S(2)}) %all-to-all-start.6) | async-done | bytes 786464 | tf_op jit(solution)/shard_map/all_to_all | solution.py:296
  230.6 3.5 %all-to-all-start.7 = ((bf16[4,16,2,32,128]{4,3,2,1,0:T(8,128)(2,1)}), bf16[4,16,2,32,128]{4,3,2,1,0:T(8,128)(2,1)S(1)}, u32[]{:S(2)}, u32[]{:S(2)}) async-start(bf16[4,16,2,32,128]{4,3,2,1,0:T(8,128)(2,1)} %collective-permute-done.19), calls=%async_computation.7 | async-start | bytes 2097152 | tf_op jit(solution)/shard_map/all_to_all | solution.py:296
  235.1 12.6 %all-to-all-done.7.refs_0_ = bf16[4,16,2,32,128]{4,3,2,1,0:T(8,128)(2,1)S(1)} async-done(((bf16[4,16,2,32,128]{4,3,2,1,0:T(8,128)(2,1)}), bf16[4,16,2,32,128]{4,3,2,1,0:T(8,128)(2,1)S(1)}, u32[]{:S(2)}, u32[]{:S(2)}) %all-to-all-start.7) | async-done | bytes 1048608 | tf_op jit(solution)/shard_map/all_to_all | solution.py:296
  247.8 3.5 %all-to-all-start.8 = ((bf16[4,16,2,32,128]{4,3,2,1,0:T(8,128)(2,1)}), bf16[4,16,2,32,128]{4,3,2,1,0:T(8,128)(2,1)S(1)}, u32[]{:S(2)}, u32[]{:S(2)}) async-start(bf16[4,16,2,32,128]{4,3,2,1,0:T(8,128)(2,1)} %copy-done.13), calls=%async_computation.8 | async-start | bytes 2097152 | tf_op jit(solution)/shard_map/all_to_all | solution.py:296
  253.9 5.1 %shard_map.62.state_hbm = bf16[128,8192]{1,0:T(8,128)(2,1)} custom-call(s32[1]{0:T(128)} %bitcast.z_ref, f32[4,128,128]{2,1,0:T(8,128)} %copy-done.3, bf16[128,8192]{1,0:T(8,128)(2,1)} %bitcast.32, bf16[4,2,3,2,64,128]{5,4,3,2,1,0:T(8,128)(2,1)} %all-to-all-done.2.refs_0_, bf16[4,2,4,2,64,128]{5,4,3,2,1,0:T(8,128)(2,1)} %all-to-all-done.3.refs_1_, ...), custom_call_target="tpu_custom_call" | custom-call | flops 536870912 | bytes 6291456 | tf_op jit(solution)/shard_map/pallas_call | solution.py:263
  259.5 4.2 %all-to-all-done.8.refs_1_ = bf16[4,16,2,32,128]{4,3,2,1,0:T(8,128)(2,1)S(1)} async-done(((bf16[4,16,2,32,128]{4,3,2,1,0:T(8,128)(2,1)}), bf16[4,16,2,32,128]{4,3,2,1,0:T(8,128)(2,1)S(1)}, u32[]{:S(2)}, u32[]{:S(2)}) %all-to-all-start.8) | async-done | bytes 1048608 | tf_op jit(solution)/shard_map/all_to_all | solution.py:296
  264.7 5.6 %shard_map.63 = bf16[128,8192]{1,0:T(8,128)(2,1)} custom-call(s32[1]{0:T(128)} %bitcast.z_ref, bf16[128,8192]{1,0:T(8,128)(2,1)} %shard_map.62.state_hbm, bf16[4,16,2,32,128]{4,3,2,1,0:T(8,128)(2,1)} %copy-done.11, bf16[4,16,2,32,128]{4,3,2,1,0:T(8,128)(2,1)} %copy-done.12, bf16[4,3,2,64,128]{4,3,2,1,0:T(8,128)(2,1)} %copy-done.6, ...), custom_call_target="tpu_custom_call" | custom-call | flops 536870912 | bytes 6291456 | tf_op jit(solution)/shard_map/pallas_call | solution.py:263
  (78 shorter events, 14.6 us)
Async XLA Ops:
  6.5 173.7 %all-gather.2.cloned.1.call-start = ((), (), s32[]{:S(2)}) async-start(), calls=%async_computation.9 | async-start | bytes 8912896 | tf_op jit(solution)/shard_map/all_gather | solution.py:298
  7.3 23.5 %collective-permute-start.1 = (bf16[32,64,128]{2,1,0:T(8,128)(2,1)}, bf16[32,64,128]{2,1,0:T(8,128)(2,1)S(1)}, u32[]{:S(2)}, u32[]{:S(2)}) collective-permute-start(bf16[32,64,128]{2,1,0:T(8,128)(2,1)} %bitcast.34), channel_id=1, source_target_pairs={{0,1},{1,2},{2,3},{3,4},{4,5},{5,6},{6,7},{7,8},{8,9},{9,10},{10,1... | collective-permute-start | bytes 1572872 | tf_op jit(solution)/shard_map/ppermute | solution.py:314
  11.1 23.9 %collective-permute-start.8 = (bf16[32,64,128]{2,1,0:T(8,128)(2,1)}, bf16[32,64,128]{2,1,0:T(8,128)(2,1)}, u32[]{:S(2)}, u32[]{:S(2)}) collective-permute-start(bf16[32,64,128]{2,1,0:T(8,128)(2,1)} %bitcast.35), channel_id=1, source_target_pairs={{0,15},{1,0},{2,1},{3,2},{4,3},{5,4},{6,5},{7,6},{8,7},{9,8},{10,9... | collective-permute-start | bytes 1572872 | tf_op jit(solution)/shard_map/ppermute | solution.py:316
  20.6 1.6 copy-start
  23.2 1.3 copy-start.2
  24.5 16.1 %copy-start.16 = (s32[1,32]{1,0:T(1,128)S(1)}, s32[1,32]{1,0:T(1,128)}, u32[]{:S(2)}) copy-start(s32[1,32]{1,0:T(1,128)} %param.8) | copy-start | bytes 388
  24.5 43.4 %copy-start.17 = (s32[1,32]{1,0:T(1,128)S(1)}, s32[1,32]{1,0:T(1,128)}, u32[]{:S(2)}) copy-start(s32[1,32]{1,0:T(1,128)} %param.9) | copy-start | bytes 388
  24.5 46.7 %copy-start.7 = (bf16[1,32,64,128]{3,2,1,0:T(8,128)(2,1)S(1)}, bf16[1,32,64,128]{3,2,1,0:T(8,128)(2,1)}, u32[]{:S(2)}) copy-start(bf16[1,32,64,128]{3,2,1,0:T(8,128)(2,1)} %param.7) | copy-start | bytes 1572868
  24.5 46.7 %all-to-all-start = ((bf16[4,128,2048]{2,1,0:T(8,128)(2,1)}), bf16[4,128,2048]{2,1,0:T(8,128)(2,1)S(1)}, u32[]{:S(2)}, u32[]{:S(2)}) async-start(bf16[4,128,2048]{2,1,0:T(8,128)(2,1)} %copy-done.2), calls=%async_computation | async-start | bytes 4194304 | tf_op jit(solution)/shard_map/all_to_all | solution.py:296
  30.8 28.5 %collective-permute-start.2 = (bf16[32,64,128]{2,1,0:T(8,128)(2,1)S(1)}, bf16[32,64,128]{2,1,0:T(8,128)(2,1)}, u32[]{:S(2)}, u32[]{:S(2)}) collective-permute-start(bf16[32,64,128]{2,1,0:T(8,128)(2,1)S(1)} %collective-permute-done.1.refs_1_), channel_id=1, source_target_pairs={{0,1},{1,2},{2,3},{3,4},{4,5},{5,6},{6,7},{7,8},{8,9},{9,10},{10,1... | collective-permute-start | bytes 1572872 | tf_op jit(solution)/shard_map/ppermute | solution.py:314
  35.0 27.3 %collective-permute-start.9 = (bf16[32,64,128]{2,1,0:T(8,128)(2,1)}, bf16[32,64,128]{2,1,0:T(8,128)(2,1)}, u32[]{:S(2)}, u32[]{:S(2)}) collective-permute-start(bf16[32,64,128]{2,1,0:T(8,128)(2,1)} %collective-permute-done.8.refs_2_), channel_id=1, source_target_pairs={{0,15},{1,0},{2,1},{3,2},{4,3},{5,4},{6,5},{7,6},{8,7},{9,8},{10,9... | collective-permute-start | bytes 1572872 | tf_op jit(solution)/shard_map/ppermute | solution.py:316
  59.3 28.5 %collective-permute-start.3 = (bf16[32,64,128]{2,1,0:T(8,128)(2,1)}, bf16[32,64,128]{2,1,0:T(8,128)(2,1)}, u32[]{:S(2)}, u32[]{:S(2)}) collective-permute-start(bf16[32,64,128]{2,1,0:T(8,128)(2,1)} %collective-permute-done.2.refs_0_), channel_id=1, source_target_pairs={{0,1},{1,2},{2,3},{3,4},{4,5},{5,6},{6,7},{7,8},{8,9},{9,10},{10,1... | collective-permute-start | bytes 1572872 | tf_op jit(solution)/shard_map/ppermute | solution.py:314
  62.3 27.8 %collective-permute-start.10 = (bf16[32,64,128]{2,1,0:T(8,128)(2,1)}, bf16[32,64,128]{2,1,0:T(8,128)(2,1)}, u32[]{:S(2)}, u32[]{:S(2)}) collective-permute-start(bf16[32,64,128]{2,1,0:T(8,128)(2,1)} %collective-permute-done.9.refs_1_), channel_id=1, source_target_pairs={{0,15},{1,0},{2,1},{3,2},{4,3},{5,4},{6,5},{7,6},{8,7},{9,8},{10,9... | collective-permute-start | bytes 1572872 | tf_op jit(solution)/shard_map/ppermute | solution.py:316
  68.0 3.0 %collective-permute-start = (s32[128]{0:T(128)S(1)}, s32[128]{0:T(128)S(1)}, u32[]{:S(2)}, u32[]{:S(2)}) collective-permute-start(s32[128]{0:T(128)S(1)} %select_reduce_fusion.2), channel_id=1, source_target_pairs={{0,64},{64,128},{128,192},{192,256},{256,320},{320,384},{384,448},... | collective-permute-start | bytes 1544 | tf_op jit(solution)/shard_map/ppermute | solution.py:285
  73.2 52.9 %all-to-all-start.2 = ((bf16[4,2,3,2,64,128]{5,4,3,2,1,0:T(8,128)(2,1)}), bf16[4,2,3,2,64,128]{5,4,3,2,1,0:T(8,128)(2,1)}, u32[]{:S(2)}, u32[]{:S(2)}) async-start(bf16[4,2,3,2,64,128]{5,4,3,2,1,0:T(8,128)(2,1)} %shard_map.57), calls=%async_computation.2 | async-start | bytes 1572864 | tf_op jit(solution)/shard_map/all_to_all | solution.py:296
  87.8 28.1 %collective-permute-start.4 = (bf16[32,64,128]{2,1,0:T(8,128)(2,1)}, bf16[32,64,128]{2,1,0:T(8,128)(2,1)S(1)}, u32[]{:S(2)}, u32[]{:S(2)}) collective-permute-start(bf16[32,64,128]{2,1,0:T(8,128)(2,1)} %collective-permute-done.3.refs_2_), channel_id=1, source_target_pairs={{0,1},{1,2},{2,3},{3,4},{4,5},{5,6},{6,7},{7,8},{8,9},{9,10},{10,1... | collective-permute-start | bytes 1572872 | tf_op jit(solution)/shard_map/ppermute | solution.py:314
  90.1 27.8 %collective-permute-start.11 = (bf16[32,64,128]{2,1,0:T(8,128)(2,1)}, bf16[32,64,128]{2,1,0:T(8,128)(2,1)}, u32[]{:S(2)}, u32[]{:S(2)}) collective-permute-start(bf16[32,64,128]{2,1,0:T(8,128)(2,1)} %collective-permute-done.10.refs_3_), channel_id=1, source_target_pairs={{0,15},{1,0},{2,1},{3,2},{4,3},{5,4},{6,5},{7,6},{8,7},{9,8},{10,9... | collective-permute-start | bytes 1572872 | tf_op jit(solution)/shard_map/ppermute | solution.py:316
  115.9 27.7 %collective-permute-start.5 = (bf16[32,64,128]{2,1,0:T(8,128)(2,1)S(1)}, bf16[32,64,128]{2,1,0:T(8,128)(2,1)}, u32[]{:S(2)}, u32[]{:S(2)}) collective-permute-start(bf16[32,64,128]{2,1,0:T(8,128)(2,1)S(1)} %collective-permute-done.4.refs_0_), channel_id=1, source_target_pairs={{0,1},{1,2},{2,3},{3,4},{4,5},{5,6},{6,7},{7,8},{8,9},{9,10},{10,1... | collective-permute-start | bytes 1572872 | tf_op jit(solution)/shard_map/ppermute | solution.py:314
  117.9 27.7 %collective-permute-start.12 = (bf16[32,64,128]{2,1,0:T(8,128)(2,1)}, bf16[32,64,128]{2,1,0:T(8,128)(2,1)}, u32[]{:S(2)}, u32[]{:S(2)}) collective-permute-start(bf16[32,64,128]{2,1,0:T(8,128)(2,1)} %collective-permute-done.11.refs_1_), channel_id=1, source_target_pairs={{0,15},{1,0},{2,1},{3,2},{4,3},{5,4},{6,5},{7,6},{8,7},{9,8},{10,9... | collective-permute-start | bytes 1572872 | tf_op jit(solution)/shard_map/ppermute | solution.py:316
  126.1 27.7 %all-to-all-start.3 = ((bf16[4,2,4,2,64,128]{5,4,3,2,1,0:T(8,128)(2,1)}), bf16[4,2,4,2,64,128]{5,4,3,2,1,0:T(8,128)(2,1)}, u32[]{:S(2)}, u32[]{:S(2)}) async-start(bf16[4,2,4,2,64,128]{5,4,3,2,1,0:T(8,128)(2,1)} %shard_map.58), calls=%async_computation.3 | async-start | bytes 2097152 | tf_op jit(solution)/shard_map/all_to_all | solution.py:296
  131.9 19.3 %collective-permute-start.15 = (bf16[4,3,2,64,128]{4,3,2,1,0:T(8,128)(2,1)S(1)}, bf16[4,3,2,64,128]{4,3,2,1,0:T(8,128)(2,1)S(1)}, u32[]{:S(2)}, u32[]{:S(2)}) collective-permute-start(bf16[4,3,2,64,128]{4,3,2,1,0:T(8,128)(2,1)S(1)} %slice_bitcast_fusion.3), channel_id=1, source_target_pairs={{0,448},{64,0},{128,64},{192,128},{256,192},{320,256},{384,320},{4... | collective-permute-start | bytes 1179656 | tf_op jit(solution)/shard_map/ppermute | solution.py:310
  143.6 27.6 %collective-permute-start.6 = (bf16[32,64,128]{2,1,0:T(8,128)(2,1)}, bf16[32,64,128]{2,1,0:T(8,128)(2,1)S(1)}, u32[]{:S(2)}, u32[]{:S(2)}) collective-permute-start(bf16[32,64,128]{2,1,0:T(8,128)(2,1)} %collective-permute-done.5.refs_2_), channel_id=1, source_target_pairs={{0,1},{1,2},{2,3},{3,4},{4,5},{5,6},{6,7},{7,8},{8,9},{9,10},{10,1... | collective-permute-start | bytes 1572872 | tf_op jit(solution)/shard_map/ppermute | solution.py:314
  145.6 27.5 %collective-permute-start.13 = (bf16[32,64,128]{2,1,0:T(8,128)(2,1)}, bf16[32,64,128]{2,1,0:T(8,128)(2,1)}, u32[]{:S(2)}, u32[]{:S(2)}) collective-permute-start(bf16[32,64,128]{2,1,0:T(8,128)(2,1)} %collective-permute-done.12.refs_3_), channel_id=1, source_target_pairs={{0,15},{1,0},{2,1},{3,2},{4,3},{5,4},{6,5},{7,6},{8,7},{9,8},{10,9... | collective-permute-start | bytes 1572872 | tf_op jit(solution)/shard_map/ppermute | solution.py:316
  151.2 2.6 copy-start.6
  153.8 34.0 %all-to-all-start.4 = ((bf16[4,2,4,2,64,128]{5,4,3,2,1,0:T(8,128)(2,1)}), bf16[4,2,4,2,64,128]{5,4,3,2,1,0:T(8,128)(2,1)}, u32[]{:S(2)}, u32[]{:S(2)}) async-start(bf16[4,2,4,2,64,128]{5,4,3,2,1,0:T(8,128)(2,1)} %shard_map.59), calls=%async_computation.4 | async-start | bytes 2097152 | tf_op jit(solution)/shard_map/all_to_all | solution.py:296
  171.2 16.6 %collective-permute-start.7 = (bf16[32,64,128]{2,1,0:T(8,128)(2,1)S(1)}, bf16[32,64,128]{2,1,0:T(8,128)(2,1)}, u32[]{:S(2)}, u32[]{:S(2)}) collective-permute-start(bf16[32,64,128]{2,1,0:T(8,128)(2,1)S(1)} %collective-permute-done.6.refs_0_), channel_id=1, source_target_pairs={{0,1},{1,2},{2,3},{3,4},{4,5},{5,6},{6,7},{7,8},{8,9},{9,10},{10,1... | collective-permute-start | bytes 1572872 | tf_op jit(solution)/shard_map/ppermute | solution.py:314
  173.1 14.6 %collective-permute-start.14 = (bf16[32,64,128]{2,1,0:T(8,128)(2,1)}, bf16[32,64,128]{2,1,0:T(8,128)(2,1)}, u32[]{:S(2)}, u32[]{:S(2)}) collective-permute-start(bf16[32,64,128]{2,1,0:T(8,128)(2,1)} %collective-permute-done.13.refs_1_), channel_id=1, source_target_pairs={{0,15},{1,0},{2,1},{3,2},{4,3},{5,4},{6,5},{7,6},{8,7},{9,8},{10,9... | collective-permute-start | bytes 1572872 | tf_op jit(solution)/shard_map/ppermute | solution.py:316
  180.2 16.9 %collective-permute-start.16 = (bf16[4,4,2,64,128]{4,3,2,1,0:T(8,128)(2,1)}, bf16[4,4,2,64,128]{4,3,2,1,0:T(8,128)(2,1)S(1)}, u32[]{:S(2)}, u32[]{:S(2)}) collective-permute-start(bf16[4,4,2,64,128]{4,3,2,1,0:T(8,128)(2,1)} %slice_bitcast_fusion.1), channel_id=1, source_target_pairs={{0,448},{64,0},{128,64},{192,128},{256,192},{320,256},{384,320},{4... | collective-permute-start | bytes 1572872 | tf_op jit(solution)/shard_map/ppermute | solution.py:310
  180.2 3.4 %copy-start.1 = (bf16[16,32,64,128]{3,2,1,0:T(8,128)(2,1)S(1)}, bf16[16,32,64,128]{3,2,1,0:T(8,128)(2,1)}, u32[]{:S(2)}) copy-start(bf16[16,32,64,128]{3,2,1,0:T(8,128)(2,1)} %all-gather.2.cloned.1.call-done.gathered) | copy-start | bytes 25165828
  185.8 1.0 copy-start.8
  187.8 11.9 %all-to-all-start.1 = ((f32[4,128,128]{2,1,0:T(8,128)}), f32[4,128,128]{2,1,0:T(8,128)S(1)}, u32[]{:S(2)}, u32[]{:S(2)}) async-start(f32[4,128,128]{2,1,0:T(8,128)} %get-tuple-element.12), calls=%async_computation.1 | async-start | bytes 524288 | tf_op jit(solution)/shard_map/all_to_all | solution.py:296
  194.2 9.7 %collective-permute-start.18 = (bf16[4,4,2,64,128]{4,3,2,1,0:T(8,128)(2,1)}, bf16[4,4,2,64,128]{4,3,2,1,0:T(8,128)(2,1)S(1)}, u32[]{:S(2)}, u32[]{:S(2)}) collective-permute-start(bf16[4,4,2,64,128]{4,3,2,1,0:T(8,128)(2,1)} %slice_bitcast_fusion), channel_id=1, source_target_pairs={{0,448},{64,0},{128,64},{192,128},{256,192},{320,256},{384,320},{4... | collective-permute-start | bytes 1572872 | tf_op jit(solution)/shard_map/ppermute | solution.py:310
  194.9 17.0 %collective-permute-start.17 = (bf16[32,64,128]{2,1,0:T(8,128)(2,1)}, bf16[32,64,128]{2,1,0:T(8,128)(2,1)S(1)}, u32[]{:S(2)}, u32[]{:S(2)}) collective-permute-start(bf16[32,64,128]{2,1,0:T(8,128)(2,1)} %collective-permute-done.7.refs_0_), channel_id=1, source_target_pairs={{0,1},{1,2},{2,3},{3,4},{4,5},{5,6},{6,7},{7,8},{8,9},{9,10},{10,1... | collective-permute-start | bytes 1572872 | tf_op jit(solution)/shard_map/ppermute | solution.py:314
  196.8 22.1 %collective-permute-start.19 = (bf16[4,16,2,32,128]{4,3,2,1,0:T(8,128)(2,1)}, bf16[4,16,2,32,128]{4,3,2,1,0:T(8,128)(2,1)}, u32[]{:S(2)}, u32[]{:S(2)}) collective-permute-start(bf16[4,16,2,32,128]{4,3,2,1,0:T(8,128)(2,1)} %copy-done.9), channel_id=1, source_target_pairs={{0,448},{64,0},{128,64},{192,128},{256,192},{320,256},{384,320},{4... | collective-permute-start | bytes 3145736 | tf_op jit(solution)/shard_map/ppermute | solution.py:321
  197.1 16.9 %copy-start.4 = (bf16[4,4,2,64,128]{4,3,2,1,0:T(8,128)(2,1)}, bf16[4,4,2,64,128]{4,3,2,1,0:T(8,128)(2,1)S(1)}, u32[]{:S(2)}) copy-start(bf16[4,4,2,64,128]{4,3,2,1,0:T(8,128)(2,1)S(1)} %collective-permute-done.16.refs_2_.refs_3_) | copy-start | bytes 1572868
  199.7 14.3 %copy-start.3 = (f32[4,128,128]{2,1,0:T(8,128)}, f32[4,128,128]{2,1,0:T(8,128)S(1)}, u32[]{:S(2)}) copy-start(f32[4,128,128]{2,1,0:T(8,128)S(1)} %all-to-all-done.1.refs_4_.rank_ref) | copy-start | bytes 786436
  199.7 14.3 %all-to-all-start.5 = ((bf16[4,2,2,2,64,128]{5,4,3,2,1,0:T(8,128)(2,1)}), bf16[4,2,2,2,64,128]{5,4,3,2,1,0:T(8,128)(2,1)}, u32[]{:S(2)}, u32[]{:S(2)}) async-start(bf16[4,2,2,2,64,128]{5,4,3,2,1,0:T(8,128)(2,1)} %shard_map.60), calls=%async_computation.5 | async-start | bytes 1048576 | tf_op jit(solution)/shard_map/all_to_all | solution.py:296
  204.0 10.1 %copy-start.5 = (bf16[4,4,2,64,128]{4,3,2,1,0:T(8,128)(2,1)}, bf16[4,4,2,64,128]{4,3,2,1,0:T(8,128)(2,1)S(1)}, u32[]{:S(2)}) copy-start(bf16[4,4,2,64,128]{4,3,2,1,0:T(8,128)(2,1)S(1)} %collective-permute-done.18.refs_3_.refs_4_) | copy-start | bytes 1572868
  214.0 16.6 %all-to-all-start.6 = ((bf16[4,2,3,2,64,128]{5,4,3,2,1,0:T(8,128)(2,1)}), bf16[4,2,3,2,64,128]{5,4,3,2,1,0:T(8,128)(2,1)S(1)}, u32[]{:S(2)}, u32[]{:S(2)}) async-start(bf16[4,2,3,2,64,128]{5,4,3,2,1,0:T(8,128)(2,1)} %shard_map.61), calls=%async_computation.6 | async-start | bytes 1572864 | tf_op jit(solution)/shard_map/all_to_all | solution.py:296
  218.8 15.3 %collective-permute-start.20 = (bf16[4,16,2,32,128]{4,3,2,1,0:T(8,128)(2,1)}, bf16[4,16,2,32,128]{4,3,2,1,0:T(8,128)(2,1)S(1)}, u32[]{:S(2)}, u32[]{:S(2)}) collective-permute-start(bf16[4,16,2,32,128]{4,3,2,1,0:T(8,128)(2,1)} %copy-done.8), channel_id=1, source_target_pairs={{0,448},{64,0},{128,64},{192,128},{256,192},{320,256},{384,320},{4... | collective-permute-start | bytes 3145736 | tf_op jit(solution)/shard_map/ppermute | solution.py:321
  230.6 20.7 %copy-start.10 = (bf16[4,2,3,2,64,128]{5,4,3,2,1,0:T(8,128)(2,1)}, bf16[4,2,3,2,64,128]{5,4,3,2,1,0:T(8,128)(2,1)S(1)}, u32[]{:S(2)}) copy-start(bf16[4,2,3,2,64,128]{5,4,3,2,1,0:T(8,128)(2,1)S(1)} %all-to-all-done.6.refs_4_) | copy-start | bytes 2359300
  230.6 17.2 %all-to-all-start.7 = ((bf16[4,16,2,32,128]{4,3,2,1,0:T(8,128)(2,1)}), bf16[4,16,2,32,128]{4,3,2,1,0:T(8,128)(2,1)S(1)}, u32[]{:S(2)}, u32[]{:S(2)}) async-start(bf16[4,16,2,32,128]{4,3,2,1,0:T(8,128)(2,1)} %collective-permute-done.19), calls=%async_computation.7 | async-start | bytes 2097152 | tf_op jit(solution)/shard_map/all_to_all | solution.py:296
  247.8 11.2 %copy-start.11 = (bf16[4,16,2,32,128]{4,3,2,1,0:T(8,128)(2,1)}, bf16[4,16,2,32,128]{4,3,2,1,0:T(8,128)(2,1)S(1)}, u32[]{:S(2)}) copy-start(bf16[4,16,2,32,128]{4,3,2,1,0:T(8,128)(2,1)S(1)} %all-to-all-done.7.refs_0_) | copy-start | bytes 3145732
  247.8 15.9 %all-to-all-start.8 = ((bf16[4,16,2,32,128]{4,3,2,1,0:T(8,128)(2,1)}), bf16[4,16,2,32,128]{4,3,2,1,0:T(8,128)(2,1)S(1)}, u32[]{:S(2)}, u32[]{:S(2)}) async-start(bf16[4,16,2,32,128]{4,3,2,1,0:T(8,128)(2,1)} %copy-done.13), calls=%async_computation.8 | async-start | bytes 2097152 | tf_op jit(solution)/shard_map/all_to_all | solution.py:296
  251.3 8.1 %collective-permute-start.22 = (bf16[4,3,2,64,128]{4,3,2,1,0:T(8,128)(2,1)S(1)}, bf16[4,3,2,64,128]{4,3,2,1,0:T(8,128)(2,1)S(1)}, u32[]{:S(2)}, u32[]{:S(2)}) collective-permute-start(bf16[4,3,2,64,128]{4,3,2,1,0:T(8,128)(2,1)S(1)} %slice_bitcast_fusion.2), channel_id=1, source_target_pairs={{0,448},{64,0},{128,64},{192,128},{256,192},{320,256},{384,320},{4... | collective-permute-start | bytes 1179656 | tf_op jit(solution)/shard_map/ppermute | solution.py:310
  252.3 7.1 %collective-permute-start.21 = (bf16[4,2,2,64,128]{4,3,2,1,0:T(8,128)(2,1)S(1)}, bf16[4,2,2,64,128]{4,3,2,1,0:T(8,128)(2,1)S(1)}, u32[]{:S(2)}, u32[]{:S(2)}) collective-permute-start(bf16[4,2,2,64,128]{4,3,2,1,0:T(8,128)(2,1)S(1)} %slice_bitcast_fusion.4), channel_id=1, source_target_pairs={{0,448},{64,0},{128,64},{192,128},{256,192},{320,256},{384,320},{4... | collective-permute-start | bytes 786440 | tf_op jit(solution)/shard_map/ppermute | solution.py:310
  259.5 4.2 %copy-start.15 = (bf16[4,2,2,64,128]{4,3,2,1,0:T(8,128)(2,1)}, bf16[4,2,2,64,128]{4,3,2,1,0:T(8,128)(2,1)S(1)}, u32[]{:S(2)}) copy-start(bf16[4,2,2,64,128]{4,3,2,1,0:T(8,128)(2,1)S(1)} %collective-permute-done.21.refs_5_) | copy-start | bytes 786436
  259.5 4.2 %copy-start.14 = (bf16[4,3,2,64,128]{4,3,2,1,0:T(8,128)(2,1)}, bf16[4,3,2,64,128]{4,3,2,1,0:T(8,128)(2,1)S(1)}, u32[]{:S(2)}) copy-start(bf16[4,3,2,64,128]{4,3,2,1,0:T(8,128)(2,1)S(1)} %collective-permute-done.22.refs_6_) | copy-start | bytes 1179652
  (3 other events, 2.9 us)
Sparse Core Ops, SparseCore 0:
  9.4 168.1 all-gather.1

commit v4 on v3

--- a/solution.py
+++ b/solution.py
@@ -321,7 +321,7 @@
     halves = [lax.ppermute(half, SEGMENT, back) for half in halves]
     rank = over_y(after(partial, chunks[7], chunks[9]))
     halves = [over_y(after(halves[0], rank)), over_y(after(halves[1], chunks[8]))]
-    send_on(second[2], rank)
+    send_on(second[2])
     z = z.astype(jnp.int32)[None]
     smem, vmem = (pl.BlockSpec(memory_space=m) for m in (pltpu.SMEM, pltpu.VMEM))
     state = layer_call(

time: 280 us -> 282 us (level)
  waiting for transfers between devices: 120 us -> 124 us
    ppermute x7, waiting for transfers between devices: 3.81 us -> 25.2 us  [shards(): chunks[Z - step] = lax.ppermute(chunks[(Z + 1 - step) % Z], 'z', low)]
    ppermute x8, waiting for transfers between devices: 82.5 us -> 65.2 us  [shards(): chunks[step] = lax.ppermute(chunks[step - 1], 'z', up)]
    unnamed x36 -> x38, local copies, waits for them, and re-layouts: 10.2 us -> 10 us
where the time goes in v4:
time: 282 us; the launch traced here: 280 us
  waiting for transfers between devices  124 us (44%)
  starting transfers between devices  102 us (36%)
  Pallas kernels  25.2 us (9%)
  local copies, waits for them, and re-layouts  15.3 us (5%)
  between operations  13.8 us (5%)
    ppermute x8, waiting for transfers between devices, shards(): chunks[step] = lax.ppermute(chunks[step - 1], 'z', up)  65.2 us
    ppermute x7, starting transfers between devices, shards(): chunks[Z - step] = lax.ppermute(chunks[(Z + 1 - step) % Z], 'z', low)  42.9 us
    all_to_all x9, starting transfers between devices, over_y(): return lax.all_to_all(x, 'y', split_axis=0, concat_axis=0, tiled=True)  40.4 us
    all_to_all x9, waiting for transfers between devices, over_y(): return lax.all_to_all(x, 'y', split_axis=0, concat_axis=0, tiled=True)  31.4 us
    ppermute x7, waiting for transfers between devices, shards(): chunks[Z - step] = lax.ppermute(chunks[(Z + 1 - step) % Z], 'z', low)  25.2 us
    ppermute x8, starting transfers between devices, shards(): chunks[step] = lax.ppermute(chunks[step - 1], 'z', up)  17.2 us
    pallas_call x5, Pallas kernels, pick(): pl.pallas_call(functools.partial(pick_kernel, count), out_shape=jax.Shape...  11 us
    pallas_call x2, Pallas kernels, layer_call(): pl.pallas_call(kernel, out_shape=jax.ShapeDtypeStruct((ROWS, WIDTH), jnp....  10.7 us
  transfers between devices with their start and end apart: 33, of which 17 were waited for; matrix products, arithmetic and copies ran while one was open for 2% of the time, Pallas kernels for 7%

profile of v4, /device:TPU:6, one launch (start us, length us, event | category | flops | bytes accessed | tf_op | source)
XLA Modules:
  0.0 280.4 jit_solution(1751234517317844764)
XLA Ops:
  11.2 4.6 %all-to-all-start = ((bf16[4,128,2048]{2,1,0:T(8,128)(2,1)}), bf16[4,128,2048]{2,1,0:T(8,128)(2,1)S(1)}, u32[]{:S(2)}, u32[]{:S(2)}) async-start(bf16[4,128,2048]{2,1,0:T(8,128)(2,1)} %copy-done.2), calls=%async_computation | async-start | bytes 4194304 | tf_op jit(solution)/shard_map/all_to_all | solution.py:296
  15.8 3.8 %collective-permute-start.1 = (bf16[32,64,128]{2,1,0:T(8,128)(2,1)S(1)}, bf16[32,64,128]{2,1,0:T(8,128)(2,1)S(1)}, u32[]{:S(2)}, u32[]{:S(2)}) collective-permute-start(bf16[32,64,128]{2,1,0:T(8,128)(2,1)S(1)} %bitcast.34), channel_id=1, source_target_pairs={{0,1},{1,2},{2,3},{3,4},{4,5},{5,6},{6,7},{7,8},{8,9},{9,10},{10,1... | collective-permute-start | bytes 1572872 | tf_op jit(solution)/shard_map/ppermute | solution.py:314
  19.6 9.5 %collective-permute-start.8 = (bf16[32,64,128]{2,1,0:T(8,128)(2,1)S(1)}, bf16[32,64,128]{2,1,0:T(8,128)(2,1)}, u32[]{:S(2)}, u32[]{:S(2)}) collective-permute-start(bf16[32,64,128]{2,1,0:T(8,128)(2,1)S(1)} %bitcast.35), channel_id=1, source_target_pairs={{0,15},{1,0},{2,1},{3,2},{4,3},{5,4},{6,5},{7,6},{8,7},{9,8},{10,9... | collective-permute-start | bytes 1572872 | tf_op jit(solution)/shard_map/ppermute | solution.py:316
  29.1 14.9 %collective-permute-done.1.refs_1_ = bf16[32,64,128]{2,1,0:T(8,128)(2,1)S(1)} collective-permute-done((bf16[32,64,128]{2,1,0:T(8,128)(2,1)S(1)}, bf16[32,64,128]{2,1,0:T(8,128)(2,1)S(1)}, u32[]{:S(2)}, u32[]{:S(2)}) %collective-permute-start.1) | collective-permute-done | bytes 524320 | tf_op jit(solution)/shard_map/ppermute | solution.py:314
  44.0 1.9 collective-permute-start.2
  45.9 5.3 %collective-permute-done.8.refs_2_ = bf16[32,64,128]{2,1,0:T(8,128)(2,1)} collective-permute-done((bf16[32,64,128]{2,1,0:T(8,128)(2,1)S(1)}, bf16[32,64,128]{2,1,0:T(8,128)(2,1)}, u32[]{:S(2)}, u32[]{:S(2)}) %collective-permute-start.8) | collective-permute-done | bytes 524320 | tf_op jit(solution)/shard_map/ppermute | solution.py:316
  51.2 5.7 %collective-permute-start.9 = (bf16[32,64,128]{2,1,0:T(8,128)(2,1)}, bf16[32,64,128]{2,1,0:T(8,128)(2,1)}, u32[]{:S(2)}, u32[]{:S(2)}) collective-permute-start(bf16[32,64,128]{2,1,0:T(8,128)(2,1)} %collective-permute-done.8.refs_2_), channel_id=1, source_target_pairs={{0,15},{1,0},{2,1},{3,2},{4,3},{5,4},{6,5},{7,6},{8,7},{9,8},{10,9... | collective-permute-start | bytes 1572872 | tf_op jit(solution)/shard_map/ppermute | solution.py:316
  57.1 14.7 %collective-permute-done.2.refs_0_ = bf16[32,64,128]{2,1,0:T(8,128)(2,1)} collective-permute-done((bf16[32,64,128]{2,1,0:T(8,128)(2,1)S(1)}, bf16[32,64,128]{2,1,0:T(8,128)(2,1)}, u32[]{:S(2)}, u32[]{:S(2)}) %collective-permute-start.2) | collective-permute-done | bytes 524320 | tf_op jit(solution)/shard_map/ppermute | solution.py:314
  71.8 1.9 collective-permute-start.3
  73.7 5.3 %collective-permute-done.9.refs_1_ = bf16[32,64,128]{2,1,0:T(8,128)(2,1)} collective-permute-done((bf16[32,64,128]{2,1,0:T(8,128)(2,1)}, bf16[32,64,128]{2,1,0:T(8,128)(2,1)}, u32[]{:S(2)}, u32[]{:S(2)}) %collective-permute-start.9) | collective-permute-done | bytes 524320 | tf_op jit(solution)/shard_map/ppermute | solution.py:316
  79.0 5.6 %collective-permute-start.10 = (bf16[32,64,128]{2,1,0:T(8,128)(2,1)}, bf16[32,64,128]{2,1,0:T(8,128)(2,1)}, u32[]{:S(2)}, u32[]{:S(2)}) collective-permute-start(bf16[32,64,128]{2,1,0:T(8,128)(2,1)} %collective-permute-done.9.refs_1_), channel_id=1, source_target_pairs={{0,15},{1,0},{2,1},{3,2},{4,3},{5,4},{6,5},{7,6},{8,7},{9,8},{10,9... | collective-permute-start | bytes 1572872 | tf_op jit(solution)/shard_map/ppermute | solution.py:316
  85.1 2.0 shard_map.57
  87.0 4.8 %all-to-all-start.2 = ((bf16[4,2,3,2,64,128]{5,4,3,2,1,0:T(8,128)(2,1)}), bf16[4,2,3,2,64,128]{5,4,3,2,1,0:T(8,128)(2,1)}, u32[]{:S(2)}, u32[]{:S(2)}) async-start(bf16[4,2,3,2,64,128]{5,4,3,2,1,0:T(8,128)(2,1)} %shard_map.57), calls=%async_computation.2 | async-start | bytes 1572864 | tf_op jit(solution)/shard_map/all_to_all | solution.py:296
  91.8 7.7 %collective-permute-done.3.refs_2_ = bf16[32,64,128]{2,1,0:T(8,128)(2,1)} collective-permute-done((bf16[32,64,128]{2,1,0:T(8,128)(2,1)}, bf16[32,64,128]{2,1,0:T(8,128)(2,1)}, u32[]{:S(2)}, u32[]{:S(2)}) %collective-permute-start.3) | collective-permute-done | bytes 524320 | tf_op jit(solution)/shard_map/ppermute | solution.py:314
  99.5 1.9 collective-permute-start.4
  101.4 5.0 %collective-permute-done.10.refs_3_ = bf16[32,64,128]{2,1,0:T(8,128)(2,1)} collective-permute-done((bf16[32,64,128]{2,1,0:T(8,128)(2,1)}, bf16[32,64,128]{2,1,0:T(8,128)(2,1)}, u32[]{:S(2)}, u32[]{:S(2)}) %collective-permute-start.10) | collective-permute-done | bytes 524320 | tf_op jit(solution)/shard_map/ppermute | solution.py:316
  106.5 5.6 %collective-permute-start.11 = (bf16[32,64,128]{2,1,0:T(8,128)(2,1)}, bf16[32,64,128]{2,1,0:T(8,128)(2,1)S(1)}, u32[]{:S(2)}, u32[]{:S(2)}) collective-permute-start(bf16[32,64,128]{2,1,0:T(8,128)(2,1)} %collective-permute-done.10.refs_3_), channel_id=1, source_target_pairs={{0,15},{1,0},{2,1},{3,2},{4,3},{5,4},{6,5},{7,6},{8,7},{9,8},{10,9... | collective-permute-start | bytes 1572872 | tf_op jit(solution)/shard_map/ppermute | solution.py:316
  112.1 2.6 shard_map.58
  114.6 5.0 %all-to-all-start.3 = ((bf16[4,2,4,2,64,128]{5,4,3,2,1,0:T(8,128)(2,1)}), bf16[4,2,4,2,64,128]{5,4,3,2,1,0:T(8,128)(2,1)}, u32[]{:S(2)}, u32[]{:S(2)}) async-start(bf16[4,2,4,2,64,128]{5,4,3,2,1,0:T(8,128)(2,1)} %shard_map.58), calls=%async_computation.3 | async-start | bytes 2097152 | tf_op jit(solution)/shard_map/all_to_all | solution.py:296
  119.7 7.2 %collective-permute-done.4.refs_0_ = bf16[32,64,128]{2,1,0:T(8,128)(2,1)S(1)} collective-permute-done((bf16[32,64,128]{2,1,0:T(8,128)(2,1)}, bf16[32,64,128]{2,1,0:T(8,128)(2,1)S(1)}, u32[]{:S(2)}, u32[]{:S(2)}) %collective-permute-start.4) | collective-permute-done | bytes 524320 | tf_op jit(solution)/shard_map/ppermute | solution.py:314
  126.8 1.9 collective-permute-start.5
  128.8 5.1 %collective-permute-done.11.refs_1_ = bf16[32,64,128]{2,1,0:T(8,128)(2,1)S(1)} collective-permute-done((bf16[32,64,128]{2,1,0:T(8,128)(2,1)}, bf16[32,64,128]{2,1,0:T(8,128)(2,1)S(1)}, u32[]{:S(2)}, u32[]{:S(2)}) %collective-permute-start.11) | collective-permute-done | bytes 524320 | tf_op jit(solution)/shard_map/ppermute | solution.py:316
  133.9 5.5 %collective-permute-start.12 = (bf16[32,64,128]{2,1,0:T(8,128)(2,1)S(1)}, bf16[32,64,128]{2,1,0:T(8,128)(2,1)S(1)}, u32[]{:S(2)}, u32[]{:S(2)}) collective-permute-start(bf16[32,64,128]{2,1,0:T(8,128)(2,1)S(1)} %collective-permute-done.11.refs_1_), channel_id=1, source_target_pairs={{0,15},{1,0},{2,1},{3,2},{4,3},{5,4},{6,5},{7,6},{8,7},{9,8},{10,9... | collective-permute-start | bytes 1572872 | tf_op jit(solution)/shard_map/ppermute | solution.py:316
  140.4 13.6 %collective-permute-done.5.refs_2_ = bf16[32,64,128]{2,1,0:T(8,128)(2,1)} collective-permute-done((bf16[32,64,128]{2,1,0:T(8,128)(2,1)S(1)}, bf16[32,64,128]{2,1,0:T(8,128)(2,1)}, u32[]{:S(2)}, u32[]{:S(2)}) %collective-permute-start.5) | collective-permute-done | bytes 524320 | tf_op jit(solution)/shard_map/ppermute | solution.py:314
  154.0 1.9 collective-permute-start.6
  155.9 4.4 %collective-permute-done.12.refs_3_ = bf16[32,64,128]{2,1,0:T(8,128)(2,1)S(1)} collective-permute-done((bf16[32,64,128]{2,1,0:T(8,128)(2,1)S(1)}, bf16[32,64,128]{2,1,0:T(8,128)(2,1)S(1)}, u32[]{:S(2)}, u32[]{:S(2)}) %collective-permute-start.12) | collective-permute-done | bytes 524320 | tf_op jit(solution)/shard_map/ppermute | solution.py:316
  160.4 2.1 shard_map.59
  163.3 5.5 %all-to-all-start.4 = ((bf16[4,2,4,2,64,128]{5,4,3,2,1,0:T(8,128)(2,1)}), bf16[4,2,4,2,64,128]{5,4,3,2,1,0:T(8,128)(2,1)}, u32[]{:S(2)}, u32[]{:S(2)}) async-start(bf16[4,2,4,2,64,128]{5,4,3,2,1,0:T(8,128)(2,1)} %shard_map.59), calls=%async_computation.4 | async-start | bytes 2097152 | tf_op jit(solution)/shard_map/all_to_all | solution.py:296
  168.7 5.6 %collective-permute-start.13 = (bf16[32,64,128]{2,1,0:T(8,128)(2,1)S(1)}, bf16[32,64,128]{2,1,0:T(8,128)(2,1)}, u32[]{:S(2)}, u32[]{:S(2)}) collective-permute-start(bf16[32,64,128]{2,1,0:T(8,128)(2,1)S(1)} %copy-done.8), channel_id=1, source_target_pairs={{0,15},{1,0},{2,1},{3,2},{4,3},{5,4},{6,5},{7,6},{8,7},{9,8},{10,9... | collective-permute-start | bytes 1572872 | tf_op jit(solution)/shard_map/ppermute | solution.py:316
  175.4 3.9 %collective-permute-done.6.refs_0_ = bf16[32,64,128]{2,1,0:T(8,128)(2,1)} collective-permute-done((bf16[32,64,128]{2,1,0:T(8,128)(2,1)}, bf16[32,64,128]{2,1,0:T(8,128)(2,1)}, u32[]{:S(2)}, u32[]{:S(2)}) %collective-permute-start.6) | collective-permute-done | bytes 524320 | tf_op jit(solution)/shard_map/ppermute | solution.py:314
  179.3 1.9 collective-permute-start.7
  181.3 5.5 %collective-permute-start.14 = (bf16[32,64,128]{2,1,0:T(8,128)(2,1)}, bf16[32,64,128]{2,1,0:T(8,128)(2,1)}, u32[]{:S(2)}, u32[]{:S(2)}) collective-permute-start(bf16[32,64,128]{2,1,0:T(8,128)(2,1)} %collective-permute-done.13.refs_1_), channel_id=1, source_target_pairs={{0,15},{1,0},{2,1},{3,2},{4,3},{5,4},{6,5},{7,6},{8,7},{9,8},{10,9... | collective-permute-start | bytes 1572872 | tf_op jit(solution)/shard_map/ppermute | solution.py:316
  186.8 2.2 shard_map.60
  189.0 5.1 %all-to-all-start.5 = ((bf16[4,2,2,2,64,128]{5,4,3,2,1,0:T(8,128)(2,1)}), bf16[4,2,2,2,64,128]{5,4,3,2,1,0:T(8,128)(2,1)}, u32[]{:S(2)}, u32[]{:S(2)}) async-start(bf16[4,2,2,2,64,128]{5,4,3,2,1,0:T(8,128)(2,1)} %shard_map.60), calls=%async_computation.5 | async-start | bytes 1048576 | tf_op jit(solution)/shard_map/all_to_all | solution.py:296
  196.1 1.9 collective-permute-start.17
  198.0 3.4 %copy-done.1 = bf16[16,32,64,128]{3,2,1,0:T(8,128)(2,1)S(1)} copy-done((bf16[16,32,64,128]{3,2,1,0:T(8,128)(2,1)S(1)}, bf16[16,32,64,128]{3,2,1,0:T(8,128)(2,1)}, u32[]{:S(2)}) %copy-start.1) | copy-done | bytes 8388632
  201.4 2.4 shard_map.56
  205.6 4.8 %all-to-all-start.1 = ((f32[4,128,128]{2,1,0:T(8,128)}), f32[4,128,128]{2,1,0:T(8,128)S(1)}, u32[]{:S(2)}, u32[]{:S(2)}) async-start(f32[4,128,128]{2,1,0:T(8,128)} %get-tuple-element.12), calls=%async_computation.1 | async-start | bytes 524288 | tf_op jit(solution)/shard_map/all_to_all | solution.py:296
  210.4 3.3 %collective-permute-done.17.refs_2_ = bf16[32,64,128]{2,1,0:T(8,128)(2,1)S(1)} collective-permute-done((bf16[32,64,128]{2,1,0:T(8,128)(2,1)}, bf16[32,64,128]{2,1,0:T(8,128)(2,1)S(1)}, u32[]{:S(2)}, u32[]{:S(2)}) %collective-permute-start.17) | collective-permute-done | bytes 524320 | tf_op jit(solution)/shard_map/ppermute | solution.py:314
  213.7 2.1 shard_map.61
  217.1 3.6 %all-to-all-start.6 = ((bf16[4,2,3,2,64,128]{5,4,3,2,1,0:T(8,128)(2,1)}), bf16[4,2,3,2,64,128]{5,4,3,2,1,0:T(8,128)(2,1)S(1)}, u32[]{:S(2)}, u32[]{:S(2)}) async-start(bf16[4,2,3,2,64,128]{5,4,3,2,1,0:T(8,128)(2,1)} %shard_map.61), calls=%async_computation.6 | async-start | bytes 1572864 | tf_op jit(solution)/shard_map/all_to_all | solution.py:296
  220.7 12.2 %all-to-all-done.6.refs_4_ = bf16[4,2,3,2,64,128]{5,4,3,2,1,0:T(8,128)(2,1)S(1)} async-done(((bf16[4,2,3,2,64,128]{5,4,3,2,1,0:T(8,128)(2,1)}), bf16[4,2,3,2,64,128]{5,4,3,2,1,0:T(8,128)(2,1)S(1)}, u32[]{:S(2)}, u32[]{:S(2)}) %all-to-all-start.6) | async-done | bytes 786464 | tf_op jit(solution)/shard_map/all_to_all | solution.py:296
  232.8 3.5 %all-to-all-start.7 = ((bf16[4,16,2,32,128]{4,3,2,1,0:T(8,128)(2,1)}), bf16[4,16,2,32,128]{4,3,2,1,0:T(8,128)(2,1)S(1)}, u32[]{:S(2)}, u32[]{:S(2)}) async-start(bf16[4,16,2,32,128]{4,3,2,1,0:T(8,128)(2,1)} %collective-permute-done.19), calls=%async_computation.7 | async-start | bytes 2097152 | tf_op jit(solution)/shard_map/all_to_all | solution.py:296
  237.3 13.0 %all-to-all-done.7.refs_0_ = bf16[4,16,2,32,128]{4,3,2,1,0:T(8,128)(2,1)S(1)} async-done(((bf16[4,16,2,32,128]{4,3,2,1,0:T(8,128)(2,1)}), bf16[4,16,2,32,128]{4,3,2,1,0:T(8,128)(2,1)S(1)}, u32[]{:S(2)}, u32[]{:S(2)}) %all-to-all-start.7) | async-done | bytes 1048608 | tf_op jit(solution)/shard_map/all_to_all | solution.py:296
  250.4 3.5 %all-to-all-start.8 = ((bf16[4,16,2,32,128]{4,3,2,1,0:T(8,128)(2,1)}), bf16[4,16,2,32,128]{4,3,2,1,0:T(8,128)(2,1)S(1)}, u32[]{:S(2)}, u32[]{:S(2)}) async-start(bf16[4,16,2,32,128]{4,3,2,1,0:T(8,128)(2,1)} %copy-done.14), calls=%async_computation.8 | async-start | bytes 2097152 | tf_op jit(solution)/shard_map/all_to_all | solution.py:296
  255.7 5.1 %shard_map.62.state_hbm = bf16[128,8192]{1,0:T(8,128)(2,1)} custom-call(s32[1]{0:T(128)} %bitcast.z_ref, f32[4,128,128]{2,1,0:T(8,128)} %copy-done.13, bf16[128,8192]{1,0:T(8,128)(2,1)} %bitcast.32, bf16[4,2,3,2,64,128]{5,4,3,2,1,0:T(8,128)(2,1)} %all-to-all-done.2.refs_0_, bf16[4,2,4,2,64,128]{5,4,3,2,1,0:T(8,128)(2,1)} %all-to-all-done.3.refs_1_, ...), custom_call_target="tpu_custom_call" | custom-call | flops 536870912 | bytes 6291456 | tf_op jit(solution)/shard_map/pallas_call | solution.py:263
  262.1 4.9 %all-to-all-done.8.refs_1_ = bf16[4,16,2,32,128]{4,3,2,1,0:T(8,128)(2,1)S(1)} async-done(((bf16[4,16,2,32,128]{4,3,2,1,0:T(8,128)(2,1)}), bf16[4,16,2,32,128]{4,3,2,1,0:T(8,128)(2,1)S(1)}, u32[]{:S(2)}, u32[]{:S(2)}) %all-to-all-start.8) | async-done | bytes 1048608 | tf_op jit(solution)/shard_map/all_to_all | solution.py:296
  268.0 5.6 %shard_map.63 = bf16[128,8192]{1,0:T(8,128)(2,1)} custom-call(s32[1]{0:T(128)} %bitcast.z_ref, bf16[128,8192]{1,0:T(8,128)(2,1)} %shard_map.62.state_hbm, bf16[4,16,2,32,128]{4,3,2,1,0:T(8,128)(2,1)} %copy-done.11, bf16[4,16,2,32,128]{4,3,2,1,0:T(8,128)(2,1)} %copy-done.12, bf16[4,3,2,64,128]{4,3,2,1,0:T(8,128)(2,1)} %copy-done.5, ...), custom_call_target="tpu_custom_call" | custom-call | flops 536870912 | bytes 6291456 | tf_op jit(solution)/shard_map/pallas_call | solution.py:263
  (80 shorter events, 18.0 us)
Async XLA Ops:
  6.5 191.5 %all-gather.2.cloned.1.call-start = ((), (), s32[]{:S(2)}) async-start(), calls=%async_computation.9 | async-start | bytes 8912896 | tf_op jit(solution)/shard_map/all_gather | solution.py:298
  7.3 1.6 copy-start
  9.8 1.3 copy-start.2
  11.2 4.6 %copy-start.6 = (bf16[1,32,64,128]{3,2,1,0:T(8,128)(2,1)S(1)}, bf16[1,32,64,128]{3,2,1,0:T(8,128)(2,1)}, u32[]{:S(2)}) copy-start(bf16[1,32,64,128]{3,2,1,0:T(8,128)(2,1)} %param.7) | copy-start | bytes 1572868
  11.2 45.8 %copy-start.17 = (s32[1,32]{1,0:T(1,128)S(1)}, s32[1,32]{1,0:T(1,128)}, u32[]{:S(2)}) copy-start(s32[1,32]{1,0:T(1,128)} %param.8) | copy-start | bytes 388
  11.2 45.9 %copy-start.18 = (s32[1,32]{1,0:T(1,128)S(1)}, s32[1,32]{1,0:T(1,128)}, u32[]{:S(2)}) copy-start(s32[1,32]{1,0:T(1,128)} %param.9) | copy-start | bytes 388
  11.2 73.9 %all-to-all-start = ((bf16[4,128,2048]{2,1,0:T(8,128)(2,1)}), bf16[4,128,2048]{2,1,0:T(8,128)(2,1)S(1)}, u32[]{:S(2)}, u32[]{:S(2)}) async-start(bf16[4,128,2048]{2,1,0:T(8,128)(2,1)} %copy-done.2), calls=%async_computation | async-start | bytes 4194304 | tf_op jit(solution)/shard_map/all_to_all | solution.py:296
  15.8 28.2 %collective-permute-start.1 = (bf16[32,64,128]{2,1,0:T(8,128)(2,1)S(1)}, bf16[32,64,128]{2,1,0:T(8,128)(2,1)S(1)}, u32[]{:S(2)}, u32[]{:S(2)}) collective-permute-start(bf16[32,64,128]{2,1,0:T(8,128)(2,1)S(1)} %bitcast.34), channel_id=1, source_target_pairs={{0,1},{1,2},{2,3},{3,4},{4,5},{5,6},{6,7},{7,8},{8,9},{9,10},{10,1... | collective-permute-start | bytes 1572872 | tf_op jit(solution)/shard_map/ppermute | solution.py:314
  19.6 31.6 %collective-permute-start.8 = (bf16[32,64,128]{2,1,0:T(8,128)(2,1)S(1)}, bf16[32,64,128]{2,1,0:T(8,128)(2,1)}, u32[]{:S(2)}, u32[]{:S(2)}) collective-permute-start(bf16[32,64,128]{2,1,0:T(8,128)(2,1)S(1)} %bitcast.35), channel_id=1, source_target_pairs={{0,15},{1,0},{2,1},{3,2},{4,3},{5,4},{6,5},{7,6},{8,7},{9,8},{10,9... | collective-permute-start | bytes 1572872 | tf_op jit(solution)/shard_map/ppermute | solution.py:316
  44.0 27.8 %collective-permute-start.2 = (bf16[32,64,128]{2,1,0:T(8,128)(2,1)S(1)}, bf16[32,64,128]{2,1,0:T(8,128)(2,1)}, u32[]{:S(2)}, u32[]{:S(2)}) collective-permute-start(bf16[32,64,128]{2,1,0:T(8,128)(2,1)S(1)} %collective-permute-done.1.refs_1_), channel_id=1, source_target_pairs={{0,1},{1,2},{2,3},{3,4},{4,5},{5,6},{6,7},{7,8},{8,9},{9,10},{10,1... | collective-permute-start | bytes 1572872 | tf_op jit(solution)/shard_map/ppermute | solution.py:314
  51.2 27.8 %collective-permute-start.9 = (bf16[32,64,128]{2,1,0:T(8,128)(2,1)}, bf16[32,64,128]{2,1,0:T(8,128)(2,1)}, u32[]{:S(2)}, u32[]{:S(2)}) collective-permute-start(bf16[32,64,128]{2,1,0:T(8,128)(2,1)} %collective-permute-done.8.refs_2_), channel_id=1, source_target_pairs={{0,15},{1,0},{2,1},{3,2},{4,3},{5,4},{6,5},{7,6},{8,7},{9,8},{10,9... | collective-permute-start | bytes 1572872 | tf_op jit(solution)/shard_map/ppermute | solution.py:316
  57.1 27.7 %collective-permute-start = (s32[128]{0:T(128)S(1)}, s32[128]{0:T(128)S(1)}, u32[]{:S(2)}, u32[]{:S(2)}) collective-permute-start(s32[128]{0:T(128)S(1)} %select_reduce_fusion.2), channel_id=1, source_target_pairs={{0,64},{64,128},{128,192},{192,256},{256,320},{320,384},{384,448},... | collective-permute-start | bytes 1544 | tf_op jit(solution)/shard_map/ppermute | solution.py:285
  71.8 27.7 %collective-permute-start.3 = (bf16[32,64,128]{2,1,0:T(8,128)(2,1)}, bf16[32,64,128]{2,1,0:T(8,128)(2,1)}, u32[]{:S(2)}, u32[]{:S(2)}) collective-permute-start(bf16[32,64,128]{2,1,0:T(8,128)(2,1)} %collective-permute-done.2.refs_0_), channel_id=1, source_target_pairs={{0,1},{1,2},{2,3},{3,4},{4,5},{5,6},{6,7},{7,8},{8,9},{9,10},{10,1... | collective-permute-start | bytes 1572872 | tf_op jit(solution)/shard_map/ppermute | solution.py:314
  79.0 27.4 %collective-permute-start.10 = (bf16[32,64,128]{2,1,0:T(8,128)(2,1)}, bf16[32,64,128]{2,1,0:T(8,128)(2,1)}, u32[]{:S(2)}, u32[]{:S(2)}) collective-permute-start(bf16[32,64,128]{2,1,0:T(8,128)(2,1)} %collective-permute-done.9.refs_1_), channel_id=1, source_target_pairs={{0,15},{1,0},{2,1},{3,2},{4,3},{5,4},{6,5},{7,6},{8,7},{9,8},{10,9... | collective-permute-start | bytes 1572872 | tf_op jit(solution)/shard_map/ppermute | solution.py:316
  87.0 27.6 %all-to-all-start.2 = ((bf16[4,2,3,2,64,128]{5,4,3,2,1,0:T(8,128)(2,1)}), bf16[4,2,3,2,64,128]{5,4,3,2,1,0:T(8,128)(2,1)}, u32[]{:S(2)}, u32[]{:S(2)}) async-start(bf16[4,2,3,2,64,128]{5,4,3,2,1,0:T(8,128)(2,1)} %shard_map.57), calls=%async_computation.2 | async-start | bytes 1572864 | tf_op jit(solution)/shard_map/all_to_all | solution.py:296
  99.5 27.3 %collective-permute-start.4 = (bf16[32,64,128]{2,1,0:T(8,128)(2,1)}, bf16[32,64,128]{2,1,0:T(8,128)(2,1)S(1)}, u32[]{:S(2)}, u32[]{:S(2)}) collective-permute-start(bf16[32,64,128]{2,1,0:T(8,128)(2,1)} %collective-permute-done.3.refs_2_), channel_id=1, source_target_pairs={{0,1},{1,2},{2,3},{3,4},{4,5},{5,6},{6,7},{7,8},{8,9},{9,10},{10,1... | collective-permute-start | bytes 1572872 | tf_op jit(solution)/shard_map/ppermute | solution.py:314
  106.5 27.4 %collective-permute-start.11 = (bf16[32,64,128]{2,1,0:T(8,128)(2,1)}, bf16[32,64,128]{2,1,0:T(8,128)(2,1)S(1)}, u32[]{:S(2)}, u32[]{:S(2)}) collective-permute-start(bf16[32,64,128]{2,1,0:T(8,128)(2,1)} %collective-permute-done.10.refs_3_), channel_id=1, source_target_pairs={{0,15},{1,0},{2,1},{3,2},{4,3},{5,4},{6,5},{7,6},{8,7},{9,8},{10,9... | collective-permute-start | bytes 1572872 | tf_op jit(solution)/shard_map/ppermute | solution.py:316
  114.6 48.6 %all-to-all-start.3 = ((bf16[4,2,4,2,64,128]{5,4,3,2,1,0:T(8,128)(2,1)}), bf16[4,2,4,2,64,128]{5,4,3,2,1,0:T(8,128)(2,1)}, u32[]{:S(2)}, u32[]{:S(2)}) async-start(bf16[4,2,4,2,64,128]{5,4,3,2,1,0:T(8,128)(2,1)} %shard_map.58), calls=%async_computation.3 | async-start | bytes 2097152 | tf_op jit(solution)/shard_map/all_to_all | solution.py:296
  126.8 27.2 %collective-permute-start.5 = (bf16[32,64,128]{2,1,0:T(8,128)(2,1)S(1)}, bf16[32,64,128]{2,1,0:T(8,128)(2,1)}, u32[]{:S(2)}, u32[]{:S(2)}) collective-permute-start(bf16[32,64,128]{2,1,0:T(8,128)(2,1)S(1)} %collective-permute-done.4.refs_0_), channel_id=1, source_target_pairs={{0,1},{1,2},{2,3},{3,4},{4,5},{5,6},{6,7},{7,8},{8,9},{9,10},{10,1... | collective-permute-start | bytes 1572872 | tf_op jit(solution)/shard_map/ppermute | solution.py:314
  133.9 26.5 %collective-permute-start.12 = (bf16[32,64,128]{2,1,0:T(8,128)(2,1)S(1)}, bf16[32,64,128]{2,1,0:T(8,128)(2,1)S(1)}, u32[]{:S(2)}, u32[]{:S(2)}) collective-permute-start(bf16[32,64,128]{2,1,0:T(8,128)(2,1)S(1)} %collective-permute-done.11.refs_1_), channel_id=1, source_target_pairs={{0,15},{1,0},{2,1},{3,2},{4,3},{5,4},{6,5},{7,6},{8,7},{9,8},{10,9... | collective-permute-start | bytes 1572872 | tf_op jit(solution)/shard_map/ppermute | solution.py:316
  140.4 15.5 %collective-permute-start.15 = (bf16[4,3,2,64,128]{4,3,2,1,0:T(8,128)(2,1)S(1)}, bf16[4,3,2,64,128]{4,3,2,1,0:T(8,128)(2,1)S(1)}, u32[]{:S(2)}, u32[]{:S(2)}) collective-permute-start(bf16[4,3,2,64,128]{4,3,2,1,0:T(8,128)(2,1)S(1)} %slice_bitcast_fusion.3), channel_id=1, source_target_pairs={{0,448},{64,0},{128,64},{192,128},{256,192},{320,256},{384,320},{4... | collective-permute-start | bytes 1179656 | tf_op jit(solution)/shard_map/ppermute | solution.py:310
  154.0 25.3 %collective-permute-start.6 = (bf16[32,64,128]{2,1,0:T(8,128)(2,1)}, bf16[32,64,128]{2,1,0:T(8,128)(2,1)}, u32[]{:S(2)}, u32[]{:S(2)}) collective-permute-start(bf16[32,64,128]{2,1,0:T(8,128)(2,1)} %collective-permute-done.5.refs_2_), channel_id=1, source_target_pairs={{0,1},{1,2},{2,3},{3,4},{4,5},{5,6},{6,7},{7,8},{8,9},{9,10},{10,1... | collective-permute-start | bytes 1572872 | tf_op jit(solution)/shard_map/ppermute | solution.py:314
  155.9 7.3 %copy-start.5 = (bf16[4,3,2,64,128]{4,3,2,1,0:T(8,128)(2,1)}, bf16[4,3,2,64,128]{4,3,2,1,0:T(8,128)(2,1)S(1)}, u32[]{:S(2)}) copy-start(bf16[4,3,2,64,128]{4,3,2,1,0:T(8,128)(2,1)S(1)} %collective-permute-done.15.refs_4_.refs_2_) | copy-start | bytes 1179652
  163.3 5.5 %copy-start.8 = (bf16[32,64,128]{2,1,0:T(8,128)(2,1)S(1)}, bf16[32,64,128]{2,1,0:T(8,128)(2,1)}, u32[]{:S(2)}) copy-start(bf16[32,64,128]{2,1,0:T(8,128)(2,1)} %copy-done.7) | copy-start | bytes 1572868
  163.3 25.8 %all-to-all-start.4 = ((bf16[4,2,4,2,64,128]{5,4,3,2,1,0:T(8,128)(2,1)}), bf16[4,2,4,2,64,128]{5,4,3,2,1,0:T(8,128)(2,1)}, u32[]{:S(2)}, u32[]{:S(2)}) async-start(bf16[4,2,4,2,64,128]{5,4,3,2,1,0:T(8,128)(2,1)} %shard_map.59), calls=%async_computation.4 | async-start | bytes 2097152 | tf_op jit(solution)/shard_map/all_to_all | solution.py:296
  168.7 12.6 %collective-permute-start.13 = (bf16[32,64,128]{2,1,0:T(8,128)(2,1)S(1)}, bf16[32,64,128]{2,1,0:T(8,128)(2,1)}, u32[]{:S(2)}, u32[]{:S(2)}) collective-permute-start(bf16[32,64,128]{2,1,0:T(8,128)(2,1)S(1)} %copy-done.8), channel_id=1, source_target_pairs={{0,15},{1,0},{2,1},{3,2},{4,3},{5,4},{6,5},{7,6},{8,7},{9,8},{10,9... | collective-permute-start | bytes 1572872 | tf_op jit(solution)/shard_map/ppermute | solution.py:316
  175.4 11.4 %collective-permute-start.16 = (bf16[4,4,2,64,128]{4,3,2,1,0:T(8,128)(2,1)S(1)}, bf16[4,4,2,64,128]{4,3,2,1,0:T(8,128)(2,1)S(1)}, u32[]{:S(2)}, u32[]{:S(2)}) collective-permute-start(bf16[4,4,2,64,128]{4,3,2,1,0:T(8,128)(2,1)S(1)} %slice_bitcast_fusion.1), channel_id=1, source_target_pairs={{0,448},{64,0},{128,64},{192,128},{256,192},{320,256},{384,320},{4... | collective-permute-start | bytes 1572872 | tf_op jit(solution)/shard_map/ppermute | solution.py:310
  179.3 16.7 %collective-permute-start.7 = (bf16[32,64,128]{2,1,0:T(8,128)(2,1)}, bf16[32,64,128]{2,1,0:T(8,128)(2,1)}, u32[]{:S(2)}, u32[]{:S(2)}) collective-permute-start(bf16[32,64,128]{2,1,0:T(8,128)(2,1)} %collective-permute-done.6.refs_0_), channel_id=1, source_target_pairs={{0,1},{1,2},{2,3},{3,4},{4,5},{5,6},{6,7},{7,8},{8,9},{9,10},{10,1... | collective-permute-start | bytes 1572872 | tf_op jit(solution)/shard_map/ppermute | solution.py:314
  181.3 24.3 %collective-permute-start.14 = (bf16[32,64,128]{2,1,0:T(8,128)(2,1)}, bf16[32,64,128]{2,1,0:T(8,128)(2,1)}, u32[]{:S(2)}, u32[]{:S(2)}) collective-permute-start(bf16[32,64,128]{2,1,0:T(8,128)(2,1)} %collective-permute-done.13.refs_1_), channel_id=1, source_target_pairs={{0,15},{1,0},{2,1},{3,2},{4,3},{5,4},{6,5},{7,6},{8,7},{9,8},{10,9... | collective-permute-start | bytes 1572872 | tf_op jit(solution)/shard_map/ppermute | solution.py:316
  186.8 9.3 %copy-start.3 = (bf16[4,4,2,64,128]{4,3,2,1,0:T(8,128)(2,1)}, bf16[4,4,2,64,128]{4,3,2,1,0:T(8,128)(2,1)S(1)}, u32[]{:S(2)}) copy-start(bf16[4,4,2,64,128]{4,3,2,1,0:T(8,128)(2,1)S(1)} %collective-permute-done.16.refs_2_.refs_3_) | copy-start | bytes 1572868
  189.0 16.6 %all-to-all-start.5 = ((bf16[4,2,2,2,64,128]{5,4,3,2,1,0:T(8,128)(2,1)}), bf16[4,2,2,2,64,128]{5,4,3,2,1,0:T(8,128)(2,1)}, u32[]{:S(2)}, u32[]{:S(2)}) async-start(bf16[4,2,2,2,64,128]{5,4,3,2,1,0:T(8,128)(2,1)} %shard_map.60), calls=%async_computation.5 | async-start | bytes 1048576 | tf_op jit(solution)/shard_map/all_to_all | solution.py:296
  196.1 14.4 %collective-permute-start.18 = (bf16[4,4,2,64,128]{4,3,2,1,0:T(8,128)(2,1)}, bf16[4,4,2,64,128]{4,3,2,1,0:T(8,128)(2,1)S(1)}, u32[]{:S(2)}, u32[]{:S(2)}) collective-permute-start(bf16[4,4,2,64,128]{4,3,2,1,0:T(8,128)(2,1)} %slice_bitcast_fusion), channel_id=1, source_target_pairs={{0,448},{64,0},{128,64},{192,128},{256,192},{320,256},{384,320},{4... | collective-permute-start | bytes 1572872 | tf_op jit(solution)/shard_map/ppermute | solution.py:310
  196.1 17.6 %collective-permute-start.17 = (bf16[32,64,128]{2,1,0:T(8,128)(2,1)}, bf16[32,64,128]{2,1,0:T(8,128)(2,1)S(1)}, u32[]{:S(2)}, u32[]{:S(2)}) collective-permute-start(bf16[32,64,128]{2,1,0:T(8,128)(2,1)} %collective-permute-done.7.refs_0_), channel_id=1, source_target_pairs={{0,1},{1,2},{2,3},{3,4},{4,5},{5,6},{6,7},{7,8},{8,9},{9,10},{10,1... | collective-permute-start | bytes 1572872 | tf_op jit(solution)/shard_map/ppermute | solution.py:314
  198.0 3.4 %copy-start.1 = (bf16[16,32,64,128]{3,2,1,0:T(8,128)(2,1)S(1)}, bf16[16,32,64,128]{3,2,1,0:T(8,128)(2,1)}, u32[]{:S(2)}) copy-start(bf16[16,32,64,128]{3,2,1,0:T(8,128)(2,1)} %all-gather.2.cloned.1.call-done.gathered) | copy-start | bytes 25165828
  204.8 15.8 %collective-permute-start.19 = (bf16[4,16,2,32,128]{4,3,2,1,0:T(8,128)(2,1)}, bf16[4,16,2,32,128]{4,3,2,1,0:T(8,128)(2,1)}, u32[]{:S(2)}, u32[]{:S(2)}) collective-permute-start(bf16[4,16,2,32,128]{4,3,2,1,0:T(8,128)(2,1)} %get-tuple-element.13), channel_id=1, source_target_pairs={{0,448},{64,0},{128,64},{192,128},{256,192},{320,256},{384,320},{4... | collective-permute-start | bytes 3145736 | tf_op jit(solution)/shard_map/ppermute | solution.py:321
  205.6 11.5 %all-to-all-start.1 = ((f32[4,128,128]{2,1,0:T(8,128)}), f32[4,128,128]{2,1,0:T(8,128)S(1)}, u32[]{:S(2)}, u32[]{:S(2)}) async-start(f32[4,128,128]{2,1,0:T(8,128)} %get-tuple-element.12), calls=%async_computation.1 | async-start | bytes 524288 | tf_op jit(solution)/shard_map/all_to_all | solution.py:296
  210.4 6.7 %copy-start.4 = (bf16[4,4,2,64,128]{4,3,2,1,0:T(8,128)(2,1)}, bf16[4,4,2,64,128]{4,3,2,1,0:T(8,128)(2,1)S(1)}, u32[]{:S(2)}) copy-start(bf16[4,4,2,64,128]{4,3,2,1,0:T(8,128)(2,1)S(1)} %collective-permute-done.18.refs_3_.refs_4_) | copy-start | bytes 1572868
  217.1 33.3 %copy-start.13 = (f32[4,128,128]{2,1,0:T(8,128)}, f32[4,128,128]{2,1,0:T(8,128)S(1)}, u32[]{:S(2)}) copy-start(f32[4,128,128]{2,1,0:T(8,128)S(1)} %all-to-all-done.1.rank_ref) | copy-start | bytes 786436
  217.1 15.7 %all-to-all-start.6 = ((bf16[4,2,3,2,64,128]{5,4,3,2,1,0:T(8,128)(2,1)}), bf16[4,2,3,2,64,128]{5,4,3,2,1,0:T(8,128)(2,1)S(1)}, u32[]{:S(2)}, u32[]{:S(2)}) async-start(bf16[4,2,3,2,64,128]{5,4,3,2,1,0:T(8,128)(2,1)} %shard_map.61), calls=%async_computation.6 | async-start | bytes 1572864 | tf_op jit(solution)/shard_map/all_to_all | solution.py:296
  220.7 15.7 %collective-permute-start.20 = (bf16[4,16,2,32,128]{4,3,2,1,0:T(8,128)(2,1)}, bf16[4,16,2,32,128]{4,3,2,1,0:T(8,128)(2,1)S(1)}, u32[]{:S(2)}, u32[]{:S(2)}) collective-permute-start(bf16[4,16,2,32,128]{4,3,2,1,0:T(8,128)(2,1)} %copy-done.9), channel_id=1, source_target_pairs={{0,448},{64,0},{128,64},{192,128},{256,192},{320,256},{384,320},{4... | collective-permute-start | bytes 3145736 | tf_op jit(solution)/shard_map/ppermute | solution.py:321
  232.8 21.1 %copy-start.10 = (bf16[4,2,3,2,64,128]{5,4,3,2,1,0:T(8,128)(2,1)}, bf16[4,2,3,2,64,128]{5,4,3,2,1,0:T(8,128)(2,1)S(1)}, u32[]{:S(2)}) copy-start(bf16[4,2,3,2,64,128]{5,4,3,2,1,0:T(8,128)(2,1)S(1)} %all-to-all-done.6.refs_4_) | copy-start | bytes 2359300
  232.8 17.5 %all-to-all-start.7 = ((bf16[4,16,2,32,128]{4,3,2,1,0:T(8,128)(2,1)}), bf16[4,16,2,32,128]{4,3,2,1,0:T(8,128)(2,1)S(1)}, u32[]{:S(2)}, u32[]{:S(2)}) async-start(bf16[4,16,2,32,128]{4,3,2,1,0:T(8,128)(2,1)} %collective-permute-done.19), calls=%async_computation.7 | async-start | bytes 2097152 | tf_op jit(solution)/shard_map/all_to_all | solution.py:296
  250.4 10.5 %copy-start.11 = (bf16[4,16,2,32,128]{4,3,2,1,0:T(8,128)(2,1)}, bf16[4,16,2,32,128]{4,3,2,1,0:T(8,128)(2,1)S(1)}, u32[]{:S(2)}) copy-start(bf16[4,16,2,32,128]{4,3,2,1,0:T(8,128)(2,1)S(1)} %all-to-all-done.7.refs_0_) | copy-start | bytes 3145732
  250.4 16.6 %all-to-all-start.8 = ((bf16[4,16,2,32,128]{4,3,2,1,0:T(8,128)(2,1)}), bf16[4,16,2,32,128]{4,3,2,1,0:T(8,128)(2,1)S(1)}, u32[]{:S(2)}, u32[]{:S(2)}) async-start(bf16[4,16,2,32,128]{4,3,2,1,0:T(8,128)(2,1)} %copy-done.14), calls=%async_computation.8 | async-start | bytes 2097152 | tf_op jit(solution)/shard_map/all_to_all | solution.py:296
  253.9 8.1 %collective-permute-start.22 = (bf16[4,3,2,64,128]{4,3,2,1,0:T(8,128)(2,1)S(1)}, bf16[4,3,2,64,128]{4,3,2,1,0:T(8,128)(2,1)S(1)}, u32[]{:S(2)}, u32[]{:S(2)}) collective-permute-start(bf16[4,3,2,64,128]{4,3,2,1,0:T(8,128)(2,1)S(1)} %slice_bitcast_fusion.2), channel_id=1, source_target_pairs={{0,448},{64,0},{128,64},{192,128},{256,192},{320,256},{384,320},{4... | collective-permute-start | bytes 1179656 | tf_op jit(solution)/shard_map/ppermute | solution.py:310
  254.9 7.1 %collective-permute-start.21 = (bf16[4,2,2,64,128]{4,3,2,1,0:T(8,128)(2,1)S(1)}, bf16[4,2,2,64,128]{4,3,2,1,0:T(8,128)(2,1)S(1)}, u32[]{:S(2)}, u32[]{:S(2)}) collective-permute-start(bf16[4,2,2,64,128]{4,3,2,1,0:T(8,128)(2,1)S(1)} %slice_bitcast_fusion.4), channel_id=1, source_target_pairs={{0,448},{64,0},{128,64},{192,128},{256,192},{320,256},{384,320},{4... | collective-permute-start | bytes 786440 | tf_op jit(solution)/shard_map/ppermute | solution.py:310
  262.1 4.9 %copy-start.16 = (bf16[4,2,2,64,128]{4,3,2,1,0:T(8,128)(2,1)}, bf16[4,2,2,64,128]{4,3,2,1,0:T(8,128)(2,1)S(1)}, u32[]{:S(2)}) copy-start(bf16[4,2,2,64,128]{4,3,2,1,0:T(8,128)(2,1)S(1)} %collective-permute-done.21.refs_5_) | copy-start | bytes 786436
  262.1 4.9 %copy-start.15 = (bf16[4,3,2,64,128]{4,3,2,1,0:T(8,128)(2,1)}, bf16[4,3,2,64,128]{4,3,2,1,0:T(8,128)(2,1)S(1)}, u32[]{:S(2)}) copy-start(bf16[4,3,2,64,128]{4,3,2,1,0:T(8,128)(2,1)S(1)} %collective-permute-done.22.refs_6_) | copy-start | bytes 1179652
  (4 other events, 3.7 us)
Sparse Core Ops, SparseCore 0:
  9.4 169.9 all-gather.1
